TPU v7x, 32 devices: a whole 2x2x4 slice. The times are simulated.
32 devices in a mesh: dp: 8 (over y, x, core), tensor: 4 (over z).
Axes of the slice: x: 2, y: 2, z: 4, core: 2. Of those that a mesh axis runs over, the one named last changes fastest.
Arguments:
- tokens: bfloat16 [16384, 768], P(('dp', 'tensor')), may hold values from -6 to 6
- lengths: int32 [8], P('dp'), may hold values from 256 to 1024, as said below
- noise_mask: int32 [8, 1024], P('dp'), may hold values 0 or 1
- cotangent: bfloat16 [16384, 768], P(('dp', 'tensor')), may hold values from -6 to 6
- attn_gain: float32 [2, 768], replicated, may hold values from 0.5 to 1.5
- query_weight: bfloat16 [2, 768, 768], P(None, None, 'tensor'), may hold values from -0.21875 to 0.21875
- key_weight: bfloat16 [2, 768, 768], P(None, None, 'tensor'), may hold values from -0.21875 to 0.21875
- value_weight: bfloat16 [2, 768, 768], P(None, None, 'tensor'), may hold values from -0.21875 to 0.21875
- out_weight: bfloat16 [2, 768, 768], P(None, 'tensor'), may hold values from -0.875 to 0.875
- mlp_gain: float32 [2, 768], replicated, may hold values from 0.5 to 1.5
- up_weight: bfloat16 [2, 768, 3072], P(None, None, 'tensor'), may hold values from -0.21875 to 0.21875
- down_weight: bfloat16 [2, 3072, 768], P(None, 'tensor'), may hold values from -0.109375 to 0.109375
Outputs:
- block_out: float32 [16384, 768], P(('dp', 'tensor'))
- tokens_grad: float32 [16384, 768], P(('dp', 'tensor'))
- attn_gain_grad: float32 [2, 768], replicated
- query_weight_grad: float32 [2, 768, 768], P(None, None, 'tensor')
- key_weight_grad: float32 [2, 768, 768], P(None, None, 'tensor')
- value_weight_grad: float32 [2, 768, 768], P(None, None, 'tensor')
- out_weight_grad: float32 [2, 768, 768], P(None, 'tensor')
- mlp_gain_grad: float32 [2, 768], replicated
- up_weight_grad: float32 [2, 768, 3072], P(None, None, 'tensor')
- down_weight_grad: float32 [2, 3072, 768], P(None, 'tensor')
Inputs may be any that keep to these rules, and one draw needn't show every extreme that they name: `lengths`: each sequence has at least 256 and at most 1024 valid tokens; some sequence has exactly 1024 and some exactly 256.
All inputs are finite; a program needn't handle non-finite values. No bound on the sum of `noise_mask` on one device may be relied on, other than what follows from the above.
Results may differ from a plain program's by a relative error of at most 0.03.
Values may be sent and summed in bfloat16 or wider, within the bound.
A program may use at most 192 MiB of HBM per device.

v0:
```python
import math

import jax
import jax.numpy as jnp
from jax import lax
from jax.sharding import PartitionSpec as P

HD = 64
BLK = 16
LMAX = 1024
LAYERS = 2


NORM_EPS = 1e-05
MASKED_SCORE = -1e30


def layer_norm(row_vals, gain_row):
    row_mean = jnp.mean(row_vals, axis=-1, keepdims=True)
    centered = row_vals - row_mean
    variance = jnp.mean(centered * centered, axis=-1, keepdims=True)
    return centered * lax.rsqrt(variance + NORM_EPS) * gain_row


def rotate(vectors, cosines, sines):
    half_dim = vectors.shape[-1] // 2
    front_half = vectors[..., :half_dim]
    back_half = vectors[..., half_dim:]
    return jnp.concatenate(
        [front_half * cosines - back_half * sines, back_half * cosines + front_half * sines],
        axis=-1,
    )


def tables(row_total):
    position = (jnp.arange(row_total, dtype=jnp.int32) % LMAX).astype(jnp.float32)
    frequency = jnp.exp(
        -math.log(10000.0) * jnp.arange(HD // 2, dtype=jnp.int32).astype(jnp.float32) / (HD // 2)
    )
    angles = position[:, None] * frequency[None, :]
    return (jnp.cos(angles)[:, None, :], jnp.sin(angles)[:, None, :])


def visible(row_ids, col_ids, seq_len):
    block_q = row_ids % LMAX // BLK
    block_k = col_ids % LMAX // BLK
    clean_q = row_ids >= LMAX
    clean_k = col_ids >= LMAX
    both_clean = clean_k[None, :] & (block_k[None, :] <= block_q[:, None])
    noisy_query = jnp.where(
        clean_k[None, :], block_k[None, :] < block_q[:, None], block_k[None, :] == block_q[:, None]
    )
    rule = jnp.where(clean_q[:, None], both_clean, noisy_query)
    live_key = col_ids % LMAX < seq_len
    return rule & live_key[None, :] | (row_ids[:, None] == col_ids[None, :])


def loss_rows(lengths, noise_mask):
    position = jnp.arange(2 * LMAX, dtype=jnp.int32) % LMAX
    live_rows = position[None, :] < lengths[:, None]
    counted = jnp.concatenate([noise_mask, jnp.ones_like(noise_mask)], axis=1)
    return (live_rows & (counted == 1)).astype(jnp.float32).reshape(-1)


def scores_of(q_block, k_seq, begin_row, seq_len):
    block_len = q_block.shape[0]
    row_ids = begin_row + jnp.arange(block_len, dtype=jnp.int32)
    col_ids = jnp.arange(k_seq.shape[0], dtype=jnp.int32)
    raw_scores = jnp.einsum("qhd,khd->hqk", q_block, k_seq, preferred_element_type=jnp.float32) * (
        1.0 / math.sqrt(HD)
    )
    return jnp.where(visible(row_ids, col_ids, seq_len)[None], raw_scores, MASKED_SCORE)


def attend(queries, key_rows, value_rows, lengths):
    seq_rows = 2 * LMAX
    block_len = min(512, seq_rows)
    blocks = seq_rows // block_len

    def one_seq(seq_item):
        q_seq, k_seq, v_seq, seq_len = seq_item

        def one_block(block_index):
            begin_row = block_index * block_len
            q_block = lax.dynamic_slice_in_dim(q_seq, begin_row, block_len, 0)
            scores = scores_of(q_block, k_seq, begin_row, seq_len)
            row_max = jnp.max(scores, axis=-1, keepdims=True)
            exp_terms = jnp.exp(scores - row_max)
            row_sum = jnp.sum(exp_terms, axis=-1, keepdims=True)
            soft_probs = (exp_terms / row_sum).astype(jnp.bfloat16)
            mixed_rows = jnp.einsum(
                "hqk,khd->qhd", soft_probs, v_seq, preferred_element_type=jnp.float32
            )
            return (mixed_rows, (row_max + jnp.log(row_sum))[..., 0])

        return lax.map(one_block, jnp.arange(blocks, dtype=jnp.int32))

    return lax.map(one_seq, (queries, key_rows, value_rows, lengths))


def attend_back(queries, key_rows, value_rows, log_total, grad_mixed, lengths):
    seq_rows = 2 * LMAX
    block_len = min(512, seq_rows)
    blocks = seq_rows // block_len
    score_scale = 1.0 / math.sqrt(HD)

    def one_seq(seq_item):
        q_seq, k_seq, v_seq, total_seq, do_seq, seq_len = seq_item

        def one_block(carry, block_item):
            key_acc, value_acc = carry
            block_index, block_total = block_item
            begin_row = block_index * block_len
            q_block = lax.dynamic_slice_in_dim(q_seq, begin_row, block_len, 0)
            do_block = lax.dynamic_slice_in_dim(do_seq, begin_row, block_len, 0)
            scores = scores_of(q_block, k_seq, begin_row, seq_len)
            soft_probs = jnp.exp(scores - block_total[..., None])
            prob_grad = jnp.einsum(
                "qhd,khd->hqk", do_block, v_seq, preferred_element_type=jnp.float32
            )
            row_inner = jnp.sum(soft_probs * prob_grad, axis=-1, keepdims=True)
            dscore = (soft_probs * (prob_grad - row_inner)).astype(jnp.bfloat16)
            q_grad = (
                jnp.einsum("hqk,khd->qhd", dscore, k_seq, preferred_element_type=jnp.float32)
                * score_scale
            )
            key_acc = (
                key_acc
                + jnp.einsum("hqk,qhd->khd", dscore, q_block, preferred_element_type=jnp.float32)
                * score_scale
            )
            value_acc = value_acc + jnp.einsum(
                "hqk,qhd->khd",
                soft_probs.astype(jnp.bfloat16),
                do_block,
                preferred_element_type=jnp.float32,
            )
            return ((key_acc, value_acc), q_grad)

        zero_acc = jnp.zeros(k_seq.shape, jnp.float32)
        (key_acc, value_acc), q_grads = lax.scan(
            one_block, (zero_acc, zero_acc), (jnp.arange(blocks, dtype=jnp.int32), total_seq)
        )
        return (q_grads.reshape(k_seq.shape), key_acc, value_acc)

    return lax.map(one_seq, (queries, key_rows, value_rows, log_total, grad_mixed, lengths))


def row_product(left_rows, right_mat):
    return jnp.dot(left_rows, right_mat, preferred_element_type=jnp.float32)


def row_product_t(left_rows, right_mat):
    return jnp.einsum("rf,df->rd", left_rows, right_mat, preferred_element_type=jnp.float32)


def gelu_back(pre_act, hidden_grad):
    unused_out, gelu_pull = jax.vjp(jax.nn.gelu, pre_act)
    return gelu_pull(hidden_grad)[0]


def on_device(
    tokens,
    lengths,
    noise_mask,
    cotangent,
    attn_gain,
    query_weight,
    key_weight,
    value_weight,
    out_weight,
    mlp_gain,
    up_weight,
    down_weight,
):
    shard_rows = tokens.shape[0]
    seq_count = lengths.shape[0]
    seq_rows = 2 * LMAX
    group_rows = seq_count * seq_rows
    local_heads = query_weight.shape[2] // HD
    head_cols = local_heads * HD
    split_shape = (seq_count, seq_rows, local_heads, HD)
    tensor_pos = lax.axis_index("tensor")
    cosines, sines = tables(group_rows)
    loss_weight = lax.dynamic_slice_in_dim(
        loss_rows(lengths, noise_mask), tensor_pos * shard_rows, shard_rows, 0
    )
    residual = tokens.astype(jnp.float32)
    saved = []
    for layer_idx in range(LAYERS):
        layer_in = residual
        normed = layer_norm(layer_in, attn_gain[layer_idx]).astype(jnp.bfloat16)
        normed_all = lax.all_gather(normed, "tensor", axis=0, tiled=True)
        query_lin = jnp.dot(normed_all, query_weight[layer_idx], preferred_element_type=jnp.float32)
        queries = rotate(query_lin.reshape(group_rows, local_heads, HD), cosines, sines).astype(
            jnp.bfloat16
        )
        key_lin = jnp.dot(normed_all, key_weight[layer_idx], preferred_element_type=jnp.float32)
        key_rows = rotate(key_lin.reshape(group_rows, local_heads, HD), cosines, sines).astype(
            jnp.bfloat16
        )
        value_rows = (
            jnp.dot(normed_all, value_weight[layer_idx], preferred_element_type=jnp.float32)
            .astype(jnp.bfloat16)
            .reshape(group_rows, local_heads, HD)
        )
        mixed_rows, log_total = attend(
            queries.reshape(split_shape),
            key_rows.reshape(split_shape),
            value_rows.reshape(split_shape),
            lengths,
        )
        mixed_rows = mixed_rows.reshape(group_rows, head_cols).astype(jnp.bfloat16)
        attn_out = lax.psum_scatter(
            row_product(mixed_rows, out_weight[layer_idx]).astype(jnp.bfloat16),
            "tensor",
            scatter_dimension=0,
            tiled=True,
        ).astype(jnp.float32)
        middle = layer_in + attn_out
        lifted = layer_norm(middle, mlp_gain[layer_idx]).astype(jnp.bfloat16)
        lifted_all = lax.all_gather(lifted, "tensor", axis=0, tiled=True)
        pre_act = jnp.dot(lifted_all, up_weight[layer_idx], preferred_element_type=jnp.float32)
        hidden = jax.nn.gelu(pre_act).astype(jnp.bfloat16)
        residual = middle + lax.psum_scatter(
            row_product(hidden, down_weight[layer_idx]).astype(jnp.bfloat16),
            "tensor",
            scatter_dimension=0,
            tiled=True,
        ).astype(jnp.float32)
        mlp_keep = (lifted_all, up_weight[layer_idx], down_weight[layer_idx])
        saved.append(
            (
                layer_in,
                normed_all,
                queries,
                key_rows,
                value_rows,
                mixed_rows,
                log_total,
                middle,
                pre_act,
                hidden,
                mlp_keep,
            )
        )
    grad_rows = cotangent.astype(jnp.float32) * loss_weight[:, None]
    grads_out = []
    for layer_idx in reversed(range(LAYERS)):
        (
            layer_in,
            normed_all,
            queries,
            key_rows,
            value_rows,
            mixed_rows,
            log_total,
            middle,
            pre_act,
            hidden,
            mlp_keep,
        ) = saved[layer_idx]
        out_grad = grad_rows.astype(jnp.bfloat16)
        lifted_all, up_local, down_local = mlp_keep
        out_grad_all = lax.all_gather(out_grad, "tensor", axis=0, tiled=True)
        hidden_grad = jnp.einsum(
            "rd,fd->rf", out_grad_all, down_local, preferred_element_type=jnp.float32
        )
        pre_grad = gelu_back(pre_act, hidden_grad).astype(jnp.bfloat16)
        up_grad = jnp.einsum("rd,rf->df", lifted_all, pre_grad, preferred_element_type=jnp.float32)
        down_grad = jnp.einsum(
            "rf,rd->fd", hidden, out_grad_all, preferred_element_type=jnp.float32
        )
        lifted_grad = lax.psum_scatter(
            row_product_t(pre_grad, up_local).astype(jnp.bfloat16),
            "tensor",
            scatter_dimension=0,
            tiled=True,
        ).astype(jnp.float32)
        unused_mid, norm_back_mid = jax.vjp(layer_norm, middle, mlp_gain[layer_idx])
        middle_part, mlp_gain_grad = norm_back_mid(lifted_grad)
        middle_grad = grad_rows + middle_part
        attn_grad = middle_grad.astype(jnp.bfloat16)
        attn_grad_all = lax.all_gather(attn_grad, "tensor", axis=0, tiled=True)
        out_w_grad = jnp.einsum(
            "re,rd->ed", mixed_rows, attn_grad_all, preferred_element_type=jnp.float32
        )
        mixed_grad = jnp.einsum(
            "rd,ed->re", attn_grad_all, out_weight[layer_idx], preferred_element_type=jnp.float32
        ).astype(jnp.bfloat16)
        q_grad, k_grad, v_grad = attend_back(
            queries.reshape(split_shape),
            key_rows.reshape(split_shape),
            value_rows.reshape(split_shape),
            log_total,
            mixed_grad.reshape(split_shape),
            lengths,
        )
        q_lin_grad = (
            rotate(q_grad.reshape(group_rows, local_heads, HD), cosines, -sines)
            .reshape(group_rows, head_cols)
            .astype(jnp.bfloat16)
        )
        k_lin_grad = (
            rotate(k_grad.reshape(group_rows, local_heads, HD), cosines, -sines)
            .reshape(group_rows, head_cols)
            .astype(jnp.bfloat16)
        )
        v_lin_grad = v_grad.reshape(group_rows, head_cols).astype(jnp.bfloat16)
        q_w_grad = jnp.einsum(
            "rd,re->de", normed_all, q_lin_grad, preferred_element_type=jnp.float32
        )
        k_w_grad = jnp.einsum(
            "rd,re->de", normed_all, k_lin_grad, preferred_element_type=jnp.float32
        )
        v_w_grad = jnp.einsum(
            "rd,re->de", normed_all, v_lin_grad, preferred_element_type=jnp.float32
        )
        w_query = query_weight[layer_idx]
        w_key = key_weight[layer_idx]
        w_value = value_weight[layer_idx]

        def input_term(
            begin_row,
            row_count,
            q_lin_grad=q_lin_grad,
            k_lin_grad=k_lin_grad,
            v_lin_grad=v_lin_grad,
            w_query=w_query,
            w_key=w_key,
            w_value=w_value,
        ):
            total_term = row_product_t(q_lin_grad, w_query)
            total_term = total_term + row_product_t(k_lin_grad, w_key)
            return total_term + row_product_t(v_lin_grad, w_value)

        normed_grad = lax.psum_scatter(
            input_term(jnp.int32(0), shard_rows * lax.axis_size("tensor")).astype(jnp.bfloat16),
            "tensor",
            scatter_dimension=0,
            tiled=True,
        ).astype(jnp.float32)
        unused_in, norm_back_in = jax.vjp(layer_norm, layer_in, attn_gain[layer_idx])
        in_part, attn_gain_grad = norm_back_in(normed_grad)
        grad_rows = middle_grad + in_part
        grads_out.append(
            (
                attn_gain_grad,
                q_w_grad,
                k_w_grad,
                v_w_grad,
                out_w_grad,
                mlp_gain_grad,
                up_grad,
                down_grad,
            )
        )
    grads_out = grads_out[::-1]
    stacked = [
        jnp.stack([layer_grads[slot_idx] for layer_grads in grads_out]) for slot_idx in range(8)
    ]
    weight_sums = lax.psum(
        (stacked[1], stacked[2], stacked[3], stacked[4], stacked[6], stacked[7]), "dp"
    )
    gain_totals = lax.psum((stacked[0], stacked[5]), ("dp", "tensor"))
    return (
        residual,
        grad_rows,
        gain_totals[0],
        weight_sums[0],
        weight_sums[1],
        weight_sums[2],
        weight_sums[3],
        gain_totals[1],
        weight_sums[4],
        weight_sums[5],
    )


def solution(mesh):
    in_specs = (
        P(("dp", "tensor"), None),
        P("dp"),
        P("dp", None),
        P(("dp", "tensor"), None),
        P(),
        P(None, None, "tensor"),
        P(None, None, "tensor"),
        P(None, None, "tensor"),
        P(None, "tensor", None),
        P(),
        P(None, None, "tensor"),
        P(None, "tensor", None),
    )
    out_specs = (
        P(("dp", "tensor"), None),
        P(("dp", "tensor"), None),
        P(),
        P(None, None, "tensor"),
        P(None, None, "tensor"),
        P(None, None, "tensor"),
        P(None, "tensor", None),
        P(),
        P(None, None, "tensor"),
        P(None, "tensor", None),
    )
    return jax.shard_map(
        on_device, mesh=mesh, in_specs=in_specs, out_specs=out_specs, check_vma=False
    )
```

profile of v0, /device:TPU:0, one launch (start us, length us, event | category | flops | bytes accessed | tf_op | source)
XLA Modules:
  0.0 1893.8 jit_solution(13265354482314608953)
XLA Ops:
  18.4 63.0 %all-gather.9.cloned.1.call-done = bf16[2048,768]{1,0:T(8,128)(2,1)} async-done(((bf16[512,768]{1,0:T(8,128)(2,1)}), bf16[2048,768]{1,0:T(8,128)(2,1)}) %all-gather.9.cloned.1.call-update) | async-done | bytes 3145744 | tf_op jit(solution)/shard_map/all_gather | solution.py:193
  88.6 99.8 %while.106 = (s32[]{:T(128)}, bf16[4,512,3,64]{1,3,2,0:T(8,128)(2,1)S(1)}, f32[4,3,512]{2,1,0:T(4,128)S(1)}, s32[4]{0:T(128)S(1)}, s32[]{:T(128)}, /*index=5*/bf...) while((s32[]{:T(128)}, ...), condition=%wide.region_5.6_spmd, body=%wide.region_2.5_spmd.sunk | while | flops 852564992 | bytes 44199116 | solution.py:96
  194.1 57.8 %reduce-scatter.9.cloned.1.call-done = bf16[512,768]{1,0:T(8,128)(2,1)} async-done(((bf16[2048,768]{1,0:T(8,128)(2,1)}), bf16[512,768]{1,0:T(8,128)(2,1)}) %reduce-scatter.9.cloned.1.call-update) | async-done | bytes 786448 | tf_op jit(solution)/shard_map/reduce_scatter | solution.py:214
  257.4 63.6 %all-gather.11.cloned.1.call-done = bf16[2048,768]{1,0:T(8,128)(2,1)} async-done(((bf16[512,768]{1,0:T(8,128)(2,1)}), bf16[2048,768]{1,0:T(8,128)(2,1)}) %all-gather.11.cloned.1.call-update) | async-done | bytes 3145744 | tf_op jit(solution)/shard_map/all_gather | solution.py:222
  333.9 59.0 %reduce-scatter.11.cloned.1.call-done = bf16[512,768]{1,0:T(8,128)(2,1)} async-done(((bf16[2048,768]{1,0:T(8,128)(2,1)}), bf16[512,768]{1,0:T(8,128)(2,1)}) %reduce-scatter.11.cloned.1.call-update) | async-done | bytes 786448 | tf_op jit(solution)/shard_map/reduce_scatter | solution.py:225
  397.2 63.2 %all-gather.13.cloned.1.call-done = bf16[2048,768]{1,0:T(8,128)(2,1)} async-done(((bf16[512,768]{1,0:T(8,128)(2,1)}), bf16[2048,768]{1,0:T(8,128)(2,1)}) %all-gather.13.cloned.1.call-update) | async-done | bytes 3145744 | tf_op jit(solution)/shard_map/all_gather | solution.py:193
  467.2 96.5 %while.107 = (s32[]{:T(128)}, bf16[4,512,3,64]{1,3,2,0:T(8,128)(2,1)S(1)}, f32[4,3,512]{2,1,0:T(4,128)S(1)}, s32[4]{0:T(128)S(1)}, s32[]{:T(128)}, /*index=5*/bf...) while((s32[]{:T(128)}, ...), condition=%wide.region_15.16_spmd, body=%wide.region_12.15_spmd.sunk | while | flops 852564992 | bytes 44199116 | solution.py:96
  568.3 59.0 %reduce-scatter.13.cloned.1.call-done = bf16[512,768]{1,0:T(8,128)(2,1)} async-done(((bf16[2048,768]{1,0:T(8,128)(2,1)}), bf16[512,768]{1,0:T(8,128)(2,1)}) %reduce-scatter.13.cloned.1.call-update) | async-done | bytes 786448 | tf_op jit(solution)/shard_map/reduce_scatter | solution.py:214
  633.0 61.6 %all-gather.15.cloned.1.call-done = bf16[2048,768]{1,0:T(8,128)(2,1)} async-done(((bf16[512,768]{1,0:T(8,128)(2,1)}), bf16[2048,768]{1,0:T(8,128)(2,1)}) %all-gather.15.cloned.1.call-update) | async-done | bytes 3145744 | tf_op jit(solution)/shard_map/all_gather | solution.py:222
  702.0 56.9 %all-gather.17.cloned.1.call-done = bf16[2048,768]{1,0:T(8,128)(2,1)} async-done(((bf16[512,768]{1,0:T(8,128)(2,1)}), bf16[2048,768]{1,0:T(8,128)(2,1)}) %all-gather.17.cloned.1.call-update) | async-done | bytes 3145744 | tf_op jit(solution)/shard_map/all_gather | solution.py:265
  781.8 50.3 %reduce-scatter.17.cloned.1.call-done = bf16[512,768]{1,0:T(8,128)(2,1)} async-done(((bf16[2048,768]{1,0:T(8,128)(2,1)}), bf16[512,768]{1,0:T(8,128)(2,1)}) %reduce-scatter.17.cloned.1.call-update) | async-done | bytes 786448 | tf_op jit(solution)/shard_map/reduce_scatter | solution.py:274
  834.6 60.6 %reduce-scatter.15.cloned.1.call-done = bf16[512,768]{1,0:T(8,128)(2,1)} async-done(((bf16[2048,768]{1,0:T(8,128)(2,1)}), bf16[512,768]{1,0:T(8,128)(2,1)}) %reduce-scatter.15.cloned.1.call-update) | async-done | bytes 786448 | tf_op jit(solution)/shard_map/reduce_scatter | solution.py:225
  900.9 63.6 %all-gather.19.cloned.1.call-done = bf16[2048,768]{1,0:T(8,128)(2,1)} async-done(((bf16[512,768]{1,0:T(8,128)(2,1)}), bf16[2048,768]{1,0:T(8,128)(2,1)}) %all-gather.19.cloned.1.call-update) | async-done | bytes 3145744 | tf_op jit(solution)/shard_map/all_gather | solution.py:284
  969.8 169.6 %while.108 = (s32[]{:T(128)}, f32[2048,3,64]{0,2,1:T(8,128)}, f32[2048,3,64]{0,2,1:T(8,128)}, f32[4,512,3,64]{1,0,3,2:T(4,128)}, s32[4]{0:T(128)S(1)}, /*index=5...) while((s32[]{:T(128)}, f32[2048,3,64]{0,2,1:T(8,128)}, ...), condition=%wide.region_25.26_spmd.clone, body=%wide.region_23.25_spmd.clone.sunk | while | flops 2072026112 | bytes 151989680 | solution.py:141
  1002.3 8.6 dynamic_update_slice.83
  1045.1 8.6 dynamic_update_slice.83
  1150.7 59.0 %reduce-scatter.19.cloned.1.call-done = bf16[512,768]{1,0:T(8,128)(2,1)} async-done(((bf16[2048,768]{1,0:T(8,128)(2,1)}), bf16[512,768]{1,0:T(8,128)(2,1)}) %reduce-scatter.19.cloned.1.call-update) | async-done | bytes 786448 | tf_op jit(solution)/shard_map/reduce_scatter | solution.py:337
  1216.9 63.6 %all-gather.21.cloned.1.call-done = bf16[2048,768]{1,0:T(8,128)(2,1)} async-done(((bf16[512,768]{1,0:T(8,128)(2,1)}), bf16[2048,768]{1,0:T(8,128)(2,1)}) %all-gather.21.cloned.1.call-update) | async-done | bytes 3145744 | tf_op jit(solution)/shard_map/all_gather | solution.py:265
  1294.8 59.0 %reduce-scatter.21.cloned.1.call-done = bf16[512,768]{1,0:T(8,128)(2,1)} async-done(((bf16[2048,768]{1,0:T(8,128)(2,1)}), bf16[512,768]{1,0:T(8,128)(2,1)}) %reduce-scatter.21.cloned.1.call-update) | async-done | bytes 786448 | tf_op jit(solution)/shard_map/reduce_scatter | solution.py:274
  1360.6 63.6 %all-gather.23.cloned.1.call-done = bf16[2048,768]{1,0:T(8,128)(2,1)} async-done(((bf16[512,768]{1,0:T(8,128)(2,1)}), bf16[2048,768]{1,0:T(8,128)(2,1)}) %all-gather.23.cloned.1.call-update) | async-done | bytes 3145744 | tf_op jit(solution)/shard_map/all_gather | solution.py:284
  1429.6 177.9 %while.109 = (s32[]{:T(128)}, f32[2048,3,64]{0,2,1:T(8,128)}, f32[2048,3,64]{0,2,1:T(8,128)}, f32[4,512,3,64]{1,0,3,2:T(4,128)}, s32[4]{0:T(128)S(1)}, /*index=5...) while((s32[]{:T(128)}, f32[2048,3,64]{0,2,1:T(8,128)}, ...), condition=%wide.region_34.35_spmd.clone, body=%wide.region_32.34_spmd.clone.sunk | while | flops 2072026112 | bytes 142552400 | solution.py:141
  1658.6 19.3 %reduce-scatter.23.cloned.1.call-done = bf16[512,768]{1,0:T(8,128)(2,1)} async-done(((bf16[2048,768]{1,0:T(8,128)(2,1)}), bf16[512,768]{1,0:T(8,128)(2,1)}) %reduce-scatter.23.cloned.1.call-update) | async-done | bytes 786448 | tf_op jit(solution)/shard_map/reduce_scatter | solution.py:337
  1681.9 41.1 %all-reduce.1 = (f32[2,768]{1,0:T(2,128)}, f32[2,768]{1,0:T(2,128)}) all-reduce(f32[2,768]{1,0:T(2,128)S(1)} %pad_maximum_fusion.10, f32[2,768]{1,0:T(2,128)S(1)} %pad_maximum_fusion.11), channel_id=1, replica_groups=mesh['dp'=8,'tensor'=4] {'dp','tensor'}, use_global_device_ids=true, to_apply=%region_40.41 | all-reduce | flops 3072 | bytes 24576 | tf_op jit(solution)/shard_map/psum | solution.py:365
  1726.4 149.7 %all-reduce.5.cloned.1.call-done = (f32[2,768,192]{1,2,0:T(8,128)}, f32[2,768,192]{1,2,0:T(8,128)}, f32[2,768,192]{1,2,0:T(8,128)}, f32[2,192,768]{2,1,0:T(8,128...) async-done(((f32[2,768,192]{1,2,0:T(8,128)}, f32[2,768,192]{1,2,0:T(8,128)}, f32[2,768,192]{1,2,0:T(8,128)}, f32[2,192,768]{2,1,0:T(8,128)}, f32[2,768,768]{2,1,0:T(8,128)}, ...) | async-done | bytes 14155792 | tf_op jit(solution)/shard_map/psum | solution.py:362
  (689 shorter events, 733.2 us)
Async XLA Ops:
  7.2 74.2 %all-gather.9.cloned.1.call-start = ((), (), s32[]{:S(2)}) async-start(), calls=%async_computation.8 | async-start | bytes 3932160 | tf_op jit(solution)/shard_map/all_gather | solution.py:193
  15.1 236.8 %reduce-scatter.9.cloned.1.call-start = ((), (), s32[]{:S(2)}) async-start(), calls=%async_computation.9 | async-start | bytes 3932160 | tf_op jit(solution)/shard_map/reduce_scatter | solution.py:214
  192.8 128.2 %all-gather.11.cloned.1.call-start = ((), (), s32[]{:S(2)}) async-start(), calls=%async_computation.10 | async-start | bytes 3932160 | tf_op jit(solution)/shard_map/all_gather | solution.py:222
  257.4 135.5 %reduce-scatter.11.cloned.1.call-start = ((), (), s32[]{:S(2)}) async-start(), calls=%async_computation.11 | async-start | bytes 3932160 | tf_op jit(solution)/shard_map/reduce_scatter | solution.py:225
  333.9 126.6 %all-gather.13.cloned.1.call-start = ((), (), s32[]{:S(2)}) async-start(), calls=%async_computation.12 | async-start | bytes 3932160 | tf_op jit(solution)/shard_map/all_gather | solution.py:193
  394.5 69.2 %copy-start.89 = (f32[512]{0:T(512)}, f32[512]{0:T(512)S(1)}, u32[]{:S(2)}) copy-start(f32[512]{0:T(512)S(1)} %broadcast_multiply_fusion.1) | copy-start | bytes 6148
  394.8 68.9 %copy-start.111 = (f32[512]{0:T(512)}, f32[512]{0:T(512)S(1)}, u32[]{:S(2)}) copy-start(f32[512]{0:T(512)S(1)} %multiply_reduce_fusion.3) | copy-start | bytes 6148
  394.8 68.9 %copy-start.99 = (f32[512]{0:T(512)}, f32[512]{0:T(512)S(1)}, u32[]{:S(2)}) copy-start(f32[512]{0:T(512)S(1)} %fusion.223) | copy-start | bytes 6148
  396.8 230.5 %reduce-scatter.13.cloned.1.call-start = ((), (), s32[]{:S(2)}) async-start(), calls=%async_computation.13 | async-start | bytes 3932160 | tf_op jit(solution)/shard_map/reduce_scatter | solution.py:214
  568.2 126.4 %all-gather.15.cloned.1.call-start = ((), (), s32[]{:S(2)}) async-start(), calls=%async_computation.14 | async-start | bytes 3932160 | tf_op jit(solution)/shard_map/all_gather | solution.py:222
  630.9 128.0 %all-gather.17.cloned.1.call-start = ((), (), s32[]{:S(2)}) async-start(), calls=%async_computation.16 | async-start | bytes 3932160 | tf_op jit(solution)/shard_map/all_gather | solution.py:265
  631.7 266.7 %copy-start.101 = (f32[1,512]{1,0:T(1,128)}, f32[1,512]{1,0:T(1,128)S(1)}, u32[]{:S(2)}) copy-start(f32[1,512]{1,0:T(1,128)S(1)} %and_convert_fusion) | copy-start | bytes 6148
  632.8 199.3 %reduce-scatter.17.cloned.1.call-start = ((), (), s32[]{:S(2)}) async-start(), calls=%async_computation.17 | async-start | bytes 3932160 | tf_op jit(solution)/shard_map/reduce_scatter | solution.py:274
  773.1 122.1 %reduce-scatter.15.cloned.1.call-start = ((), (), s32[]{:S(2)}) async-start(), calls=%async_computation.15 | async-start | bytes 3932160 | tf_op jit(solution)/shard_map/reduce_scatter | solution.py:225
  781.8 182.8 %all-gather.19.cloned.1.call-start = ((), (), s32[]{:S(2)}) async-start(), calls=%async_computation.18 | async-start | bytes 3932160 | tf_op jit(solution)/shard_map/all_gather | solution.py:284
  898.4 70.0 %copy-start.105 = (f32[512]{0:T(512)}, f32[512]{0:T(512)S(1)}, u32[]{:S(2)}) copy-start(f32[512]{0:T(512)S(1)} %negate_multiply_fusion.3) | copy-start | bytes 6148
  900.8 308.8 %reduce-scatter.19.cloned.1.call-start = ((), (), s32[]{:S(2)}) async-start(), calls=%async_computation.19 | async-start | bytes 3932160 | tf_op jit(solution)/shard_map/reduce_scatter | solution.py:337
  1150.6 129.9 %all-gather.21.cloned.1.call-start = ((), (), s32[]{:S(2)}) async-start(), calls=%async_computation.20 | async-start | bytes 3932160 | tf_op jit(solution)/shard_map/all_gather | solution.py:265
  1216.8 141.5 %copy-start.28 = (f32[512,768]{1,0:T(8,128)}, f32[512,768]{1,0:T(8,128)S(1)}, u32[]{:S(2)}) copy-start(f32[512,768]{1,0:T(8,128)S(1)} %get-tuple-element.909) | copy-start | bytes 4718596
  1216.9 137.0 %reduce-scatter.21.cloned.1.call-start = ((), (), s32[]{:S(2)}) async-start(), calls=%async_computation.21 | async-start | bytes 3932160 | tf_op jit(solution)/shard_map/reduce_scatter | solution.py:274
  1294.8 129.5 %all-gather.23.cloned.1.call-start = ((), (), s32[]{:S(2)}) async-start(), calls=%async_computation.22 | async-start | bytes 3932160 | tf_op jit(solution)/shard_map/all_gather | solution.py:284
  1360.5 317.4 %reduce-scatter.23.cloned.1.call-start = ((), (), s32[]{:S(2)}) async-start(), calls=%async_computation.23 | async-start | bytes 3932160 | tf_op jit(solution)/shard_map/reduce_scatter | solution.py:337
  1360.6 68.9 %copy-start.8 = (bf16[2048,3,64]{0,2,1:T(8,128)(2,1)S(1)}, bf16[2048,3,64]{0,2,1:T(8,128)(2,1)}, u32[]{:S(2)}) copy-start(bf16[2048,3,64]{0,2,1:T(8,128)(2,1)} %copy-done.7) | copy-start | bytes 2359300
  1618.8 257.2 %all-reduce.5.cloned.1.call-start = ((), (), s32[]{:S(2)}) async-start(), calls=%async_computation.24 | async-start | bytes 28311552 | tf_op jit(solution)/shard_map/psum | solution.py:362
  (152 other events, 2436.6 us)
Sparse Core Ops, SparseCore 0:
  15.2 66.1 all-gather.8
  192.9 58.8 reduce-scatter.8
  257.5 63.5 all-gather.10
  334.0 58.8 reduce-scatter.10
  396.9 63.5 all-gather.12
  568.3 58.8 reduce-scatter.12
  631.1 63.5 all-gather.14
  696.8 62.1 all-gather.16
  773.2 58.8 reduce-scatter.16
  834.9 60.2 reduce-scatter.14
  900.9 63.5 all-gather.18
  1150.7 58.8 reduce-scatter.18
  1217.0 63.5 all-gather.20
  1294.9 58.8 reduce-scatter.20
  1360.7 63.5 all-gather.22
  1619.0 58.8 reduce-scatter.22
  1683.6 192.4 all-reduce.4
where the time goes:
time: 1910 us; the launch traced here: 1890 us
  waiting for transfers between devices  1070 us (56%)
  matrix products  398 us (21%)
  other arithmetic  219 us (11%)
  local copies, waits for them, and re-layouts  131 us (7%)
  blocking collectives  41.1 us (2%)
    psum x1, waiting for transfers between devices, on_device(): lax.psum((stacked[1], stacked[2], stacked[3], stacked[4], stacked[6], sta...  150 us
    all_gather x2, waiting for transfers between devices, on_device(): attn_grad_all = lax.all_gather(attn_grad, 'tensor', axis=0, tiled=True)  127 us
    all_gather x2, waiting for transfers between devices, on_device(): normed_all = lax.all_gather(normed, 'tensor', axis=0, tiled=True)  126 us
    all_gather x2, waiting for transfers between devices, on_device(): lifted_all = lax.all_gather(lifted, 'tensor', axis=0, tiled=True)  125 us
    all_gather x2, waiting for transfers between devices, on_device(): out_grad_all = lax.all_gather(out_grad, 'tensor', axis=0, tiled=True)  121 us
    reduce_scatter x2, waiting for transfers between devices, on_device(): lax.psum_scatter(row_product(hidden, down_weight[layer_idx]).astype(jnp.b...  120 us
    reduce_scatter x2, waiting for transfers between devices, on_device(): lax.psum_scatter(row_product(mixed_rows, out_weight[layer_idx]).astype(jn...  117 us
    reduce_scatter x2, waiting for transfers between devices, on_device(): lax.psum_scatter(row_product_t(pre_grad, up_local).astype(jnp.bfloat16),...  109 us
  transfers between devices with their start and end apart: 17, of which 17 were waited for; matrix products, arithmetic and copies ran while one was open for 3% of the time, Pallas kernels for 0%

commit v1 on v0

v1 whole, which is shorter than its diff:
```python
import functools
import math

import jax
import jax.numpy as jnp
from jax import lax
from jax.experimental import pallas as pl
from jax.experimental.pallas import tpu as pltpu
from jax.sharding import PartitionSpec as P

HD = 64
BLK = 16
LMAX = 1024
LAYERS = 2
EPS = 1e-05
NEG = -1e30
SCALE = 1.0 / math.sqrt(HD)
GC = math.sqrt(2.0 / math.pi)
GA = 0.044715
F32 = jnp.float32
BF = jnp.bfloat16
QB = 256
VMEM_LIMIT = 56 << 20

NN = (((1,), (0,)), ((), ()))
NT = (((1,), (1,)), ((), ()))
TN = (((0,), (0,)), ((), ()))


def mm(a, b, dims=NN):
    return lax.dot_general(a, b, dims, preferred_element_type=F32)


def norm_stats(x):
    mean = jnp.mean(x, axis=-1, keepdims=True)
    c = x - mean
    var = jnp.mean(c * c, axis=-1, keepdims=True)
    r = lax.rsqrt(var + EPS)
    return c * r, r


def norm_back(x, gain, dy):
    xh, r = norm_stats(x)
    gy = dy * gain
    m1 = jnp.mean(gy, axis=-1, keepdims=True)
    m2 = jnp.mean(gy * xh, axis=-1, keepdims=True)
    dz = r * (gy - m1 - xh * m2)
    return dz, jnp.sum(dy * xh, axis=0, keepdims=True)


def turn(y, cos, sin):
    lane = lax.broadcasted_iota(jnp.int32, y.shape, 1) % HD
    other = jnp.where(
        lane < HD // 2, pltpu.roll(y, 128 - HD // 2, 1), pltpu.roll(y, HD // 2, 1)
    )
    return y * cos + other * sin


def vmem(n):
    return [pl.BlockSpec(memory_space=pltpu.VMEM)] * n


def smem():
    return pl.BlockSpec(memory_space=pltpu.SMEM)


def params(**kw):
    return pltpu.CompilerParams(vmem_limit_bytes=VMEM_LIMIT, **kw)


def cost(flops, nbytes, trans=0):
    return pl.CostEstimate(flops=int(flops), bytes_accessed=int(nbytes), transcendentals=int(trans))


def own_kernel(a_ref, w_ref, cos_ref, sin_ref, q_ref, k_ref, v_ref, tmp):
    d = a_ref.shape[1]
    a = a_ref[...]
    tmp[...] = mm(a, w_ref[:, 0:d])
    for g in range(d // 128):
        s = slice(g * 128, g * 128 + 128)
        q_ref[:, s] = (turn(tmp[:, s], cos_ref[...], sin_ref[...]) ).astype(BF)
    tmp[...] = mm(a, w_ref[:, d : 2 * d])
    for g in range(d // 128):
        s = slice(g * 128, g * 128 + 128)
        k_ref[:, s] = turn(tmp[:, s], cos_ref[...], sin_ref[...]).astype(BF)
    v_ref[...] = mm(a, w_ref[:, 2 * d : 3 * d]).astype(BF)


def project_own(a, w, cos, sin):
    rows, d = a.shape
    sd = jax.ShapeDtypeStruct((rows, d), BF)
    return pl.pallas_call(
        own_kernel,
        out_shape=(sd, sd, sd),
        in_specs=vmem(4),
        out_specs=tuple(vmem(3)),
        scratch_shapes=[pltpu.VMEM((rows, d), F32)],
        compiler_params=params(),
        cost_estimate=cost(6 * rows * d * d, 2 * (3 * d * d + 4 * rows * d)),
        name="project_own",
    )(a, w, cos, sin)


def make_bias(info, bias):
    n = bias.shape[0]
    length = info[0]
    t = info[1]
    noisy = t < 2
    odd = t % 2
    base = odd * n
    i = lax.broadcasted_iota(jnp.int32, (n, n), 0)
    j = lax.broadcasted_iota(jnp.int32, (n, n), 1)
    bi = i // BLK
    bj = j // BLK
    odd_lim = jnp.where(odd == 1, length, 0)
    bias[:, 0:n] = jnp.where(j < odd_lim, 0.0, NEG)
    strict_lim = jnp.where(noisy, length - base, 0)
    bias[:, n : 2 * n] = jnp.where((bj < bi) & (j < strict_lim), 0.0, NEG)
    low = jnp.where(noisy, bi, 0)
    seen = (bj <= bi) & (bj >= low) & (j + base < length)
    bias[:, 2 * n : 3 * n] = jnp.where(seen | (i == j), 0.0, NEG)


def attend_kernel(
    info, x_ref, af_ref, as_ref, q_ref, ko_ref, vo_ref, w_ref, cosf_ref, sinf_ref,
    cos_ref, sin_ref, gain_ref,
    o_ref, lse_ref, xm_ref, m_ref, kf_ref, vf_ref, ks_ref, vs_ref,
    tmp, bias,
):
    n, d = x_ref.shape
    pairs = d // 128
    for src, kk, vv, c, s in (
        (af_ref, kf_ref, vf_ref, cosf_ref, sinf_ref),
        (as_ref, ks_ref, vs_ref, cos_ref, sin_ref),
    ):
        a = src[...]
        tmp[...] = mm(a, w_ref[:, d : 2 * d])
        for g in range(pairs):
            sl = slice(g * 128, g * 128 + 128)
            kk[:, sl] = turn(tmp[:, sl], c[...], s[...]).astype(BF)
        vv[...] = mm(a, w_ref[:, 2 * d : 3 * d]).astype(BF)
    make_bias(info, bias)
    lane = lax.broadcasted_iota(jnp.int32, (QB, 128), 1)
    lse_ref[...] = jnp.zeros_like(lse_ref)

    def pair(g, carry):
        sl = pl.ds(pl.multiple_of(g * 128, 128), 128)
        for b in range(n // QB):
            rs = slice(b * QB, b * QB + QB)
            width = (b + 1) * QB
            q2 = q_ref[rs, sl] * SCALE
            keys = (kf_ref[:, sl], ks_ref[0:width, sl], ko_ref[0:width, sl])
            vals = (vf_ref[:, sl], vs_ref[0:width, sl], vo_ref[0:width, sl])
            bs = (
                bias[rs, 0:n],
                bias[rs, n : n + width],
                bias[rs, 2 * n : 2 * n + width],
            )
            outs = []
            for h in range(2):
                mine = (lane < HD) if h == 0 else (lane >= HD)
                qh = jnp.where(mine, q2, jnp.zeros_like(q2))
                sc = [mm(qh, k, NT) + bb for k, bb in zip(keys, bs)]
                top = functools.reduce(
                    jnp.maximum, [jnp.max(s, axis=-1, keepdims=True) for s in sc]
                )
                ex = [jnp.exp(s - top) for s in sc]
                tot = functools.reduce(
                    jnp.add, [jnp.sum(e, axis=-1, keepdims=True) for e in ex]
                )
                acc = functools.reduce(
                    jnp.add, [mm(e.astype(BF), v) for e, v in zip(ex, vals)]
                )
                outs.append(acc / tot)
                head = 2 * g + h
                lse_ref[rs, :] = jnp.where(lane == head, top + jnp.log(tot), lse_ref[rs, :])
            o_ref[rs, sl] = jnp.where(lane < HD, outs[0], outs[1]).astype(BF)
        return carry

    lax.fori_loop(0, pairs, pair, 0)
    xm = x_ref[...].astype(F32) + mm(o_ref[...], w_ref[:, 3 * d : 4 * d], NT)
    xm_ref[...] = xm
    xh, _ = norm_stats(xm)
    m_ref[...] = (xh * gain_ref[...]).astype(BF)


def attend(info, x, af, as_, q, ko, vo, w, cosf, sinf, cos, sin, gain):
    n, d = x.shape
    sd = jax.ShapeDtypeStruct((n, d), BF)
    return pl.pallas_call(
        attend_kernel,
        out_shape=(
            sd,
            jax.ShapeDtypeStruct((n, 128), F32),
            jax.ShapeDtypeStruct((n, d), F32),
            sd, sd, sd, sd, sd,
        ),
        in_specs=[smem()] + vmem(12),
        out_specs=tuple(vmem(8)),
        scratch_shapes=[pltpu.VMEM((n, d), F32), pltpu.VMEM((n, 3 * n), F32)],
        compiler_params=params(),
        cost_estimate=cost(10 * n * d * d + 40 * QB * QB * d * 4, 2 * (4 * d * d + 12 * n * d)),
        name="attend",
    )(info, x, af, as_, q, ko, vo, w, cosf, sinf, cos, sin, gain)


def gelu(u):
    return 0.5 * u * (1.0 + jnp.tanh(GC * (u + GA * (u * u * u))))


def mlp_kernel(xm_ref, m_ref, up_ref, dn_ref, gain_ref, x_ref, a_ref, u_ref, acc):
    step = pl.program_id(0)

    @pl.when(step == 0)
    def _():
        acc[...] = xm_ref[...]

    u = mm(m_ref[...], up_ref[...])
    u_ref[...] = u.astype(BF)
    acc[...] += mm(gelu(u).astype(BF), dn_ref[...], NT)

    @pl.when(step == pl.num_programs(0) - 1)
    def _():
        x = acc[...]
        x_ref[...] = x
        xh, _ = norm_stats(x)
        a_ref[...] = (xh * gain_ref[...]).astype(BF)


def mlp(xm, m, w, gain, fc=512):
    n, d = xm.shape
    ff = w.shape[1] // 2
    steps = ff // fc
    full = pl.BlockSpec((n, d), lambda i: (0, 0))
    return pl.pallas_call(
        mlp_kernel,
        grid=(steps,),
        out_shape=(
            jax.ShapeDtypeStruct((n, d), F32),
            jax.ShapeDtypeStruct((n, d), BF),
            jax.ShapeDtypeStruct((n, ff), BF),
        ),
        in_specs=[
            full,
            full,
            pl.BlockSpec((d, fc), lambda i: (0, i)),
            pl.BlockSpec((d, fc), lambda i: (0, i + steps)),
            pl.BlockSpec((1, d), lambda i: (0, 0)),
        ],
        out_specs=(full, full, pl.BlockSpec((n, fc), lambda i: (0, i))),
        scratch_shapes=[pltpu.VMEM((n, d), F32)],
        compiler_params=params(),
        cost_estimate=cost(4 * n * d * ff, 4 * d * ff + 2 * n * ff + 10 * n * d),
        name="mlp",
    )(xm, m, w, w, gain)


def mlp_back_kernel(
    g_ref, xm_ref, m_ref, u_ref, up_ref, dn_ref, gain_ref,
    gm_ref, go_ref, dup_ref, ddn_ref, dgain_ref,
    gy, gyt, mt, dm,
):
    step = pl.program_id(0)

    @pl.when(step == 0)
    def _():
        gb = g_ref[...].astype(BF)
        gy[...] = gb
        gyt[...] = gb.T
        mt[...] = m_ref[...].T
        dm[...] = jnp.zeros_like(dm)

    u = u_ref[...].astype(F32)
    dh = mm(gy[...], dn_ref[...])
    u2 = u * u
    th = jnp.tanh(GC * (u + GA * (u2 * u)))
    half = 0.5 * (1.0 + th)
    h = (u * half).astype(BF)
    slope = half + 0.5 * u * (1.0 - th * th) * (GC * (1.0 + 3.0 * GA * u2))
    du = (dh * slope).astype(BF)
    dm[...] += mm(du, up_ref[...], NT)
    dup_ref[...] = mm(mt[...], du).astype(BF)
    ddn_ref[...] = mm(gyt[...], h).astype(BF)

    @pl.when(step == pl.num_programs(0) - 1)
    def _():
        dz, dgain = norm_back(xm_ref[...], gain_ref[...], dm[...])
        gm = g_ref[...] + dz
        gm_ref[...] = gm
        go_ref[...] = gm.astype(BF)
        dgain_ref[...] = dgain


def mlp_back(g, xm, m, u, w, gain, fc=512):
    n, d = xm.shape
    ff = w.shape[1] // 2
    steps = ff // fc
    full = pl.BlockSpec((n, d), lambda i: (0, 0))
    row = pl.BlockSpec((1, d), lambda i: (0, 0))
    wide = pl.BlockSpec((d, fc), lambda i: (0, i))
    return pl.pallas_call(
        mlp_back_kernel,
        grid=(steps,),
        out_shape=(
            jax.ShapeDtypeStruct((n, d), F32),
            jax.ShapeDtypeStruct((n, d), BF),
            jax.ShapeDtypeStruct((d, ff), BF),
            jax.ShapeDtypeStruct((d, ff), BF),
            jax.ShapeDtypeStruct((1, d), F32),
        ),
        in_specs=[
            full,
            full,
            full,
            pl.BlockSpec((n, fc), lambda i: (0, i)),
            wide,
            pl.BlockSpec((d, fc), lambda i: (0, i + steps)),
            row,
        ],
        out_specs=(full, full, wide, wide, row),
        scratch_shapes=[
            pltpu.VMEM((n, d), BF),
            pltpu.VMEM((d, n), BF),
            pltpu.VMEM((d, n), BF),
            pltpu.VMEM((n, d), F32),
        ],
        compiler_params=params(),
        cost_estimate=cost(8 * n * d * ff, 8 * d * ff + 2 * n * ff + 16 * n * d),
        name="mlp_back",
    )(g, xm, m, u, w, w, gain)


def attend_back_kernel(
    info, go_ref, o_ref, lse_ref, q_ref, kf_ref, vf_ref, ks_ref, vs_ref, ko_ref, vo_ref,
    w_ref, cosf_ref, sinf_ref, cos_ref, sin_ref,
    dq_ref, dkf_ref, dvf_ref, dks_ref, dvs_ref, dko_ref, dvo_ref, daf_ref, das_ref, dao_ref,
    do_s, bias, dqa, dka, dva,
):
    n, d = go_ref.shape
    pairs = d // 128
    make_bias(info, bias)
    do_s[...] = mm(go_ref[...], w_ref[:, 3 * d : 4 * d]).astype(BF)
    lane_q = lax.broadcasted_iota(jnp.int32, (QB, 128), 1)

    def pair(g, carry):
        sl = pl.ds(pl.multiple_of(g * 128, 128), 128)
        dqa[...] = jnp.zeros_like(dqa)
        dka[...] = jnp.zeros_like(dka)
        dva[...] = jnp.zeros_like(dva)
        for b in range(n // QB):
            rs = slice(b * QB, b * QB + QB)
            q2 = q_ref[rs, sl] * SCALE
            do2 = do_s[rs, sl]
            prod = do2.astype(F32) * o_ref[rs, sl].astype(F32)
            lses = lse_ref[rs, :]
            for h in range(2):
                mine = (lane_q < HD) if h == 0 else (lane_q >= HD)
                qh = jnp.where(mine, q2, jnp.zeros_like(q2))
                doh = jnp.where(mine, do2, jnp.zeros_like(do2))
                dsum = jnp.sum(jnp.where(mine, prod, 0.0), axis=-1, keepdims=True)
                ls = jnp.sum(
                    jnp.where(lane_q == 2 * g + h, lses, 0.0), axis=-1, keepdims=True
                )
                for seg, (kr, vr) in enumerate(
                    ((kf_ref, vf_ref), (ks_ref, vs_ref), (ko_ref, vo_ref))
                ):
                    tiles = n // QB if seg == 0 else b + 1
                    for c in range(tiles):
                        cs = slice(c * QB, c * QB + QB)
                        col = seg * n + c * QB
                        k2 = kr[cs, sl]
                        v2 = vr[cs, sl]
                        s = mm(qh, k2, NT) + bias[rs, col : col + QB]
                        p = jnp.exp(s - ls)
                        dp = mm(doh, v2, NT)
                        ds = (p * (dp - dsum)).astype(BF)
                        pb = p.astype(BF)
                        acc = slice(seg * n + c * QB, seg * n + c * QB + QB)
                        dva[acc, :] += mm(pb, doh, TN)
                        dka[acc, :] += mm(ds, qh, TN)
                        kh = jnp.where(mine, k2, jnp.zeros_like(k2))
                        dqa[rs, :] += mm(ds, kh)
        dq_ref[:, sl] = turn(dqa[...] * SCALE, cos_ref[...], -sin_ref[...]).astype(BF)
        dkf_ref[:, sl] = turn(dka[0:n, :], cosf_ref[...], -sinf_ref[...]).astype(BF)
        dks_ref[:, sl] = turn(dka[n : 2 * n, :], cos_ref[...], -sin_ref[...]).astype(BF)
        dko_ref[:, sl] = turn(dka[2 * n : 3 * n, :], cos_ref[...], -sin_ref[...]).astype(BF)
        dvf_ref[:, sl] = dva[0:n, :].astype(BF)
        dvs_ref[:, sl] = dva[n : 2 * n, :].astype(BF)
        dvo_ref[:, sl] = dva[2 * n : 3 * n, :].astype(BF)
        return carry

    lax.fori_loop(0, pairs, pair, 0)
    wk = w_ref[:, d : 2 * d]
    wv = w_ref[:, 2 * d : 3 * d]
    daf_ref[...] = (mm(dkf_ref[...], wk, NT) + mm(dvf_ref[...], wv, NT)).astype(BF)
    das_ref[...] = (mm(dks_ref[...], wk, NT) + mm(dvs_ref[...], wv, NT)).astype(BF)
    dao_ref[...] = (
        mm(dko_ref[...], wk, NT) + mm(dvo_ref[...], wv, NT) + mm(dq_ref[...], w_ref[:, 0:d], NT)
    )


def attend_back(info, go, o, lse, q, kf, vf, ks, vs, ko, vo, w, cosf, sinf, cos, sin):
    n, d = go.shape
    sd = jax.ShapeDtypeStruct((n, d), BF)
    return pl.pallas_call(
        attend_back_kernel,
        out_shape=(sd,) * 9 + (jax.ShapeDtypeStruct((n, d), F32),),
        in_specs=[smem()] + vmem(15),
        out_specs=tuple(vmem(10)),
        scratch_shapes=[
            pltpu.VMEM((n, d), BF),
            pltpu.VMEM((n, 3 * n), F32),
            pltpu.VMEM((n, 128), F32),
            pltpu.VMEM((3 * n, 128), F32),
            pltpu.VMEM((3 * n, 128), F32),
        ],
        compiler_params=params(),
        cost_estimate=cost(16 * n * d * d + 100 * QB * QB * d * 4, 2 * (4 * d * d + 24 * n * d)),
        name="attend_back",
    )(info, go, o, lse, q, kf, vf, ks, vs, ko, vo, w, cosf, sinf, cos, sin)


def weight_kernel(
    ao_ref, af_ref, as_ref, go_ref, o_ref, dq_ref, dkf_ref, dvf_ref, dks_ref, dvs_ref,
    dko_ref, dvo_ref, dw_ref,
):
    n, d = ao_ref.shape
    aot = ao_ref[...].T
    aft = af_ref[...].T
    ast = as_ref[...].T
    dw_ref[:, 0:d] = mm(aot, dq_ref[...]).astype(BF)
    dw_ref[:, d : 2 * d] = (
        mm(aot, dko_ref[...]) + mm(aft, dkf_ref[...]) + mm(ast, dks_ref[...])
    ).astype(BF)
    dw_ref[:, 2 * d : 3 * d] = (
        mm(aot, dvo_ref[...]) + mm(aft, dvf_ref[...]) + mm(ast, dvs_ref[...])
    ).astype(BF)
    dw_ref[:, 3 * d : 4 * d] = mm(go_ref[...].T, o_ref[...]).astype(BF)


def weight_grads(ao, af, as_, go, o, dq, dkf, dvf, dks, dvs, dko, dvo):
    n, d = ao.shape
    return pl.pallas_call(
        weight_kernel,
        out_shape=jax.ShapeDtypeStruct((d, 4 * d), BF),
        in_specs=vmem(12),
        out_specs=pl.BlockSpec(memory_space=pltpu.VMEM),
        compiler_params=params(),
        cost_estimate=cost(16 * n * d * d, 2 * (4 * d * d + 12 * n * d)),
        name="weight_grads",
    )(ao, af, as_, go, o, dq, dkf, dvf, dks, dvs, dko, dvo)


def norm_back_kernel(gm_ref, x_ref, da_ref, r1_ref, r2_ref, gain_ref, g_ref, dgain_ref):
    da = da_ref[...] + r1_ref[...].astype(F32) + r2_ref[...].astype(F32)
    dz, dgain = norm_back(x_ref[...].astype(F32), gain_ref[...], da)
    g_ref[...] = gm_ref[...] + dz
    dgain_ref[...] = dgain


def norm_back_call(gm, x, da, r1, r2, gain):
    n, d = gm.shape
    return pl.pallas_call(
        norm_back_kernel,
        out_shape=(jax.ShapeDtypeStruct((n, d), F32), jax.ShapeDtypeStruct((1, d), F32)),
        in_specs=vmem(6),
        out_specs=tuple(vmem(2)),
        compiler_params=params(),
        cost_estimate=cost(20 * n * d, 20 * n * d),
        name="norm_back",
    )(gm, x, da, r1, r2, gain)


def first_norm_kernel(x_ref, gain_ref, a_ref):
    xh, _ = norm_stats(x_ref[...].astype(F32))
    a_ref[...] = (xh * gain_ref[...]).astype(BF)


def first_norm(x, gain):
    n, d = x.shape
    return pl.pallas_call(
        first_norm_kernel,
        out_shape=jax.ShapeDtypeStruct((n, d), BF),
        in_specs=vmem(2),
        out_specs=pl.BlockSpec(memory_space=pltpu.VMEM),
        compiler_params=params(),
        cost_estimate=cost(10 * n * d, 4 * n * d),
        name="first_norm",
    )(x, gain)


def send(x, pairs):
    return lax.ppermute(x, "tensor", pairs)


def spread_clean(a, t):
    p1 = send(a, [(2, 3), (3, 1)])
    p2 = send(a, [(2, 1)])
    p3 = send(p2, [(1, 0)])
    return jnp.where(t == 1, p2, p1), jnp.where(t == 1, p1, p3)


def return_clean(daf, das, t):
    q1 = send(das, [(0, 1)])
    q3 = send(jnp.where(t == 1, das, daf), [(1, 3), (3, 2)])
    q2 = send((daf.astype(F32) + q1.astype(F32)).astype(BF), [(1, 2)])
    return q2, q3


def gather_weights(pieces, dp):
    count = lax.axis_size("dp")
    outs = []
    for w in pieces:
        rows = w.shape[0] // count
        mine = lax.dynamic_slice_in_dim(w, dp * rows, rows, 0)
        all_z = lax.all_gather(mine, "tensor", axis=0)
        outs.append(all_z.transpose(1, 0, 2).reshape(rows, -1))
    return lax.all_gather(jnp.concatenate(outs, axis=1), "dp", axis=0, tiled=True)


def reduce_weights(dw, widths):
    zs = lax.axis_size("tensor")
    part = lax.psum_scatter(dw, "dp", scatter_dimension=0, tiled=True)
    rows = part.shape[0]
    at = 0
    cols = []
    for w in widths:
        cols.append(part[:, at : at + w].reshape(rows, zs, w // zs).transpose(1, 0, 2))
        at += w
    mine = lax.psum_scatter(jnp.concatenate(cols, axis=2), "tensor", scatter_dimension=0, tiled=False)
    full = lax.all_gather(mine, "dp", axis=0, tiled=True).astype(F32)
    out = []
    at = 0
    for w in widths:
        out.append(full[:, at : at + w // zs])
        at += w // zs
    return out


def sum_all(x):
    n = lax.axis_size("dp")
    step = 1
    while step < n:
        x = x + lax.ppermute(x, "dp", [(i, i ^ step) for i in range(n)])
        step *= 2
    for step in (1, 2):
        x = x + lax.ppermute(x, "tensor", [(i, i ^ step) for i in range(4)])
    return x


def on_device(
    tokens, lengths, noise_mask, cotangent, attn_gain, query_weight, key_weight, value_weight,
    out_weight, mlp_gain, up_weight, down_weight,
):
    n, d = tokens.shape
    dp = lax.axis_index("dp")
    t = lax.axis_index("tensor")
    info = jnp.stack([lengths[0], t]).astype(jnp.int32)
    base = (t % 2) * n

    position = jnp.arange(LMAX, dtype=jnp.int32).astype(F32)
    frequency = jnp.exp(
        -math.log(10000.0) * jnp.arange(HD // 2, dtype=jnp.int32).astype(F32) / (HD // 2)
    )
    angles = position[:, None] * frequency[None, :]
    cos1 = jnp.cos(angles)
    sin1 = jnp.sin(angles)
    cos_all = jnp.concatenate([cos1] * 4, axis=1)
    sin_all = jnp.concatenate([-sin1, sin1] * 2, axis=1)
    cosf, sinf = cos_all[:n], sin_all[:n]
    cos = lax.dynamic_slice_in_dim(cos_all, base, n, 0)
    sin = lax.dynamic_slice_in_dim(sin_all, base, n, 0)

    pos = base + jnp.arange(n, dtype=jnp.int32)
    masked = lax.dynamic_slice_in_dim(noise_mask[0], base, n, 0)
    weight = ((pos < lengths[0]) & ((t >= 2) | (masked == 1))).astype(F32)

    wa = []
    wm = []
    for layer in range(LAYERS):
        wa.append(
            gather_weights(
                [query_weight[layer], key_weight[layer], value_weight[layer], out_weight[layer].T],
                dp,
            )
        )
        wm.append(gather_weights([up_weight[layer], down_weight[layer].T], dp))

    saved = []
    x = tokens
    a = first_norm(tokens, attn_gain[0:1])
    for layer in range(LAYERS):
        af, as_ = spread_clean(a, t)
        q, ko, vo = project_own(a, wa[layer], cos, sin)
        o, lse, xm, m, kf, vf, ks, vs = attend(
            info, x, af, as_, q, ko, vo, wa[layer], cosf, sinf, cos, sin, mlp_gain[layer : layer + 1]
        )
        nxt = min(layer + 1, LAYERS - 1)
        x_next, a_next, u = mlp(xm, m, wm[layer], attn_gain[nxt : nxt + 1])
        saved.append((x, a, af, as_, q, kf, vf, ks, vs, ko, vo, o, lse, xm, m, u))
        x, a = x_next, a_next
    block_out = x

    g = cotangent.astype(F32) * weight[:, None]
    gains = [None] * (2 * LAYERS)
    grads = [None] * LAYERS
    for layer in reversed(range(LAYERS)):
        x, a, af, as_, q, kf, vf, ks, vs, ko, vo, o, lse, xm, m, u = saved[layer]
        gm, go, dup, ddn, gains[LAYERS + layer] = mlp_back(
            g, xm, m, u, wm[layer], mlp_gain[layer : layer + 1]
        )
        dq, dkf, dvf, dks, dvs, dko, dvo, daf, das, dao = attend_back(
            info, go, o, lse, q, kf, vf, ks, vs, ko, vo, wa[layer], cosf, sinf, cos, sin
        )
        r1, r2 = return_clean(daf, das, t)
        dwa = weight_grads(a, af, as_, go, o, dq, dkf, dvf, dks, dvs, dko, dvo)
        ups = reduce_weights(jnp.concatenate([dup, ddn], axis=1), (dup.shape[1], ddn.shape[1]))
        ats = reduce_weights(dwa, (d, d, d, d))
        g, gains[layer] = norm_back_call(gm, x, dao, r1, r2, attn_gain[layer : layer + 1])
        grads[layer] = (ats[0], ats[1], ats[2], ats[3].T, ups[0], ups[1].T)
    gain_sums = sum_all(jnp.concatenate(gains, axis=0))
    stacked = [jnp.stack([grads[layer][i] for layer in range(LAYERS)]) for i in range(6)]
    return (
        block_out, g, gain_sums[:LAYERS], stacked[0], stacked[1], stacked[2], stacked[3],
        gain_sums[LAYERS:], stacked[4], stacked[5],
    )


def solution(mesh):
    rows = P(("dp", "tensor"), None)
    cols = P(None, None, "tensor")
    mids = P(None, "tensor", None)
    return jax.shard_map(
        on_device,
        mesh=mesh,
        in_specs=(
            rows, P("dp"), P("dp", None), rows, P(), cols, cols, cols, mids, P(), cols, mids,
        ),
        out_specs=(rows, rows, P(), cols, cols, cols, mids, P(), cols, mids),
        check_vma=False,
    )
```

time: 1910 us -> 1040 us (0.54)
  waiting for transfers between devices: 1070 us -> 431 us
  matrix products: 398 us -> 0 us
  Pallas kernels: 0 us -> 274 us
  other arithmetic: 219 us -> 53.6 us
  blocking collectives: 41.1 us -> 181 us
  local copies, waits for them, and re-layouts: 131 us -> 45.4 us
  starting transfers between devices: 1.5 us -> 34.6 us
    all_gather x8, waiting for transfers between devices: 499 us -> 54.4 us  [the longest x4 54.4 us: reduce_weights(): full = lax.all_gather(mine, 'dp', axis=0, tiled=True).astype(F32)]
    dot_general x92 -> x0, matrix products: 398 us -> none  [the longest x16 70.6 us: scores_of(): jnp.einsum('qhd,khd->hqk', q_block, k_seq, preferred_element_type=jnp.flo...]
    pallas_call x0 -> x15, Pallas kernels: none -> 274 us  [the longest x2 110 us: attend_back(): pl.pallas_call(attend_back_kernel, out_shape=(sd,) * 9 + (jax.ShapeDtypeS...]
    all_gather x0 -> x12, blocking collectives: none -> 181 us  [gather_weights(): all_z = lax.all_gather(mine, 'tensor', axis=0)]
    psum x1 -> x0, waiting for transfers between devices: 150 us -> none  [on_device(): lax.psum((stacked[1], stacked[2], stacked[3], stacked[4], stacked[6], sta...]
    reduce_scatter x8, waiting for transfers between devices: 424 us -> 283 us  [the longest x4 197 us: reduce_weights(): part = lax.psum_scatter(dw, 'dp', scatter_dimension=0, tiled=True)]
    ppermute x0 -> x17, waiting for transfers between devices: none -> 92.9 us  [the longest x12 84 us: send(): return lax.ppermute(x, 'tensor', pairs)]
    reduce_sum x24 -> x0, other arithmetic: 81.8 us -> none  [the longest x8 54.1 us: one_block(): row_sum = jnp.sum(exp_terms, axis=-1, keepdims=True)]
  transfers between devices with their start and end apart: 17 -> 33, of which waited for: 17 -> 19; matrix products, arithmetic and copies ran while one was open for 3% -> 7% of each run, Pallas kernels for 0% -> 17%
where the time goes in v1:
time: 1040 us
  waiting for transfers between devices  431 us (41%)
  Pallas kernels  274 us (26%)
  blocking collectives  181 us (17%)
  other arithmetic  53.6 us (5%)
  local copies, waits for them, and re-layouts  45.4 us (4%)
  starting transfers between devices  34.6 us (3%)
  between operations  16 us (2%)
    reduce_scatter x4, waiting for transfers between devices, reduce_weights(): part = lax.psum_scatter(dw, 'dp', scatter_dimension=0, tiled=True)  197 us
    all_gather x12, blocking collectives, gather_weights(): all_z = lax.all_gather(mine, 'tensor', axis=0)  181 us
    pallas_call x2, Pallas kernels, attend_back(): pl.pallas_call(attend_back_kernel, out_shape=(sd,) * 9 + (jax.ShapeDtypeS...  110 us
    reduce_scatter x4, waiting for transfers between devices, reduce_weights(): lax.psum_scatter(jnp.concatenate(cols, axis=2), 'tensor', scatter_dimensi...  86 us
    ppermute x12, waiting for transfers between devices, send(): return lax.ppermute(x, 'tensor', pairs)  84 us
    all_gather x4, waiting for transfers between devices, reduce_weights(): full = lax.all_gather(mine, 'dp', axis=0, tiled=True).astype(F32)  54.4 us
    pallas_call x2, Pallas kernels, attend(): pl.pallas_call(attend_kernel, out_shape=(sd, jax.ShapeDtypeStruct((n, 128...  50.8 us
    pallas_call x2, Pallas kernels, mlp_back(): pl.pallas_call(mlp_back_kernel, grid=(steps,), out_shape=(jax.ShapeDtypeS...  40.5 us
  transfers between devices with their start and end apart: 33, of which 19 were waited for; matrix products, arithmetic and copies ran while one was open for 7% of the time, Pallas kernels for 17%

profile of v1, /device:TPU:0, one launch (start us, length us, event | category | flops | bytes accessed | tf_op | source)
XLA Modules:
  0.0 1035.3 jit_solution(12903629744654023320)
XLA Ops:
  9.3 15.5 %all_gather.80 = bf16[4,96,192]{2,1,0:T(8,128)(2,1)S(1)} all-gather(bf16[1,96,192]{2,1,0:T(8,128)(2,1)S(1)} %copy.158), channel_id=1, replica_groups=mesh['dp'=8,'tensor'=4] {'tensor'}, dimensions={0}, use_global_device_ids=true | all-gather | bytes 184320 | tf_op jit(solution)/shard_map/all_gather | solution.py:516
  71.7 17.4 %all_gather.86 = bf16[4,96,768]{2,1,0:T(8,128)(2,1)S(1)} all-gather(bf16[1,96,768]{2,1,0:T(8,128)(2,1)S(1)} %constant_dynamic-slice_fusion.8), channel_id=1, replica_groups=mesh['dp'=8,'tensor'=4] {'tensor'}, dimensions={0}, use_global_device_ids=true | all-gather | bytes 737280 | tf_op jit(solution)/shard_map/all_gather | solution.py:516
  89.7 15.5 %all-gather.1 = bf16[384,768]{1,0:T(8,128)(2,1)S(1)} all-gather(bf16[96,768]{1,0:T(8,128)(2,1)S(1)} %bitcast.177), channel_id=3, replica_groups=mesh['dp'=8,'tensor'=4] {'tensor'}, dimensions={0}, use_global_device_ids=true | all-gather | bytes 737280 | tf_op jit(solution)/shard_map/all_gather | solution.py:516
  152.1 14.3 %all-gather.2 = bf16[384,192]{1,0:T(8,128)(2,1)S(1)} all-gather(bf16[96,192]{1,0:T(8,128)(2,1)S(1)} %bitcast.180), channel_id=4, replica_groups=mesh['dp'=8,'tensor'=4] {'tensor'}, dimensions={0}, use_global_device_ids=true | all-gather | bytes 184320 | tf_op jit(solution)/shard_map/all_gather | solution.py:516
  167.7 17.8 %all_gather.96 = bf16[4,96,768]{2,1,0:T(8,128)(2,1)S(1)} all-gather(bf16[1,96,768]{2,1,0:T(8,128)(2,1)S(1)} %constant_dynamic-slice_fusion.2), channel_id=1, replica_groups=mesh['dp'=8,'tensor'=4] {'tensor'}, dimensions={0}, use_global_device_ids=true | all-gather | bytes 737280 | tf_op jit(solution)/shard_map/all_gather | solution.py:516
  185.6 18.1 %all-gather.3 = bf16[384,768]{1,0:T(8,128)(2,1)S(1)} all-gather(bf16[96,768]{1,0:T(8,128)(2,1)S(1)} %bitcast.178), channel_id=5, replica_groups=mesh['dp'=8,'tensor'=4] {'tensor'}, dimensions={0}, use_global_device_ids=true | all-gather | bytes 737280 | tf_op jit(solution)/shard_map/all_gather | solution.py:516
  217.7 25.8 %collective-permute-done.2 = bf16[512,768]{1,0:T(8,128)(2,1)S(1)} collective-permute-done((bf16[512,768]{1,0:T(8,128)(2,1)S(1)}, bf16[512,768]{1,0:T(8,128)(2,1)S(1)}, u32[]{:S(2)}, u32[]{:S(2)}) %collective-permute-start.2) | collective-permute-done | bytes 786464 | tf_op jit(solution)/shard_map/ppermute | solution.py:493
  252.0 25.3 %attend.2 = (bf16[512,768]{1,0:T(8,128)(2,1)}, f32[512,128]{1,0:T(8,128)}, f32[512,768]{1,0:T(8,128)}, bf16[512,768]{1,0:T(8,128)(2,1)}, bf16[512,768]{1,0:T(8,1...) custom-call(s32[2]{0:T(128)} %pad_add_fusion.info, ...), custom_call_target="tpu_custom_call" | custom-call | flops 11072962560 | bytes 14155776 | tf_op jit(solution)/shard_map/attend/pallas_call | solution.py:190
  300.1 21.6 %collective-permute-done.5 = bf16[512,768]{1,0:T(8,128)(2,1)S(1)} collective-permute-done((bf16[512,768]{1,0:T(8,128)(2,1)S(1)}, bf16[512,768]{1,0:T(8,128)(2,1)S(1)}, u32[]{:S(2)}, u32[]{:S(2)}) %collective-permute-start.5) | collective-permute-done | bytes 786464 | tf_op jit(solution)/shard_map/ppermute | solution.py:493
  323.1 25.5 %attend.3 = (bf16[512,768]{1,0:T(8,128)(2,1)}, f32[512,128]{1,0:T(8,128)}, f32[512,768]{1,0:T(8,128)}, bf16[512,768]{1,0:T(8,128)(2,1)}, bf16[512,768]{1,0:T(8,1...) custom-call(s32[2]{0:T(128)} %pad_add_fusion.info, ...), custom_call_target="tpu_custom_call" | custom-call | flops 11072962560 | bytes 14155776 | tf_op jit(solution)/shard_map/attend/pallas_call | solution.py:190
  360.9 19.7 %mlp_back.2 = (f32[512,768]{1,0:T(8,128)}, bf16[512,768]{1,0:T(8,128)(2,1)}, bf16[768,3072]{1,0:T(8,128)(2,1)}, bf16[768,3072]{1,0:T(8,128)(2,1)}, f32[1,768]{1,0:T(1,128)}) custom-call(f32[512,768]{1,0:T(8,128)} %convert_multiply_fusion.g_ref, f32[512,768]{1,0:T(8,128)} %get-tuple-element.81.xm_ref, bf16[512,768]{1,0:T(8,128)(2,1)} %get-tuple-element.82.m_ref, ...), custom_call_target="tpu_custom_call" | custom-call | flops 9663676416 | bytes 28311552 | tf_op jit(solution)/shard_map/mlp_back/pallas_call | solution.py:301
  380.7 55.1 %attend_back.2 = (bf16[512,768]{1,0:T(8,128)(2,1)}, bf16[512,768]{1,0:T(8,128)(2,1)}, bf16[512,768]{1,0:T(8,128)(2,1)}, bf16[512,768]{1,0:T(8,128)(2,1)}, bf16[5...) custom-call(s32[2]{0:T(128)} %pad_add_fusion.info, ...), custom_call_target="tpu_custom_call" | custom-call | flops 24964497408 | bytes 23592960 | tf_op jit(solution)/shard_map/attend_back/pallas_call | solution.py:405
  465.9 20.7 %mlp_back.3 = (f32[512,768]{1,0:T(8,128)}, bf16[512,768]{1,0:T(8,128)(2,1)}, bf16[768,3072]{1,0:T(8,128)(2,1)}, bf16[768,3072]{1,0:T(8,128)(2,1)}, f32[1,768]{1,0:T(1,128)}) custom-call(f32[512,768]{1,0:T(8,128)} %get-tuple-element.96.g_ref, f32[512,768]{1,0:T(8,128)} %get-tuple-element.74.xm_ref, bf16[512,768]{1,0:T(8,128)(2,1)} %get-tuple-element.75.m_ref, ...), custom_call_target="tpu_custom_call" | custom-call | flops 9663676416 | bytes 28311552 | tf_op jit(solution)/shard_map/mlp_back/pallas_call | solution.py:301
  486.6 55.0 %attend_back.3 = (bf16[512,768]{1,0:T(8,128)(2,1)}, bf16[512,768]{1,0:T(8,128)(2,1)}, bf16[512,768]{1,0:T(8,128)(2,1)}, bf16[512,768]{1,0:T(8,128)(2,1)}, bf16[5...) custom-call(s32[2]{0:T(128)} %pad_add_fusion.info, ...), custom_call_target="tpu_custom_call" | custom-call | flops 24964497408 | bytes 23592960 | tf_op jit(solution)/shard_map/attend_back/pallas_call | solution.py:405
  574.2 42.8 %reduce-scatter.9.cloned.1.call-done = bf16[96,3072]{1,0:T(8,128)(2,1)} async-done(((bf16[768,3072]{1,0:T(8,128)(2,1)}), bf16[96,3072]{1,0:T(8,128)(2,1)}) %reduce-scatter.9.cloned.1.call-update) | async-done | bytes 589840 | tf_op jit(solution)/shard_map/reduce_scatter | solution.py:523
  620.3 76.8 %reduce-scatter.21.cloned.1.call-done = bf16[96,6144]{1,0:T(8,128)(2,1)} async-done(((bf16[768,6144]{1,0:T(8,128)(2,1)}), bf16[96,6144]{1,0:T(8,128)(2,1)}) %reduce-scatter.21.cloned.1.call-update) | async-done | bytes 1179664 | tf_op jit(solution)/shard_map/reduce_scatter | solution.py:523
  699.7 77.4 %reduce-scatter.17.cloned.1.call-done = bf16[96,6144]{1,0:T(8,128)(2,1)} async-done(((bf16[768,6144]{1,0:T(8,128)(2,1)}), bf16[96,6144]{1,0:T(8,128)(2,1)}) %reduce-scatter.17.cloned.1.call-update) | async-done | bytes 1179664 | tf_op jit(solution)/shard_map/reduce_scatter | solution.py:523
  779.8 22.3 %reduce-scatter.15.cloned.1.call-done = bf16[1,96,768]{2,1,0:T(8,128)(2,1)} async-done(((bf16[4,96,768]{2,1,0:T(8,128)(2,1)}), bf16[1,96,768]{2,1,0:T(8,128)(2,1)}) %reduce-scatter.15.cloned.1.call-update) | async-done | bytes 147472 | tf_op jit(solution)/shard_map/reduce_scatter | solution.py:530
  802.1 23.0 %reduce-scatter.11.cloned.1.call-done = bf16[1,96,768]{2,1,0:T(8,128)(2,1)} async-done(((bf16[4,96,768]{2,1,0:T(8,128)(2,1)}), bf16[1,96,768]{2,1,0:T(8,128)(2,1)}) %reduce-scatter.11.cloned.1.call-update) | async-done | bytes 147472 | tf_op jit(solution)/shard_map/reduce_scatter | solution.py:530
  825.2 30.3 %reduce-scatter.23.cloned.1.call-done = bf16[1,96,1536]{2,1,0:T(8,128)(2,1)} async-done(((bf16[4,96,1536]{2,1,0:T(8,128)(2,1)}), bf16[1,96,1536]{2,1,0:T(8,128)(2,1)}) %reduce-scatter.23.cloned.1.call-update) | async-done | bytes 294928 | tf_op jit(solution)/shard_map/reduce_scatter | solution.py:530
  857.9 27.9 %collective-permute-done.9 = bf16[512,768]{1,0:T(8,128)(2,1)S(1)} collective-permute-done((bf16[512,768]{1,0:T(8,128)(2,1)S(1)}, bf16[512,768]{1,0:T(8,128)(2,1)S(1)}, u32[]{:S(2)}, u32[]{:S(2)}) %collective-permute-start.9) | collective-permute-done | bytes 786464 | tf_op jit(solution)/shard_map/ppermute | solution.py:493
  914.4 14.8 %collective-permute-start.15 = (f32[4,768]{1,0:T(4,128)S(1)}, f32[4,768]{1,0:T(4,128)S(1)}, u32[]{:S(2)}, u32[]{:S(2)}) collective-permute-start(f32[4,768]{1,0:T(4,128)S(1)} %add.79), channel_id=1, source_target_pairs={{0,1},{1,0},{2,3},{3,2},{4,5},{5,4},{6,7},{7,6},{8,9},{9,8},{10,11... | collective-permute-start | bytes 36872 | tf_op jit(solution)/shard_map/ppermute | solution.py:547
  961.4 18.6 %all-gather.31.cloned.1.call-done = bf16[1,768,1536]{2,1,0:T(8,128)(2,1)} async-done(((bf16[1,96,1536]{2,1,0:T(8,128)(2,1)}), bf16[1,768,1536]{2,1,0:T(8,128)(2,1)}) %all-gather.31.cloned.1.call-update) | async-done | bytes 2359312 | tf_op jit(solution)/shard_map/all_gather | solution.py:531
  984.1 26.7 %all-gather.29.cloned.1.call-done = bf16[1,768,1536]{2,1,0:T(8,128)(2,1)} async-done(((bf16[1,96,1536]{2,1,0:T(8,128)(2,1)}), bf16[1,768,1536]{2,1,0:T(8,128)(2,1)}) %all-gather.29.cloned.1.call-update) | async-done | bytes 2359312 | tf_op jit(solution)/shard_map/all_gather | solution.py:531
  (257 shorter events, 311.4 us)
Async XLA Ops:
  7.2 237.6 %all-gather.17.cloned.1.call-start = ((), (), s32[]{:S(2)}) async-start(), calls=%async_computation.8 | async-start | bytes 5308416 | tf_op jit(solution)/shard_map/all_gather | solution.py:518
  71.5 205.9 %all-gather.19.cloned.1.call-start = ((), (), s32[]{:S(2)}) async-start(), calls=%async_computation.9 | async-start | bytes 10616832 | tf_op jit(solution)/shard_map/all_gather | solution.py:518
  106.5 187.7 %all-gather.21.cloned.1.call-start = ((), (), s32[]{:S(2)}) async-start(), calls=%async_computation.10 | async-start | bytes 5308416 | tf_op jit(solution)/shard_map/all_gather | solution.py:518
  167.6 181.0 %all-gather.23.cloned.1.call-start = ((), (), s32[]{:S(2)}) async-start(), calls=%async_computation.11 | async-start | bytes 10616832 | tf_op jit(solution)/shard_map/all_gather | solution.py:518
  204.9 366.0 %reduce-scatter.13.cloned.1.call-start = ((), (), s32[]{:S(2)}) async-start(), calls=%async_computation.14 | async-start | bytes 5308416 | tf_op jit(solution)/shard_map/reduce_scatter | solution.py:523
  213.0 30.5 %collective-permute-start.2 = (bf16[512,768]{1,0:T(8,128)(2,1)S(1)}, bf16[512,768]{1,0:T(8,128)(2,1)S(1)}, u32[]{:S(2)}, u32[]{:S(2)}) collective-permute-start(bf16[512,768]{1,0:T(8,128)(2,1)S(1)} %collective-permute-done), channel_id=1, source_target_pairs={{1,0},{5,4},{9,8},{13,12},{17,16},{21,20},{25,24},{29,28}} | collective-permute-start | bytes 2359304 | tf_op jit(solution)/shard_map/ppermute | solution.py:493
  291.2 30.5 %collective-permute-start.5 = (bf16[512,768]{1,0:T(8,128)(2,1)S(1)}, bf16[512,768]{1,0:T(8,128)(2,1)S(1)}, u32[]{:S(2)}, u32[]{:S(2)}) collective-permute-start(bf16[512,768]{1,0:T(8,128)(2,1)S(1)} %collective-permute-done.3), channel_id=1, source_target_pairs={{1,0},{5,4},{9,8},{13,12},{17,16},{21,20},{25,24},{29,28}} | collective-permute-start | bytes 2359304 | tf_op jit(solution)/shard_map/ppermute | solution.py:493
  446.7 170.4 %reduce-scatter.9.cloned.1.call-start = ((), (), s32[]{:S(2)}) async-start(), calls=%async_computation.12 | async-start | bytes 5308416 | tf_op jit(solution)/shard_map/reduce_scatter | solution.py:523
  447.8 10.9 %collective-permute-start.6 = (bf16[512,768]{1,0:T(8,128)(2,1)S(1)}, bf16[512,768]{1,0:T(8,128)(2,1)S(1)}, u32[]{:S(2)}, u32[]{:S(2)}) collective-permute-start(bf16[512,768]{1,0:T(8,128)(2,1)S(1)} %copy-done.8), channel_id=1, source_target_pairs={{0,1},{4,5},{8,9},{12,13},{16,17},{20,21},{24,25},{28,29}} | collective-permute-start | bytes 2359304 | tf_op jit(solution)/shard_map/ppermute | solution.py:493
  449.4 10.2 collective-permute-start.8
  552.6 144.5 %reduce-scatter.21.cloned.1.call-start = ((), (), s32[]{:S(2)}) async-start(), calls=%async_computation.18 | async-start | bytes 10616832 | tf_op jit(solution)/shard_map/reduce_scatter | solution.py:523
  561.7 215.5 %reduce-scatter.17.cloned.1.call-start = ((), (), s32[]{:S(2)}) async-start(), calls=%async_computation.16 | async-start | bytes 10616832 | tf_op jit(solution)/shard_map/reduce_scatter | solution.py:523
  570.8 231.2 %reduce-scatter.15.cloned.1.call-start = ((), (), s32[]{:S(2)}) async-start(), calls=%async_computation.15 | async-start | bytes 737280 | tf_op jit(solution)/shard_map/reduce_scatter | solution.py:530
  574.2 250.9 %reduce-scatter.11.cloned.1.call-start = ((), (), s32[]{:S(2)}) async-start(), calls=%async_computation.13 | async-start | bytes 737280 | tf_op jit(solution)/shard_map/reduce_scatter | solution.py:530
  620.3 235.2 %reduce-scatter.23.cloned.1.call-start = ((), (), s32[]{:S(2)}) async-start(), calls=%async_computation.19 | async-start | bytes 1474560 | tf_op jit(solution)/shard_map/reduce_scatter | solution.py:530
  699.7 197.7 %reduce-scatter.19.cloned.1.call-start = ((), (), s32[]{:S(2)}) async-start(), calls=%async_computation.17 | async-start | bytes 1474560 | tf_op jit(solution)/shard_map/reduce_scatter | solution.py:530
  779.7 157.4 %all-gather.27.cloned.1.call-start = ((), (), s32[]{:S(2)}) async-start(), calls=%async_computation.21 | async-start | bytes 1327104 | tf_op jit(solution)/shard_map/all_gather | solution.py:531
  802.1 147.2 %all-gather.25.cloned.1.call-start = ((), (), s32[]{:S(2)}) async-start(), calls=%async_computation.20 | async-start | bytes 1327104 | tf_op jit(solution)/shard_map/all_gather | solution.py:531
  825.1 154.9 %all-gather.31.cloned.1.call-start = ((), (), s32[]{:S(2)}) async-start(), calls=%async_computation.23 | async-start | bytes 2654208 | tf_op jit(solution)/shard_map/all_gather | solution.py:531
  855.5 155.3 %all-gather.29.cloned.1.call-start = ((), (), s32[]{:S(2)}) async-start(), calls=%async_computation.22 | async-start | bytes 2654208 | tf_op jit(solution)/shard_map/all_gather | solution.py:531
  855.6 30.2 %collective-permute-start.9 = (bf16[512,768]{1,0:T(8,128)(2,1)S(1)}, bf16[512,768]{1,0:T(8,128)(2,1)S(1)}, u32[]{:S(2)}, u32[]{:S(2)}) collective-permute-start(bf16[512,768]{1,0:T(8,128)(2,1)S(1)} %copy-done.7), channel_id=1, source_target_pairs={{0,1},{4,5},{8,9},{12,13},{16,17},{20,21},{24,25},{28,29}} | collective-permute-start | bytes 2359304 | tf_op jit(solution)/shard_map/ppermute | solution.py:493
  857.2 40.2 %collective-permute-start.11 = (bf16[512,768]{1,0:T(8,128)(2,1)S(1)}, bf16[512,768]{1,0:T(8,128)(2,1)S(1)}, u32[]{:S(2)}, u32[]{:S(2)}) collective-permute-start(bf16[512,768]{1,0:T(8,128)(2,1)S(1)} %broadcast_select_fusion), channel_id=1, source_target_pairs={{1,3},{3,2},{5,7},{7,6},{9,11},{11,10},{13,15},{15,14},{17,19},{19... | collective-permute-start | bytes 2359304 | tf_op jit(solution)/shard_map/ppermute | solution.py:493
  886.0 11.4 %collective-permute-start.10 = (bf16[512,768]{1,0:T(8,128)(2,1)S(1)}, bf16[512,768]{1,0:T(8,128)(2,1)S(1)}, u32[]{:S(2)}, u32[]{:S(2)}) collective-permute-start(bf16[512,768]{1,0:T(8,128)(2,1)S(1)} %add_convert_fusion), channel_id=1, source_target_pairs={{1,2},{5,6},{9,10},{13,14},{17,18},{21,22},{25,26},{29,30}} | collective-permute-start | bytes 2359304 | tf_op jit(solution)/shard_map/ppermute | solution.py:493
  914.4 16.4 %collective-permute-start.15 = (f32[4,768]{1,0:T(4,128)S(1)}, f32[4,768]{1,0:T(4,128)S(1)}, u32[]{:S(2)}, u32[]{:S(2)}) collective-permute-start(f32[4,768]{1,0:T(4,128)S(1)} %add.79), channel_id=1, source_target_pairs={{0,1},{1,0},{2,3},{3,2},{4,5},{5,4},{6,7},{7,6},{8,9},{9,8},{10,11... | collective-permute-start | bytes 36872 | tf_op jit(solution)/shard_map/ppermute | solution.py:547
  (33 other events, 372.9 us)
Sparse Core Ops, SparseCore 0:
  71.6 40.0 all-gather.16
  114.1 58.8 all-gather.18
  175.4 38.9 all-gather.20
  216.7 58.8 all-gather.22
  446.8 51.5 reduce-scatter.12
  552.7 64.3 reduce-scatter.8
  620.6 76.4 reduce-scatter.20
  700.6 76.4 reduce-scatter.16
  780.0 22.0 reduce-scatter.14
  804.8 20.2 reduce-scatter.10
  828.0 27.4 reduce-scatter.22
  858.2 39.0 reduce-scatter.18
  899.2 24.1 all-gather.26
  925.2 24.0 all-gather.24
  951.0 29.0 all-gather.30
  981.8 29.0 all-gather.28

commit v2 on v1

--- a/solution.py
+++ b/solution.py
@@ -70,6 +70,243 @@
 
 def cost(flops, nbytes, trans=0):
     return pl.CostEstimate(flops=int(flops), bytes_accessed=int(nbytes), transcendentals=int(trans))
+
+
+MESH = pl.DeviceIdType.MESH
+BITS = 3
+ORDERS = ((0, 1, 2), (0, 2, 1))
+
+
+def bit_of(dp, b):
+    return dp // (1 << b) % 2
+
+
+def slot_of(dp, order):
+    out = 0
+    for b in order:
+        out = out * 2 + bit_of(dp, b)
+    return out
+
+
+def partner(dp, b):
+    return dp + (1 - 2 * bit_of(dp, b)) * (1 << b)
+
+
+def greet():
+    dp = lax.axis_index("dp")
+    t = lax.axis_index("tensor")
+    barrier = pltpu.get_barrier_semaphore()
+    for b in range(BITS):
+        pl.semaphore_signal(barrier, inc=1, device_id=(partner(dp, b), t), device_id_type=MESH)
+    pl.semaphore_wait(barrier, BITS)
+
+
+def aligned(x):
+    return pl.multiple_of(x, 16)
+
+
+class Gather:
+    def __init__(self, piece, whole, send, recv, local):
+        self.piece, self.whole, self.send, self.recv, self.local = piece, whole, send, recv, local
+        self.dp = lax.axis_index("dp")
+        self.t = lax.axis_index("tensor")
+        self.rows = piece.shape[0]
+        self.half = piece.shape[1] // 2
+
+    def cols(self, i):
+        return pl.ds(i * self.half, self.half)
+
+    def own(self, i):
+        slot = slot_of(self.dp, ORDERS[i])
+        return pltpu.make_async_copy(
+            self.piece.at[:, self.cols(i)],
+            self.whole.at[pl.ds(aligned(slot * self.rows), self.rows), self.cols(i)],
+            self.local.at[i],
+        )
+
+    def copy(self, s, i):
+        b = ORDERS[i][BITS - 1 - s]
+        size = self.rows << s
+        at = slot_of(self.dp, ORDERS[i]) // (1 << s) * size
+        there = self.whole.at[pl.ds(aligned(at), size), self.cols(i)]
+        return pltpu.make_async_remote_copy(
+            src_ref=self.piece.at[:, self.cols(i)] if s == 0 else there,
+            dst_ref=there,
+            send_sem=self.send.at[2 * s + i],
+            recv_sem=self.recv.at[2 * s + i],
+            device_id=(partner(self.dp, b), self.t),
+            device_id_type=MESH,
+        )
+
+    def start(self, s):
+        for i in range(2):
+            self.copy(s, i).start()
+            if s == 0:
+                self.own(i).start()
+
+    def wait(self, s):
+        for i in range(2):
+            self.copy(s, i).wait()
+            if s == 0:
+                self.own(i).wait()
+
+    @staticmethod
+    def scratch():
+        return [
+            pltpu.SemaphoreType.DMA((2 * BITS,)),
+            pltpu.SemaphoreType.DMA((2 * BITS,)),
+            pltpu.SemaphoreType.DMA((2,)),
+        ]
+
+
+class Reduce:
+    def __init__(self, src, out, scratch):
+        self.src, self.out = src, out
+        self.keep = scratch[0:2]
+        self.got = (scratch[2 : 2 + BITS], scratch[2 + BITS : 2 + 2 * BITS])
+        self.send, self.recv, self.local = scratch[2 + 2 * BITS :]
+        self.dp = lax.axis_index("dp")
+        self.t = lax.axis_index("tensor")
+        self.full = src[0].shape[0]
+
+    def offset(self, s, i):
+        at = 0
+        for j in range(1, s):
+            at = at + bit_of(self.dp, ORDERS[i][j]) * (self.full >> (j + 1))
+        return at
+
+    def copy(self, s, i):
+        b = ORDERS[i][s]
+        size = self.full >> (s + 1)
+        at = (1 - bit_of(self.dp, b)) * size
+        if s == 0:
+            there = self.src[i].at[pl.ds(aligned(at), size), :]
+        else:
+            there = self.keep[i].at[pl.ds(aligned(self.offset(s, i) + at), size), :]
+        return pltpu.make_async_remote_copy(
+            src_ref=there,
+            dst_ref=self.got[i][s],
+            send_sem=self.send.at[2 * s + i],
+            recv_sem=self.recv.at[2 * s + i],
+            device_id=(partner(self.dp, b), self.t),
+            device_id_type=MESH,
+        )
+
+    def own(self, i):
+        size = self.full // 2
+        at = bit_of(self.dp, ORDERS[i][0]) * size
+        return pltpu.make_async_copy(
+            self.src[i].at[pl.ds(aligned(at), size), :], self.keep[i], self.local.at[i]
+        )
+
+    def start(self, s):
+        for i in range(2):
+            self.copy(s, i).start()
+            if s == 0:
+                self.own(i).start()
+
+    def wait(self, s):
+        for i in range(2):
+            self.copy(s, i).wait()
+            if s == 0:
+                self.own(i).wait()
+            size = self.full >> (s + 1)
+            base = self.offset(s + 1, i)
+            keep, got = self.keep[i], self.got[i][s]
+            last = s == BITS - 1
+            step = 48 if size % 48 == 0 else size
+
+            def add(j, carry):
+                rows = pl.ds(aligned(base + j * step), step)
+                here = pl.ds(aligned(j * step), step)
+                total = (keep[rows, :].astype(F32) + got[here, :].astype(F32)).astype(BF)
+                if last:
+                    self.out[i][here, :] = total
+                else:
+                    keep[rows, :] = total
+                return carry
+
+            lax.fori_loop(0, size // step, add, 0)
+
+    @staticmethod
+    def scratch(full, widths):
+        out = [pltpu.VMEM((full // 2, w), BF) for w in widths]
+        for w in widths:
+            out += [pltpu.VMEM((full >> (s + 1), w), BF) for s in range(BITS)]
+        return out + [
+            pltpu.SemaphoreType.DMA((2 * BITS,)),
+            pltpu.SemaphoreType.DMA((2 * BITS,)),
+            pltpu.SemaphoreType.DMA((2,)),
+        ]
+
+    COUNT = 2 + 2 * BITS + 3
+
+
+def pump(comms, point, points):
+    for s in range(BITS):
+        if s * points // BITS == point:
+            for c in comms:
+                if s > 0:
+                    c.wait(s - 1)
+                c.start(s)
+
+
+def drain(comms):
+    for c in comms:
+        c.wait(BITS - 1)
+
+
+def any_spec(n=1):
+    return [pl.BlockSpec(memory_space=pl.ANY)] * n
+
+
+def begin_kernel(p_ref, w_ref, *sems):
+    greet()
+    comms = [Gather(p_ref, w_ref, *sems)]
+    for point in range(BITS):
+        pump(comms, point, BITS)
+    drain(comms)
+
+
+def gather_call(piece):
+    rows, n = piece.shape
+    return pl.pallas_call(
+        begin_kernel,
+        out_shape=jax.ShapeDtypeStruct((rows << BITS, n), BF),
+        in_specs=vmem(1),
+        out_specs=any_spec()[0],
+        scratch_shapes=Gather.scratch(),
+        compiler_params=params(collective_id=0, has_side_effects=True),
+        cost_estimate=cost(1, 10 * rows * n * 16),
+        name="gather_weights",
+    )(piece)
+
+
+def end_kernel(count, *refs):
+    greet()
+    pieces, wholes, sems = refs[:count], refs[count : 2 * count], refs[2 * count :]
+    comms = [
+        Gather(p, w, *sems[3 * i : 3 * i + 3]) for i, (p, w) in enumerate(zip(pieces, wholes))
+    ]
+    for point in range(BITS):
+        pump(comms, point, BITS)
+    drain(comms)
+
+
+def gather_many(pieces):
+    count = len(pieces)
+    return pl.pallas_call(
+        functools.partial(end_kernel, count),
+        out_shape=tuple(
+            jax.ShapeDtypeStruct((p.shape[0] << BITS, p.shape[1]), BF) for p in pieces
+        ),
+        in_specs=vmem(count),
+        out_specs=tuple(any_spec(count)),
+        scratch_shapes=Gather.scratch() * count,
+        compiler_params=params(collective_id=1, has_side_effects=True),
+        cost_estimate=cost(1, 10 * sum(p.size for p in pieces) * 16),
+        name="gather_grads",
+    )(*pieces)
 
 
 def own_kernel(a_ref, w_ref, cos_ref, sin_ref, q_ref, k_ref, v_ref, tmp):
@@ -123,12 +360,15 @@
 
 def attend_kernel(
     info, x_ref, af_ref, as_ref, q_ref, ko_ref, vo_ref, w_ref, cosf_ref, sinf_ref,
-    cos_ref, sin_ref, gain_ref,
-    o_ref, lse_ref, xm_ref, m_ref, kf_ref, vf_ref, ks_ref, vs_ref,
-    tmp, bias,
+    cos_ref, sin_ref, gain_ref, p_ref,
+    o_ref, lse_ref, xm_ref, m_ref, kf_ref, vf_ref, ks_ref, vs_ref, wn_ref,
+    tmp, bias, *sems,
 ):
     n, d = x_ref.shape
     pairs = d // 128
+    greet()
+    comms = [Gather(p_ref, wn_ref, *sems)]
+    pump(comms, 0, 3)
     for src, kk, vv, c, s in (
         (af_ref, kf_ref, vf_ref, cosf_ref, sinf_ref),
         (as_ref, ks_ref, vs_ref, cos_ref, sin_ref),
@@ -177,14 +417,18 @@
             o_ref[rs, sl] = jnp.where(lane < HD, outs[0], outs[1]).astype(BF)
         return carry
 
-    lax.fori_loop(0, pairs, pair, 0)
+    pump(comms, 1, 3)
+    lax.fori_loop(0, pairs // 2, pair, 0)
+    pump(comms, 2, 3)
+    lax.fori_loop(pairs // 2, pairs, pair, 0)
     xm = x_ref[...].astype(F32) + mm(o_ref[...], w_ref[:, 3 * d : 4 * d], NT)
     xm_ref[...] = xm
     xh, _ = norm_stats(xm)
     m_ref[...] = (xh * gain_ref[...]).astype(BF)
-
-
-def attend(info, x, af, as_, q, ko, vo, w, cosf, sinf, cos, sin, gain):
+    drain(comms)
+
+
+def attend(info, x, af, as_, q, ko, vo, w, cosf, sinf, cos, sin, gain, piece, cid):
     n, d = x.shape
     sd = jax.ShapeDtypeStruct((n, d), BF)
     return pl.pallas_call(
@@ -194,22 +438,49 @@
             jax.ShapeDtypeStruct((n, 128), F32),
             jax.ShapeDtypeStruct((n, d), F32),
             sd, sd, sd, sd, sd,
+            jax.ShapeDtypeStruct((piece.shape[0] << BITS, piece.shape[1]), BF),
         ),
-        in_specs=[smem()] + vmem(12),
-        out_specs=tuple(vmem(8)),
-        scratch_shapes=[pltpu.VMEM((n, d), F32), pltpu.VMEM((n, 3 * n), F32)],
-        compiler_params=params(),
+        in_specs=[smem()] + vmem(13),
+        out_specs=tuple(vmem(8) + any_spec()),
+        scratch_shapes=[pltpu.VMEM((n, d), F32), pltpu.VMEM((n, 3 * n), F32)] + Gather.scratch(),
+        compiler_params=params(collective_id=cid, has_side_effects=True),
         cost_estimate=cost(10 * n * d * d + 40 * QB * QB * d * 4, 2 * (4 * d * d + 12 * n * d)),
         name="attend",
-    )(info, x, af, as_, q, ko, vo, w, cosf, sinf, cos, sin, gain)
+    )(info, x, af, as_, q, ko, vo, w, cosf, sinf, cos, sin, gain, piece)
 
 
 def gelu(u):
     return 0.5 * u * (1.0 + jnp.tanh(GC * (u + GA * (u * u * u))))
 
 
-def mlp_kernel(xm_ref, m_ref, up_ref, dn_ref, gain_ref, x_ref, a_ref, u_ref, acc):
+def grid_points(comms, step, last):
+    for s in range(BITS):
+        at = s * last // BITS
+
+        @pl.when(step == at)
+        def _(s=s):
+            for c in comms:
+                if s > 0:
+                    c.wait(s - 1)
+                c.start(s)
+
+
+def mlp_kernel(*refs):
+    xm_ref, m_ref, up_ref, dn_ref, gain_ref = refs[:5]
     step = pl.program_id(0)
+    last = pl.num_programs(0) - 1
+    comms = []
+    if len(refs) == 9:
+        x_ref, a_ref, u_ref, acc = refs[5:]
+    else:
+        p_ref, x_ref, a_ref, u_ref, wn_ref, acc = refs[5:11]
+        comms = [Gather(p_ref, wn_ref, *refs[11:])]
+
+        @pl.when(step == 0)
+        def _():
+            greet()
+
+        grid_points(comms, step, MLP_STEPS - 1)
 
     @pl.when(step == 0)
     def _():
@@ -225,13 +496,19 @@
         x_ref[...] = x
         xh, _ = norm_stats(x)
         a_ref[...] = (xh * gain_ref[...]).astype(BF)
-
-
-def mlp(xm, m, w, gain, fc=512):
+        drain(comms)
+
+
+MLP_STEPS = 6
+
+
+def mlp(xm, m, w, gain, piece=None):
     n, d = xm.shape
     ff = w.shape[1] // 2
-    steps = ff // fc
+    steps = MLP_STEPS
+    fc = ff // steps
     full = pl.BlockSpec((n, d), lambda i: (0, 0))
+    extra = [] if piece is None else [piece]
     return pl.pallas_call(
         mlp_kernel,
         grid=(steps,),
@@ -239,28 +516,40 @@
             jax.ShapeDtypeStruct((n, d), F32),
             jax.ShapeDtypeStruct((n, d), BF),
             jax.ShapeDtypeStruct((n, ff), BF),
-        ),
+        )
+        + tuple(jax.ShapeDtypeStruct((p.shape[0] << BITS, p.shape[1]), BF) for p in extra),
         in_specs=[
             full,
             full,
             pl.BlockSpec((d, fc), lambda i: (0, i)),
             pl.BlockSpec((d, fc), lambda i: (0, i + steps)),
             pl.BlockSpec((1, d), lambda i: (0, 0)),
-        ],
-        out_specs=(full, full, pl.BlockSpec((n, fc), lambda i: (0, i))),
-        scratch_shapes=[pltpu.VMEM((n, d), F32)],
-        compiler_params=params(),
+        ]
+        + vmem(len(extra)),
+        out_specs=(full, full, pl.BlockSpec((n, fc), lambda i: (0, i))) + tuple(any_spec(len(extra))),
+        scratch_shapes=[pltpu.VMEM((n, d), F32)] + (Gather.scratch() if extra else []),
+        compiler_params=params(collective_id=3, has_side_effects=True) if extra else params(),
         cost_estimate=cost(4 * n * d * ff, 4 * d * ff + 2 * n * ff + 10 * n * d),
         name="mlp",
-    )(xm, m, w, w, gain)
-
-
-def mlp_back_kernel(
-    g_ref, xm_ref, m_ref, u_ref, up_ref, dn_ref, gain_ref,
-    gm_ref, go_ref, dup_ref, ddn_ref, dgain_ref,
-    gy, gyt, mt, dm,
-):
+    )(xm, m, w, w, gain, *extra)
+
+
+def mlp_back_kernel(*refs):
+    g_ref, xm_ref, m_ref, u_ref, up_ref, dn_ref, gain_ref = refs[:7]
     step = pl.program_id(0)
+    comms = []
+    if len(refs) == 16:
+        gm_ref, go_ref, dup_ref, ddn_ref, dgain_ref, gy, gyt, mt, dm = refs[7:]
+    else:
+        da_ref, db_ref, gm_ref, go_ref, dup_ref, ddn_ref, dgain_ref, sa_ref, sb_ref = refs[7:16]
+        gy, gyt, mt, dm = refs[16:20]
+        comms = [Reduce((da_ref, db_ref), (sa_ref, sb_ref), refs[20:])]
+
+        @pl.when(step == 0)
+        def _():
+            greet()
+
+        grid_points(comms, step, MLP_STEPS - 1)
 
     @pl.when(step == 0)
     def _():
@@ -289,12 +578,15 @@
         gm_ref[...] = gm
         go_ref[...] = gm.astype(BF)
         dgain_ref[...] = dgain
-
-
-def mlp_back(g, xm, m, u, w, gain, fc=512):
+        drain(comms)
+
+
+def mlp_back(g, xm, m, u, w, gain, extra=()):
     n, d = xm.shape
     ff = w.shape[1] // 2
-    steps = ff // fc
+    steps = MLP_STEPS
+    fc = ff // steps
+    sums = [jax.ShapeDtypeStruct((e.shape[0] >> BITS, e.shape[1]), BF) for e in extra]
     full = pl.BlockSpec((n, d), lambda i: (0, 0))
     row = pl.BlockSpec((1, d), lambda i: (0, 0))
     wide = pl.BlockSpec((d, fc), lambda i: (0, i))
@@ -307,7 +599,8 @@
             jax.ShapeDtypeStruct((d, ff), BF),
             jax.ShapeDtypeStruct((d, ff), BF),
             jax.ShapeDtypeStruct((1, d), F32),
-        ),
+        )
+        + tuple(sums),
         in_specs=[
             full,
             full,
@@ -316,28 +609,35 @@
             wide,
             pl.BlockSpec((d, fc), lambda i: (0, i + steps)),
             row,
-        ],
-        out_specs=(full, full, wide, wide, row),
+        ]
+        + any_spec(len(extra)),
+        out_specs=(full, full, wide, wide, row)
+        + tuple(pl.BlockSpec(e.shape, lambda i: (0, 0)) for e in sums),
         scratch_shapes=[
             pltpu.VMEM((n, d), BF),
             pltpu.VMEM((d, n), BF),
             pltpu.VMEM((d, n), BF),
             pltpu.VMEM((n, d), F32),
-        ],
-        compiler_params=params(),
+        ]
+        + (Reduce.scratch(extra[0].shape[0], [e.shape[1] for e in extra]) if extra else []),
+        compiler_params=params(collective_id=4, has_side_effects=True) if extra else params(),
         cost_estimate=cost(8 * n * d * ff, 8 * d * ff + 2 * n * ff + 16 * n * d),
         name="mlp_back",
-    )(g, xm, m, u, w, w, gain)
+    )(g, xm, m, u, w, w, gain, *extra)
 
 
 def attend_back_kernel(
     info, go_ref, o_ref, lse_ref, q_ref, kf_ref, vf_ref, ks_ref, vs_ref, ko_ref, vo_ref,
-    w_ref, cosf_ref, sinf_ref, cos_ref, sin_ref,
+    w_ref, cosf_ref, sinf_ref, cos_ref, sin_ref, ga_ref, gb_ref,
     dq_ref, dkf_ref, dvf_ref, dks_ref, dvs_ref, dko_ref, dvo_ref, daf_ref, das_ref, dao_ref,
-    do_s, bias, dqa, dka, dva,
+    sa_ref, sb_ref,
+    do_s, bias, dqa, dka, dva, *rest,
 ):
     n, d = go_ref.shape
     pairs = d // 128
+    greet()
+    comms = [Reduce((ga_ref, gb_ref), (sa_ref, sb_ref), rest)]
+    pump(comms, 0, 3)
     make_bias(info, bias)
     do_s[...] = mm(go_ref[...], w_ref[:, 3 * d : 4 * d]).astype(BF)
     lane_q = lax.broadcasted_iota(jnp.int32, (QB, 128), 1)
@@ -389,7 +689,11 @@
         dvo_ref[:, sl] = dva[2 * n : 3 * n, :].astype(BF)
         return carry
 
-    lax.fori_loop(0, pairs, pair, 0)
+    lax.fori_loop(0, pairs // 3, pair, 0)
+    pump(comms, 1, 3)
+    lax.fori_loop(pairs // 3, 2 * pairs // 3 + 1, pair, 0)
+    pump(comms, 2, 3)
+    lax.fori_loop(2 * pairs // 3 + 1, pairs, pair, 0)
     wk = w_ref[:, d : 2 * d]
     wv = w_ref[:, 2 * d : 3 * d]
     daf_ref[...] = (mm(dkf_ref[...], wk, NT) + mm(dvf_ref[...], wv, NT)).astype(BF)
@@ -397,58 +701,84 @@
     dao_ref[...] = (
         mm(dko_ref[...], wk, NT) + mm(dvo_ref[...], wv, NT) + mm(dq_ref[...], w_ref[:, 0:d], NT)
     )
-
-
-def attend_back(info, go, o, lse, q, kf, vf, ks, vs, ko, vo, w, cosf, sinf, cos, sin):
+    drain(comms)
+
+
+def attend_back(info, go, o, lse, q, kf, vf, ks, vs, ko, vo, w, cosf, sinf, cos, sin, extra, cid):
     n, d = go.shape
+    sums = [jax.ShapeDtypeStruct((e.shape[0] >> BITS, e.shape[1]), BF) for e in extra]
     sd = jax.ShapeDtypeStruct((n, d), BF)
     return pl.pallas_call(
         attend_back_kernel,
-        out_shape=(sd,) * 9 + (jax.ShapeDtypeStruct((n, d), F32),),
-        in_specs=[smem()] + vmem(15),
-        out_specs=tuple(vmem(10)),
+        out_shape=(sd,) * 9 + (jax.ShapeDtypeStruct((n, d), F32),) + tuple(sums),
+        in_specs=[smem()] + vmem(15) + any_spec(2),
+        out_specs=tuple(vmem(12)),
         scratch_shapes=[
             pltpu.VMEM((n, d), BF),
             pltpu.VMEM((n, 3 * n), F32),
             pltpu.VMEM((n, 128), F32),
             pltpu.VMEM((3 * n, 128), F32),
             pltpu.VMEM((3 * n, 128), F32),
-        ],
-        compiler_params=params(),
+        ]
+        + Reduce.scratch(extra[0].shape[0], [e.shape[1] for e in extra]),
+        compiler_params=params(collective_id=cid, has_side_effects=True),
         cost_estimate=cost(16 * n * d * d + 100 * QB * QB * d * 4, 2 * (4 * d * d + 24 * n * d)),
         name="attend_back",
-    )(info, go, o, lse, q, kf, vf, ks, vs, ko, vo, w, cosf, sinf, cos, sin)
+    )(info, go, o, lse, q, kf, vf, ks, vs, ko, vo, w, cosf, sinf, cos, sin, *extra)
 
 
 def weight_kernel(
     ao_ref, af_ref, as_ref, go_ref, o_ref, dq_ref, dkf_ref, dvf_ref, dks_ref, dvs_ref,
-    dko_ref, dvo_ref, dw_ref,
+    dko_ref, dvo_ref, da_ref, db_ref,
 ):
     n, d = ao_ref.shape
     aot = ao_ref[...].T
     aft = af_ref[...].T
     ast = as_ref[...].T
-    dw_ref[:, 0:d] = mm(aot, dq_ref[...]).astype(BF)
-    dw_ref[:, d : 2 * d] = (
+    da_ref[:, 0:d] = mm(aot, dq_ref[...]).astype(BF)
+    da_ref[:, d : 2 * d] = (
         mm(aot, dko_ref[...]) + mm(aft, dkf_ref[...]) + mm(ast, dks_ref[...])
     ).astype(BF)
-    dw_ref[:, 2 * d : 3 * d] = (
+    db_ref[:, 0:d] = (
         mm(aot, dvo_ref[...]) + mm(aft, dvf_ref[...]) + mm(ast, dvs_ref[...])
     ).astype(BF)
-    dw_ref[:, 3 * d : 4 * d] = mm(go_ref[...].T, o_ref[...]).astype(BF)
+    db_ref[:, d : 2 * d] = mm(go_ref[...].T, o_ref[...]).astype(BF)
 
 
 def weight_grads(ao, af, as_, go, o, dq, dkf, dvf, dks, dvs, dko, dvo):
     n, d = ao.shape
+    sd = jax.ShapeDtypeStruct((d, 2 * d), BF)
     return pl.pallas_call(
         weight_kernel,
-        out_shape=jax.ShapeDtypeStruct((d, 4 * d), BF),
+        out_shape=(sd, sd),
         in_specs=vmem(12),
-        out_specs=pl.BlockSpec(memory_space=pltpu.VMEM),
+        out_specs=tuple(vmem(2)),
         compiler_params=params(),
         cost_estimate=cost(16 * n * d * d, 2 * (4 * d * d + 12 * n * d)),
         name="weight_grads",
     )(ao, af, as_, go, o, dq, dkf, dvf, dks, dvs, dko, dvo)
+
+
+def reduce_kernel(a_ref, b_ref, sa_ref, sb_ref, *rest):
+    greet()
+    comms = [Reduce((a_ref, b_ref), (sa_ref, sb_ref), rest)]
+    for point in range(BITS):
+        pump(comms, point, BITS)
+    drain(comms)
+
+
+def reduce_call(a, b):
+    sums = tuple(jax.ShapeDtypeStruct((e.shape[0] >> BITS, e.shape[1]), BF) for e in (a, b))
+    return pl.pallas_call(
+        reduce_kernel,
+        out_shape=sums,
+        in_specs=any_spec(2),
+        out_specs=tuple(vmem(2)),
+        scratch_shapes=Reduce.scratch(a.shape[0], [a.shape[1], b.shape[1]]),
+        compiler_params=params(collective_id=6, has_side_effects=True),
+        cost_estimate=cost(1, 100 * a.size),
+        name="reduce_grads",
+    )(a, b)
 
 
 def norm_back_kernel(gm_ref, x_ref, da_ref, r1_ref, r2_ref, gain_ref, g_ref, dgain_ref):
@@ -507,34 +837,45 @@
     return q2, q3
 
 
-def gather_weights(pieces, dp):
-    count = lax.axis_size("dp")
+def turn_round(x, t):
+    got = [x] + [send(x, [(i, (i + s) % 4) for i in range(4)]) for s in (1, 2, 3)]
+    out = []
+    for j in range(4):
+        k = (t - j) % 4
+        out.append(jnp.where(k < 2, jnp.where(k == 0, got[0], got[1]), jnp.where(k == 2, got[2], got[3])))
+    return out
+
+
+def piece_of(halves, dp, t):
+    rows = halves[0][0].shape[0] >> BITS
+    parts = []
+    for i, ws in enumerate(halves):
+        at = slot_of(dp, ORDERS[i]) * rows
+        parts += [lax.dynamic_slice_in_dim(w, at, rows, 0) for w in ws]
+    all_z = turn_round(jnp.concatenate(parts, axis=1), t)
     outs = []
-    for w in pieces:
-        rows = w.shape[0] // count
-        mine = lax.dynamic_slice_in_dim(w, dp * rows, rows, 0)
-        all_z = lax.all_gather(mine, "tensor", axis=0)
-        outs.append(all_z.transpose(1, 0, 2).reshape(rows, -1))
-    return lax.all_gather(jnp.concatenate(outs, axis=1), "dp", axis=0, tiled=True)
-
-
-def reduce_weights(dw, widths):
-    zs = lax.axis_size("tensor")
-    part = lax.psum_scatter(dw, "dp", scatter_dimension=0, tiled=True)
-    rows = part.shape[0]
     at = 0
+    for p in parts:
+        outs += [z[:, at : at + p.shape[1]] for z in all_z]
+        at += p.shape[1]
+    return jnp.concatenate(outs, axis=1)
+
+
+def sum_over_z(halves, counts, t):
+    n = lax.axis_size("dp")
+    rows = halves[0].shape[0]
     cols = []
-    for w in widths:
-        cols.append(part[:, at : at + w].reshape(rows, zs, w // zs).transpose(1, 0, 2))
-        at += w
-    mine = lax.psum_scatter(jnp.concatenate(cols, axis=2), "tensor", scatter_dimension=0, tiled=False)
-    full = lax.all_gather(mine, "dp", axis=0, tiled=True).astype(F32)
-    out = []
-    at = 0
-    for w in widths:
-        out.append(full[:, at : at + w // zs])
-        at += w // zs
-    return out
+    for x, c in zip(halves, counts):
+        for b in range(BITS, n.bit_length() - 1):
+            x = x + lax.ppermute(x, "dp", [(i, i ^ (1 << b)) for i in range(n)])
+        w = x.shape[1] // c
+        cols += [x[:, j * w : (j + 1) * w].reshape(rows, 4, w // 4) for j in range(c)]
+    every = jnp.concatenate(cols, axis=2).transpose(1, 0, 2)
+    pick = lambda s: lax.dynamic_index_in_dim(every, (t + s) % 4, 0, keepdims=False)
+    total = pick(0).astype(F32)
+    for s in (1, 2, 3):
+        total = total + send(pick(s), [(i, (i + s) % 4) for i in range(4)]).astype(F32)
+    return total.astype(BF)
 
 
 def sum_all(x):
@@ -575,16 +916,21 @@
     masked = lax.dynamic_slice_in_dim(noise_mask[0], base, n, 0)
     weight = ((pos < lengths[0]) & ((t >= 2) | (masked == 1))).astype(F32)
 
-    wa = []
-    wm = []
+    pa = []
+    pm = []
     for layer in range(LAYERS):
-        wa.append(
-            gather_weights(
-                [query_weight[layer], key_weight[layer], value_weight[layer], out_weight[layer].T],
-                dp,
+        pa.append(
+            piece_of(
+                (
+                    (query_weight[layer], key_weight[layer]),
+                    (value_weight[layer], out_weight[layer].T),
+                ),
+                dp, t,
             )
         )
-        wm.append(gather_weights([up_weight[layer], down_weight[layer].T], dp))
+        pm.append(piece_of(((up_weight[layer],), (down_weight[layer].T,)), dp, t))
+    wa = [gather_call(pa[0])] + [None] * (LAYERS - 1)
+    wm = [None] * LAYERS
 
     saved = []
     x = tokens
@@ -592,37 +938,60 @@
     for layer in range(LAYERS):
         af, as_ = spread_clean(a, t)
         q, ko, vo = project_own(a, wa[layer], cos, sin)
-        o, lse, xm, m, kf, vf, ks, vs = attend(
-            info, x, af, as_, q, ko, vo, wa[layer], cosf, sinf, cos, sin, mlp_gain[layer : layer + 1]
+        o, lse, xm, m, kf, vf, ks, vs, wm[layer] = attend(
+            info, x, af, as_, q, ko, vo, wa[layer], cosf, sinf, cos, sin,
+            mlp_gain[layer : layer + 1], pm[layer], 10 + layer,
         )
-        nxt = min(layer + 1, LAYERS - 1)
-        x_next, a_next, u = mlp(xm, m, wm[layer], attn_gain[nxt : nxt + 1])
+        if layer + 1 < LAYERS:
+            x_next, a_next, u, wa[layer + 1] = mlp(
+                xm, m, wm[layer], attn_gain[layer + 1 : layer + 2], pa[layer + 1]
+            )
+        else:
+            x_next, a_next, u = mlp(xm, m, wm[layer], attn_gain[layer : layer + 1])
         saved.append((x, a, af, as_, q, kf, vf, ks, vs, ko, vo, o, lse, xm, m, u))
         x, a = x_next, a_next
     block_out = x
 
     g = cotangent.astype(F32) * weight[:, None]
     gains = [None] * (2 * LAYERS)
-    grads = [None] * LAYERS
+    att = [None] * LAYERS
+    mlps = [None] * LAYERS
+    above = ()
     for layer in reversed(range(LAYERS)):
         x, a, af, as_, q, kf, vf, ks, vs, ko, vo, o, lse, xm, m, u = saved[layer]
-        gm, go, dup, ddn, gains[LAYERS + layer] = mlp_back(
-            g, xm, m, u, wm[layer], mlp_gain[layer : layer + 1]
+        outs = mlp_back(g, xm, m, u, wm[layer], mlp_gain[layer : layer + 1], above)
+        gm, go, dup, ddn, gains[LAYERS + layer] = outs[:5]
+        if above:
+            att[layer + 1] = sum_over_z(outs[5:], (2, 2), t)
+        dq, dkf, dvf, dks, dvs, dko, dvo, daf, das, dao, su, sd = attend_back(
+            info, go, o, lse, q, kf, vf, ks, vs, ko, vo, wa[layer], cosf, sinf, cos, sin, (dup, ddn),
+            12 + layer,
         )
-        dq, dkf, dvf, dks, dvs, dko, dvo, daf, das, dao = attend_back(
-            info, go, o, lse, q, kf, vf, ks, vs, ko, vo, wa[layer], cosf, sinf, cos, sin
-        )
+        mlps[layer] = sum_over_z((su, sd), (1, 1), t)
         r1, r2 = return_clean(daf, das, t)
-        dwa = weight_grads(a, af, as_, go, o, dq, dkf, dvf, dks, dvs, dko, dvo)
-        ups = reduce_weights(jnp.concatenate([dup, ddn], axis=1), (dup.shape[1], ddn.shape[1]))
-        ats = reduce_weights(dwa, (d, d, d, d))
+        above = weight_grads(a, af, as_, go, o, dq, dkf, dvf, dks, dvs, dko, dvo)
         g, gains[layer] = norm_back_call(gm, x, dao, r1, r2, attn_gain[layer : layer + 1])
-        grads[layer] = (ats[0], ats[1], ats[2], ats[3].T, ups[0], ups[1].T)
+    att[0] = sum_over_z(reduce_call(*above), (2, 2), t)
     gain_sums = sum_all(jnp.concatenate(gains, axis=0))
-    stacked = [jnp.stack([grads[layer][i] for layer in range(LAYERS)]) for i in range(6)]
+    full = gather_many(att + mlps)
+    w = d // 4
+    f = up_weight.shape[2]
+
+    def stack(parts):
+        return jnp.stack(parts).astype(F32)
+
+    layers = range(LAYERS)
     return (
-        block_out, g, gain_sums[:LAYERS], stacked[0], stacked[1], stacked[2], stacked[3],
-        gain_sums[LAYERS:], stacked[4], stacked[5],
+        block_out,
+        g,
+        gain_sums[:LAYERS],
+        stack([full[i][:, 0:w] for i in layers]),
+        stack([full[i][:, w : 2 * w] for i in layers]),
+        stack([full[i][:, 2 * w : 3 * w] for i in layers]),
+        stack([full[i][:, 3 * w : 4 * w].T for i in layers]),
+        gain_sums[LAYERS:],
+        stack([full[LAYERS + i][:, 0:f] for i in layers]),
+        stack([full[LAYERS + i][:, f : 2 * f].T for i in layers]),
     )
 
 

time: 1040 us -> 853 us (0.82)
  waiting for transfers between devices: 431 us -> 148 us
  Pallas kernels: 274 us -> 491 us
  blocking collectives: 181 us -> 0 us
  starting transfers between devices: 34.6 us -> 130 us
  other arithmetic: 53.6 us -> 28.6 us
  between operations: 16 us -> 2.99 us
    reduce_scatter x8 -> x0, waiting for transfers between devices: 283 us -> none  [the longest x4 197 us: reduce_weights(): part = lax.psum_scatter(dw, 'dp', scatter_dimension=0, tiled=True)]
    all_gather x12 -> x0, blocking collectives: 181 us -> none  [gather_weights(): all_z = lax.all_gather(mine, 'tensor', axis=0)]
    ppermute x12 -> x36, starting transfers between devices: 12.1 us -> 107 us  [send(): return lax.ppermute(x, 'tensor', pairs)]
    pallas_call x2 -> x5, Pallas kernels: 21.8 us -> 115 us  [the longest x1 34.4 us: gather_many(): pl.pallas_call(functools.partial(end_kernel, count), out_shape=tuple((jax...]
    pallas_call x2, Pallas kernels: 50.8 us -> 117 us  [attend(): pl.pallas_call(attend_kernel, out_shape=(sd, jax.ShapeDtypeStruct((n, 128...]
    ppermute x12 -> x36, waiting for transfers between devices: 84 us -> 145 us  [send(): return lax.ppermute(x, 'tensor', pairs)]
    all_gather x8 -> x0, waiting for transfers between devices: 54.4 us -> none  [the longest x4 54.4 us: reduce_weights(): full = lax.all_gather(mine, 'dp', axis=0, tiled=True).astype(F32)]
    pallas_call x2, Pallas kernels: 110 us -> 135 us  [attend_back(): pl.pallas_call(attend_back_kernel, out_shape=(sd,) * 9 + (jax.ShapeDtypeS...]
  transfers between devices with their start and end apart: 33 -> 41, of which waited for: 19 -> 14; matrix products, arithmetic and copies ran while one was open for 7% -> 7% of each run, Pallas kernels for 17% -> 10%
where the time goes in v2:
time: 853 us; the launch traced here: 845 us
  Pallas kernels  491 us (58%)
  waiting for transfers between devices  148 us (17%)
  starting transfers between devices  130 us (15%)
  local copies, waits for them, and re-layouts  44.1 us (5%)
  other arithmetic  28.6 us (3%)
    ppermute x36, waiting for transfers between devices, send(): return lax.ppermute(x, 'tensor', pairs)  145 us
    pallas_call x2, Pallas kernels, attend_back(): pl.pallas_call(attend_back_kernel, out_shape=(sd,) * 9 + (jax.ShapeDtypeS...  135 us
    pallas_call x2, Pallas kernels, attend(): pl.pallas_call(attend_kernel, out_shape=(sd, jax.ShapeDtypeStruct((n, 128...  117 us
    ppermute x36, starting transfers between devices, send(): return lax.ppermute(x, 'tensor', pairs)  107 us
    pallas_call x2, Pallas kernels, mlp_back(): pl.pallas_call(mlp_back_kernel, grid=(steps,), out_shape=(jax.ShapeDtypeS...  54.2 us
    pallas_call x2, Pallas kernels, mlp(): pl.pallas_call(mlp_kernel, grid=(steps,), out_shape=(jax.ShapeDtypeStruct...  44.6 us
    pallas_call x1, Pallas kernels, gather_many(): pl.pallas_call(functools.partial(end_kernel, count), out_shape=tuple((jax...  34.4 us
    pallas_call x1, Pallas kernels, reduce_call(): pl.pallas_call(reduce_kernel, out_shape=sums, in_specs=any_spec(2), out_s...  30.7 us
  transfers between devices with their start and end apart: 41, of which 14 were waited for; matrix products, arithmetic and copies ran while one was open for 7% of the time, Pallas kernels for 10%

profile of v2, /device:TPU:0, one launch (start us, length us, event | category | flops | bytes accessed | tf_op | source)
XLA Modules:
  0.0 845.0 jit_solution(6706958491370107177)
XLA Ops:
  37.4 21.7 %collective-permute-done.4 = bf16[96,768]{1,0:T(8,128)(2,1)} collective-permute-done((bf16[96,768]{1,0:T(8,128)(2,1)}, bf16[96,768]{1,0:T(8,128)(2,1)}, u32[]{:S(2)}, u32[]{:S(2)}) %collective-permute-start.4) | collective-permute-done | bytes 147488 | tf_op jit(solution)/shard_map/ppermute | solution.py:823
  65.6 29.7 %gather_weights.1.w_ref = bf16[768,3072]{1,0:T(8,128)(2,1)} custom-call(bf16[96,3072]{1,0:T(8,128)(2,1)} %concatenate.46.p_ref), custom_call_target="tpu_custom_call" | custom-call | flops 1 | bytes 47185920 | tf_op jit(solution)/shard_map/gather_weights/pallas_call | solution.py:273
  120.5 15.9 %collective-permute-start.15 = (bf16[96,1536]{1,0:T(8,128)(2,1)S(1)}, bf16[96,1536]{1,0:T(8,128)(2,1)S(1)}, u32[]{:S(2)}, u32[]{:S(2)}) collective-permute-start(bf16[96,1536]{1,0:T(8,128)(2,1)S(1)} %pad_maximum_fusion.5), channel_id=1, source_target_pairs={{0,1},{1,2},{2,3},{3,0},{4,5},{5,6},{6,7},{7,4},{8,9},{9,10},{10,1... | collective-permute-start | bytes 884744 | tf_op jit(solution)/shard_map/ppermute | solution.py:823
  152.5 19.0 %collective-permute-done.2 = bf16[512,768]{1,0:T(8,128)(2,1)S(1)} collective-permute-done((bf16[512,768]{1,0:T(8,128)(2,1)}, bf16[512,768]{1,0:T(8,128)(2,1)S(1)}, u32[]{:S(2)}, u32[]{:S(2)}) %collective-permute-start.2) | collective-permute-done | bytes 786464 | tf_op jit(solution)/shard_map/ppermute | solution.py:823
  174.0 58.3 %attend.2 = (bf16[512,768]{1,0:T(8,128)(2,1)}, f32[512,128]{1,0:T(8,128)}, f32[512,768]{1,0:T(8,128)}, bf16[512,768]{1,0:T(8,128)(2,1)}, bf16[512,768]{1,0:T(8,1...) custom-call(s32[2]{0:T(128)} %pad_add_fusion.info, ...), custom_call_target="tpu_custom_call" | custom-call | flops 11072962560 | bytes 14155776 | tf_op jit(solution)/shard_map/attend/pallas_call | solution.py:434
  232.3 32.2 %mlp.2 = (f32[512,768]{1,0:T(8,128)}, bf16[512,768]{1,0:T(8,128)(2,1)}, bf16[512,3072]{1,0:T(8,128)(2,1)}, bf16[768,3072]{1,0:T(8,128)(2,1)}) custom-call(f32[512,768]{1,0:T(8,128)} %get-tuple-element.93.refs_0_.refs_1_, bf16[512,768]{1,0:T(8,128)(2,1)} %get-tuple-element.94.refs_1_.refs_2_, ...), custom_call_target="tpu_custom_call" | custom-call | flops 4831838208 | bytes 16515072 | tf_op jit(solution)/shard_map/mlp/pallas_call | solution.py:512
  266.4 12.8 %collective-permute-start.14 = (bf16[512,768]{1,0:T(8,128)(2,1)S(1)}, bf16[512,768]{1,0:T(8,128)(2,1)S(1)}, u32[]{:S(2)}, u32[]{:S(2)}) collective-permute-start(bf16[512,768]{1,0:T(8,128)(2,1)S(1)} %collective-permute-done.12), channel_id=1, source_target_pairs={{1,0},{5,4},{9,8},{13,12},{17,16},{21,20},{25,24},{29,28}} | collective-permute-start | bytes 2359304 | tf_op jit(solution)/shard_map/ppermute | solution.py:823
  285.6 36.3 %collective-permute-done.14 = bf16[512,768]{1,0:T(8,128)(2,1)S(1)} collective-permute-done((bf16[512,768]{1,0:T(8,128)(2,1)S(1)}, bf16[512,768]{1,0:T(8,128)(2,1)S(1)}, u32[]{:S(2)}, u32[]{:S(2)}) %collective-permute-start.14) | collective-permute-done | bytes 786464 | tf_op jit(solution)/shard_map/ppermute | solution.py:823
  323.1 58.9 %attend.3 = (bf16[512,768]{1,0:T(8,128)(2,1)}, f32[512,128]{1,0:T(8,128)}, f32[512,768]{1,0:T(8,128)}, bf16[512,768]{1,0:T(8,128)(2,1)}, bf16[512,768]{1,0:T(8,1...) custom-call(s32[2]{0:T(128)} %pad_add_fusion.info, ...), custom_call_target="tpu_custom_call" | custom-call | flops 11072962560 | bytes 14155776 | tf_op jit(solution)/shard_map/attend/pallas_call | solution.py:434
  382.1 12.4 %mlp.3 = (f32[512,768]{1,0:T(8,128)}, bf16[512,768]{1,0:T(8,128)(2,1)}, bf16[512,3072]{1,0:T(8,128)(2,1)}) custom-call(f32[512,768]{1,0:T(8,128)} %get-tuple-element.102.refs_0_.refs_1_, bf16[512,768]{1,0:T(8,128)(2,1)} %get-tuple-element.103.refs_1_.refs_2_, bf16[768,6144]{1,0:T(8,128)(2,1)} %get-tuple-element.104.refs_2_.refs_3_.refs_4_.refs_5_, ...), custom_call_target="tpu_custom_call" | custom-call | flops 4831838208 | bytes 16515072 | tf_op jit(solution)/shard_map/mlp/pallas_call | solution.py:512
  394.4 20.1 %mlp_back.2 = (f32[512,768]{1,0:T(8,128)}, bf16[512,768]{1,0:T(8,128)(2,1)}, bf16[768,3072]{1,0:T(8,128)(2,1)}, bf16[768,3072]{1,0:T(8,128)(2,1)}, f32[1,768]{1,0:T(1,128)}) custom-call(f32[512,768]{1,0:T(8,128)} %convert_multiply_fusion.refs_0_, f32[512,768]{1,0:T(8,128)} %get-tuple-element.102.refs_0_.refs_1_, ...), custom_call_target="tpu_custom_call" | custom-call | flops 9663676416 | bytes 28311552 | tf_op jit(solution)/shard_map/mlp_back/pallas_call | solution.py:593
  414.6 68.2 %attend_back.2 = (bf16[512,768]{1,0:T(8,128)(2,1)}, bf16[512,768]{1,0:T(8,128)(2,1)}, bf16[512,768]{1,0:T(8,128)(2,1)}, bf16[512,768]{1,0:T(8,128)(2,1)}, bf16[5...) custom-call(s32[2]{0:T(128)} %pad_add_fusion.info, ...), custom_call_target="tpu_custom_call" | custom-call | flops 24964497408 | bytes 23592960 | tf_op jit(solution)/shard_map/attend_back/pallas_call | solution.py:711
  490.1 13.7 %collective-permute-done.18 = bf16[512,768]{1,0:T(8,128)(2,1)S(1)} collective-permute-done((bf16[512,768]{1,0:T(8,128)(2,1)}, bf16[512,768]{1,0:T(8,128)(2,1)S(1)}, u32[]{:S(2)}, u32[]{:S(2)}) %collective-permute-start.18) | collective-permute-done | bytes 786464 | tf_op jit(solution)/shard_map/ppermute | solution.py:823
  504.8 10.2 %weight_grads.2 = (bf16[768,1536]{1,0:T(8,128)(2,1)}, bf16[768,1536]{1,0:T(8,128)(2,1)}) custom-call(bf16[512,768]{1,0:T(8,128)(2,1)} %get-tuple-element.97.a_ref.ao_ref, bf16[512,768]{1,0:T(8,128)(2,1)} %get-tuple-element.229.af_ref, bf16[512,768]{1,0:T(8,128)(2,1)} %get-tuple-element.228.as_ref, bf16[512,768]{1,0:T(8,128)(2,1)} %get-tuple-element.108.go_ref, ...), custom_call_target="tpu_custom_call" | custom-call | flops 4831838208 | bytes 14155776 | tf_op jit(solution)/shard_map/weight_grads/pallas_call | solution.py:751
  530.4 34.1 %mlp_back.3 = (f32[512,768]{1,0:T(8,128)}, bf16[512,768]{1,0:T(8,128)(2,1)}, bf16[768,3072]{1,0:T(8,128)(2,1)}, bf16[768,3072]{1,0:T(8,128)(2,1)}, f32[1,768]{1,...) custom-call(f32[512,768]{1,0:T(8,128)} %get-tuple-element.120.refs_0_, ...), custom_call_target="tpu_custom_call" | custom-call | flops 9663676416 | bytes 28311552 | tf_op jit(solution)/shard_map/mlp_back/pallas_call | solution.py:593
  564.5 67.0 %attend_back.3 = (bf16[512,768]{1,0:T(8,128)(2,1)}, bf16[512,768]{1,0:T(8,128)(2,1)}, bf16[512,768]{1,0:T(8,128)(2,1)}, bf16[512,768]{1,0:T(8,128)(2,1)}, bf16[5...) custom-call(s32[2]{0:T(128)} %pad_add_fusion.info, ...), custom_call_target="tpu_custom_call" | custom-call | flops 24964497408 | bytes 23592960 | tf_op jit(solution)/shard_map/attend_back/pallas_call | solution.py:711
  631.5 10.2 %weight_grads.3 = (bf16[768,1536]{1,0:T(8,128)(2,1)}, bf16[768,1536]{1,0:T(8,128)(2,1)}) custom-call(bf16[512,768]{1,0:T(8,128)(2,1)} %first_norm.1.a_ref.ao_ref, bf16[512,768]{1,0:T(8,128)(2,1)} %get-tuple-element.231.af_ref, bf16[512,768]{1,0:T(8,128)(2,1)} %get-tuple-element.230.as_ref, bf16[512,768]{1,0:T(8,128)(2,1)} %get-tuple-element.132.go_ref, ...), custom_call_target="tpu_custom_call" | custom-call | flops 4831838208 | bytes 14155776 | tf_op jit(solution)/shard_map/weight_grads/pallas_call | solution.py:751
  641.7 30.7 %reduce_grads.1 = (bf16[96,1536]{1,0:T(8,128)(2,1)}, bf16[96,1536]{1,0:T(8,128)(2,1)}) custom-call(bf16[768,1536]{1,0:T(8,128)(2,1)} %get-tuple-element.156.a_ref, bf16[768,1536]{1,0:T(8,128)(2,1)} %get-tuple-element.157.b_ref), custom_call_target="tpu_custom_call" | custom-call | flops 1 | bytes 117964800 | tf_op jit(solution)/shard_map/reduce_grads/pallas_call | solution.py:772
  678.9 19.9 %collective-permute-start.30 = (bf16[96,768]{1,0:T(8,128)(2,1)S(1)}, bf16[96,768]{1,0:T(8,128)(2,1)S(1)}, u32[]{:S(2)}, u32[]{:S(2)}) collective-permute-start(bf16[96,768]{1,0:T(8,128)(2,1)S(1)} %get-tuple-element.237), channel_id=1, source_target_pairs={{0,2},{1,3},{2,0},{3,1},{4,6},{5,7},{6,4},{7,5},{8,10},{9,11},{10,... | collective-permute-start | bytes 442376 | tf_op jit(solution)/shard_map/ppermute | solution.py:823
  708.9 8.9 %collective-permute-done.30 = bf16[96,768]{1,0:T(8,128)(2,1)S(1)} collective-permute-done((bf16[96,768]{1,0:T(8,128)(2,1)S(1)}, bf16[96,768]{1,0:T(8,128)(2,1)S(1)}, u32[]{:S(2)}, u32[]{:S(2)}) %collective-permute-start.30) | collective-permute-done | bytes 147488 | tf_op jit(solution)/shard_map/ppermute | solution.py:823
  723.7 14.5 %collective-permute-done.33 = bf16[96,768]{1,0:T(8,128)(2,1)S(1)} collective-permute-done((bf16[96,768]{1,0:T(8,128)(2,1)S(1)}, bf16[96,768]{1,0:T(8,128)(2,1)S(1)}, u32[]{:S(2)}, u32[]{:S(2)}) %collective-permute-start.33) | collective-permute-done | bytes 147488 | tf_op jit(solution)/shard_map/ppermute | solution.py:823
  740.3 9.0 %collective-permute-done.36 = bf16[96,1536]{1,0:T(8,128)(2,1)S(1)} collective-permute-done((bf16[96,1536]{1,0:T(8,128)(2,1)S(1)}, bf16[96,1536]{1,0:T(8,128)(2,1)S(1)}, u32[]{:S(2)}, u32[]{:S(2)}) %collective-permute-start.36) | collective-permute-done | bytes 294944 | tf_op jit(solution)/shard_map/ppermute | solution.py:823
  750.9 34.4 %gather_grads.1 = (bf16[768,768]{1,0:T(8,128)(2,1)}, bf16[768,768]{1,0:T(8,128)(2,1)}, bf16[768,1536]{1,0:T(8,128)(2,1)}, bf16[768,1536]{1,0:T(8,128)(2,1)}) custom-call(bf16[96,768]{1,0:T(8,128)(2,1)} %fusion.11.refs_0_, bf16[96,768]{1,0:T(8,128)(2,1)} %fusion.8.refs_1_, bf16[96,1536]{1,0:T(8,128)(2,1)} %fusion.5.refs_2_, bf16[96,1536]{1,0:T(8,128)(2,1)} %fusion.2.refs_3_), custom_call_target="tpu_custom_call" | custom-call | flops 1 | bytes 70778880 | tf_op jit(solution)/shard_map/gather_grads/pallas_call | solution.py:298
  810.5 14.5 %collective-permute-start.27 = (f32[4,768]{1,0:T(4,128)S(1)}, f32[4,768]{1,0:T(4,128)S(1)}, u32[]{:S(2)}, u32[]{:S(2)}) collective-permute-start(f32[4,768]{1,0:T(4,128)S(1)} %add.263), channel_id=1, source_target_pairs={{0,1},{1,0},{2,3},{3,2},{4,5},{5,4},{6,7},{7,6},{8,9},{9,8},{10,11... | collective-permute-start | bytes 36872 | tf_op jit(solution)/shard_map/ppermute | solution.py:888
  (299 shorter events, 189.3 us)
Async XLA Ops:
  4.5 148.0 %collective-permute-start.1 = (bf16[512,768]{1,0:T(8,128)(2,1)}, bf16[512,768]{1,0:T(8,128)(2,1)}, u32[]{:S(2)}, u32[]{:S(2)}) collective-permute-start(bf16[512,768]{1,0:T(8,128)(2,1)} %first_norm.1.a_ref.ao_ref), channel_id=1, source_target_pairs={{2,3},{3,1},{6,7},{7,5},{10,11},{11,9},{14,15},{15,13},{18,19},{19... | collective-permute-start | bytes 2359304 | tf_op jit(solution)/shard_map/ppermute | solution.py:823
  6.2 143.8 %collective-permute-start = (bf16[512,768]{1,0:T(8,128)(2,1)}, bf16[512,768]{1,0:T(8,128)(2,1)}, u32[]{:S(2)}, u32[]{:S(2)}) collective-permute-start(bf16[512,768]{1,0:T(8,128)(2,1)} %first_norm.1.a_ref.ao_ref), channel_id=1, source_target_pairs={{2,1},{6,5},{10,9},{14,13},{18,17},{22,21},{26,25},{30,29}} | collective-permute-start | bytes 2359304 | tf_op jit(solution)/shard_map/ppermute | solution.py:823
  12.1 47.0 %collective-permute-start.4 = (bf16[96,768]{1,0:T(8,128)(2,1)}, bf16[96,768]{1,0:T(8,128)(2,1)}, u32[]{:S(2)}, u32[]{:S(2)}) collective-permute-start(bf16[96,768]{1,0:T(8,128)(2,1)} %pad_maximum_fusion.6), channel_id=1, source_target_pairs={{0,2},{1,3},{2,0},{3,1},{4,6},{5,7},{6,4},{7,5},{8,10},{9,11},{10,... | collective-permute-start | bytes 442376 | tf_op jit(solution)/shard_map/ppermute | solution.py:823
  19.6 39.5 %collective-permute-start.5 = (bf16[96,768]{1,0:T(8,128)(2,1)}, bf16[96,768]{1,0:T(8,128)(2,1)}, u32[]{:S(2)}, u32[]{:S(2)}) collective-permute-start(bf16[96,768]{1,0:T(8,128)(2,1)} %pad_maximum_fusion.6), channel_id=1, source_target_pairs={{0,3},{1,0},{2,1},{3,2},{4,7},{5,4},{6,5},{7,6},{8,11},{9,8},{10,9... | collective-permute-start | bytes 442376 | tf_op jit(solution)/shard_map/ppermute | solution.py:823
  19.6 39.5 %collective-permute-start.3 = (bf16[96,768]{1,0:T(8,128)(2,1)}, bf16[96,768]{1,0:T(8,128)(2,1)}, u32[]{:S(2)}, u32[]{:S(2)}) collective-permute-start(bf16[96,768]{1,0:T(8,128)(2,1)} %pad_maximum_fusion.6), channel_id=1, source_target_pairs={{0,1},{1,2},{2,3},{3,0},{4,5},{5,6},{6,7},{7,4},{8,9},{9,10},{10,1... | collective-permute-start | bytes 442376 | tf_op jit(solution)/shard_map/ppermute | solution.py:823
  59.1 36.2 %collective-permute-start.10 = (bf16[96,768]{1,0:T(8,128)(2,1)S(1)}, bf16[96,768]{1,0:T(8,128)(2,1)S(1)}, u32[]{:S(2)}, u32[]{:S(2)}) collective-permute-start(bf16[96,768]{1,0:T(8,128)(2,1)S(1)} %pad_maximum_fusion.7), channel_id=1, source_target_pairs={{0,2},{1,3},{2,0},{3,1},{4,6},{5,7},{6,4},{7,5},{8,10},{9,11},{10,... | collective-permute-start | bytes 442376 | tf_op jit(solution)/shard_map/ppermute | solution.py:823
  59.1 37.8 %collective-permute-start.11 = (bf16[96,768]{1,0:T(8,128)(2,1)S(1)}, bf16[96,768]{1,0:T(8,128)(2,1)S(1)}, u32[]{:S(2)}, u32[]{:S(2)}) collective-permute-start(bf16[96,768]{1,0:T(8,128)(2,1)S(1)} %pad_maximum_fusion.7), channel_id=1, source_target_pairs={{0,3},{1,0},{2,1},{3,2},{4,7},{5,4},{6,5},{7,6},{8,11},{9,8},{10,9... | collective-permute-start | bytes 442376 | tf_op jit(solution)/shard_map/ppermute | solution.py:823
  59.1 40.7 %collective-permute-start.9 = (bf16[96,768]{1,0:T(8,128)(2,1)S(1)}, bf16[96,768]{1,0:T(8,128)(2,1)S(1)}, u32[]{:S(2)}, u32[]{:S(2)}) collective-permute-start(bf16[96,768]{1,0:T(8,128)(2,1)S(1)} %pad_maximum_fusion.7), channel_id=1, source_target_pairs={{0,1},{1,2},{2,3},{3,0},{4,5},{5,6},{6,7},{7,4},{8,9},{9,10},{10,1... | collective-permute-start | bytes 442376 | tf_op jit(solution)/shard_map/ppermute | solution.py:823
  112.5 29.2 %collective-permute-start.16 = (bf16[96,1536]{1,0:T(8,128)(2,1)S(1)}, bf16[96,1536]{1,0:T(8,128)(2,1)S(1)}, u32[]{:S(2)}, u32[]{:S(2)}) collective-permute-start(bf16[96,1536]{1,0:T(8,128)(2,1)S(1)} %pad_maximum_fusion.5), channel_id=1, source_target_pairs={{0,2},{1,3},{2,0},{3,1},{4,6},{5,7},{6,4},{7,5},{8,10},{9,11},{10,... | collective-permute-start | bytes 884744 | tf_op jit(solution)/shard_map/ppermute | solution.py:823
  112.5 37.4 %collective-permute-start.17 = (bf16[96,1536]{1,0:T(8,128)(2,1)S(1)}, bf16[96,1536]{1,0:T(8,128)(2,1)S(1)}, u32[]{:S(2)}, u32[]{:S(2)}) collective-permute-start(bf16[96,1536]{1,0:T(8,128)(2,1)S(1)} %pad_maximum_fusion.5), channel_id=1, source_target_pairs={{0,3},{1,0},{2,1},{3,2},{4,7},{5,4},{6,5},{7,6},{8,11},{9,8},{10,9... | collective-permute-start | bytes 884744 | tf_op jit(solution)/shard_map/ppermute | solution.py:823
  120.5 29.3 %collective-permute-start.15 = (bf16[96,1536]{1,0:T(8,128)(2,1)S(1)}, bf16[96,1536]{1,0:T(8,128)(2,1)S(1)}, u32[]{:S(2)}, u32[]{:S(2)}) collective-permute-start(bf16[96,1536]{1,0:T(8,128)(2,1)S(1)} %pad_maximum_fusion.5), channel_id=1, source_target_pairs={{0,1},{1,2},{2,3},{3,0},{4,5},{5,6},{6,7},{7,4},{8,9},{9,10},{10,1... | collective-permute-start | bytes 884744 | tf_op jit(solution)/shard_map/ppermute | solution.py:823
  266.4 55.5 %collective-permute-start.14 = (bf16[512,768]{1,0:T(8,128)(2,1)S(1)}, bf16[512,768]{1,0:T(8,128)(2,1)S(1)}, u32[]{:S(2)}, u32[]{:S(2)}) collective-permute-start(bf16[512,768]{1,0:T(8,128)(2,1)S(1)} %collective-permute-done.12), channel_id=1, source_target_pairs={{1,0},{5,4},{9,8},{13,12},{17,16},{21,20},{25,24},{29,28}} | collective-permute-start | bytes 2359304 | tf_op jit(solution)/shard_map/ppermute | solution.py:823
  486.8 37.3 %collective-permute-start.20 = (bf16[512,768]{1,0:T(8,128)(2,1)S(1)}, bf16[512,768]{1,0:T(8,128)(2,1)S(1)}, u32[]{:S(2)}, u32[]{:S(2)}) collective-permute-start(bf16[512,768]{1,0:T(8,128)(2,1)S(1)} %broadcast_select_fusion.1), channel_id=1, source_target_pairs={{1,3},{3,2},{5,7},{7,6},{9,11},{11,10},{13,15},{15,14},{17,19},{19... | collective-permute-start | bytes 2359304 | tf_op jit(solution)/shard_map/ppermute | solution.py:823
  488.0 27.1 %collective-permute-start.40 = (bf16[96,1536]{1,0:T(8,128)(2,1)S(1)}, bf16[96,1536]{1,0:T(8,128)(2,1)S(1)}, u32[]{:S(2)}, u32[]{:S(2)}) collective-permute-start(bf16[96,1536]{1,0:T(8,128)(2,1)S(1)} %get-tuple-element.217), channel_id=1, source_target_pairs={{0,3},{1,0},{2,1},{3,2},{4,7},{5,4},{6,5},{7,6},{8,11},{9,8},{10,9... | collective-permute-start | bytes 884744 | tf_op jit(solution)/shard_map/ppermute | solution.py:823
  488.1 28.3 %collective-permute-start.39 = (bf16[96,1536]{1,0:T(8,128)(2,1)S(1)}, bf16[96,1536]{1,0:T(8,128)(2,1)S(1)}, u32[]{:S(2)}, u32[]{:S(2)}) collective-permute-start(bf16[96,1536]{1,0:T(8,128)(2,1)S(1)} %get-tuple-element.218), channel_id=1, source_target_pairs={{0,2},{1,3},{2,0},{3,1},{4,6},{5,7},{6,4},{7,5},{8,10},{9,11},{10,... | collective-permute-start | bytes 884744 | tf_op jit(solution)/shard_map/ppermute | solution.py:823
  489.3 33.9 %collective-permute-start.38 = (bf16[96,1536]{1,0:T(8,128)(2,1)S(1)}, bf16[96,1536]{1,0:T(8,128)(2,1)S(1)}, u32[]{:S(2)}, u32[]{:S(2)}) collective-permute-start(bf16[96,1536]{1,0:T(8,128)(2,1)S(1)} %get-tuple-element.216), channel_id=1, source_target_pairs={{0,1},{1,2},{2,3},{3,0},{4,5},{5,6},{6,7},{7,4},{8,9},{9,10},{10,1... | collective-permute-start | bytes 884744 | tf_op jit(solution)/shard_map/ppermute | solution.py:823
  674.8 30.5 %collective-permute-start.31 = (bf16[96,768]{1,0:T(8,128)(2,1)S(1)}, bf16[96,768]{1,0:T(8,128)(2,1)S(1)}, u32[]{:S(2)}, u32[]{:S(2)}) collective-permute-start(bf16[96,768]{1,0:T(8,128)(2,1)S(1)} %get-tuple-element.236), channel_id=1, source_target_pairs={{0,3},{1,0},{2,1},{3,2},{4,7},{5,4},{6,5},{7,6},{8,11},{9,8},{10,9... | collective-permute-start | bytes 442376 | tf_op jit(solution)/shard_map/ppermute | solution.py:823
  678.9 38.9 %collective-permute-start.30 = (bf16[96,768]{1,0:T(8,128)(2,1)S(1)}, bf16[96,768]{1,0:T(8,128)(2,1)S(1)}, u32[]{:S(2)}, u32[]{:S(2)}) collective-permute-start(bf16[96,768]{1,0:T(8,128)(2,1)S(1)} %get-tuple-element.237), channel_id=1, source_target_pairs={{0,2},{1,3},{2,0},{3,1},{4,6},{5,7},{6,4},{7,5},{8,10},{9,11},{10,... | collective-permute-start | bytes 442376 | tf_op jit(solution)/shard_map/ppermute | solution.py:823
  704.0 34.2 %collective-permute-start.33 = (bf16[96,768]{1,0:T(8,128)(2,1)S(1)}, bf16[96,768]{1,0:T(8,128)(2,1)S(1)}, u32[]{:S(2)}, u32[]{:S(2)}) collective-permute-start(bf16[96,768]{1,0:T(8,128)(2,1)S(1)} %get-tuple-element.234), channel_id=1, source_target_pairs={{0,2},{1,3},{2,0},{3,1},{4,6},{5,7},{6,4},{7,5},{8,10},{9,11},{10,... | collective-permute-start | bytes 442376 | tf_op jit(solution)/shard_map/ppermute | solution.py:823
  705.3 34.3 %collective-permute-start.32 = (bf16[96,768]{1,0:T(8,128)(2,1)S(1)}, bf16[96,768]{1,0:T(8,128)(2,1)S(1)}, u32[]{:S(2)}, u32[]{:S(2)}) collective-permute-start(bf16[96,768]{1,0:T(8,128)(2,1)S(1)} %get-tuple-element.232), channel_id=1, source_target_pairs={{0,1},{1,2},{2,3},{3,0},{4,5},{5,6},{6,7},{7,4},{8,9},{9,10},{10,1... | collective-permute-start | bytes 442376 | tf_op jit(solution)/shard_map/ppermute | solution.py:823
  717.8 31.5 %collective-permute-start.36 = (bf16[96,1536]{1,0:T(8,128)(2,1)S(1)}, bf16[96,1536]{1,0:T(8,128)(2,1)S(1)}, u32[]{:S(2)}, u32[]{:S(2)}) collective-permute-start(bf16[96,1536]{1,0:T(8,128)(2,1)S(1)} %get-tuple-element.221), channel_id=1, source_target_pairs={{0,2},{1,3},{2,0},{3,1},{4,6},{5,7},{6,4},{7,5},{8,10},{9,11},{10,... | collective-permute-start | bytes 884744 | tf_op jit(solution)/shard_map/ppermute | solution.py:823
  721.0 28.4 %collective-permute-start.35 = (bf16[96,1536]{1,0:T(8,128)(2,1)S(1)}, bf16[96,1536]{1,0:T(8,128)(2,1)S(1)}, u32[]{:S(2)}, u32[]{:S(2)}) collective-permute-start(bf16[96,1536]{1,0:T(8,128)(2,1)S(1)} %get-tuple-element.219), channel_id=1, source_target_pairs={{0,1},{1,2},{2,3},{3,0},{4,5},{5,6},{6,7},{7,4},{8,9},{9,10},{10,1... | collective-permute-start | bytes 884744 | tf_op jit(solution)/shard_map/ppermute | solution.py:823
  738.2 48.9 %collective-permute-start.21 = (bf16[512,768]{1,0:T(8,128)(2,1)S(1)}, bf16[512,768]{1,0:T(8,128)(2,1)S(1)}, u32[]{:S(2)}, u32[]{:S(2)}) collective-permute-start(bf16[512,768]{1,0:T(8,128)(2,1)S(1)} %copy-done.10), channel_id=1, source_target_pairs={{0,1},{4,5},{8,9},{12,13},{16,17},{20,21},{24,25},{28,29}} | collective-permute-start | bytes 2359304 | tf_op jit(solution)/shard_map/ppermute | solution.py:823
  750.2 42.9 %collective-permute-start.23 = (bf16[512,768]{1,0:T(8,128)(2,1)S(1)}, bf16[512,768]{1,0:T(8,128)(2,1)S(1)}, u32[]{:S(2)}, u32[]{:S(2)}) collective-permute-start(bf16[512,768]{1,0:T(8,128)(2,1)S(1)} %broadcast_select_fusion), channel_id=1, source_target_pairs={{1,3},{3,2},{5,7},{7,6},{9,11},{11,10},{13,15},{15,14},{17,19},{19... | collective-permute-start | bytes 2359304 | tf_op jit(solution)/shard_map/ppermute | solution.py:823
  (62 other events, 519.2 us)

commit v3 on v1

v3 whole, which is shorter than its diff:
```python
import functools
import math

import jax
import jax.numpy as jnp
from jax import lax
from jax.experimental import pallas as pl
from jax.experimental.pallas import tpu as pltpu
from jax.sharding import PartitionSpec as P

HD = 64
BLK = 16
LMAX = 1024
LAYERS = 2
EPS = 1e-05
NEG = -1e30
SCALE = 1.0 / math.sqrt(HD)
GC = math.sqrt(2.0 / math.pi)
GA = 0.044715
F32 = jnp.float32
BF = jnp.bfloat16
QB = 256
VMEM_LIMIT = 56 << 20

NN = (((1,), (0,)), ((), ()))
NT = (((1,), (1,)), ((), ()))
TN = (((0,), (0,)), ((), ()))


def mm(a, b, dims=NN):
    return lax.dot_general(a, b, dims, preferred_element_type=F32)


def norm_stats(x):
    mean = jnp.mean(x, axis=-1, keepdims=True)
    c = x - mean
    var = jnp.mean(c * c, axis=-1, keepdims=True)
    r = lax.rsqrt(var + EPS)
    return c * r, r


def norm_back(x, gain, dy):
    xh, r = norm_stats(x)
    gy = dy * gain
    m1 = jnp.mean(gy, axis=-1, keepdims=True)
    m2 = jnp.mean(gy * xh, axis=-1, keepdims=True)
    dz = r * (gy - m1 - xh * m2)
    return dz, jnp.sum(dy * xh, axis=0, keepdims=True)


def turn(y, cos, sin):
    lane = lax.broadcasted_iota(jnp.int32, y.shape, 1) % HD
    other = jnp.where(
        lane < HD // 2, pltpu.roll(y, 128 - HD // 2, 1), pltpu.roll(y, HD // 2, 1)
    )
    return y * cos + other * sin


def vmem(n):
    return [pl.BlockSpec(memory_space=pltpu.VMEM)] * n


def smem():
    return pl.BlockSpec(memory_space=pltpu.SMEM)


def params(**kw):
    return pltpu.CompilerParams(vmem_limit_bytes=VMEM_LIMIT, **kw)


def cost(flops, nbytes, trans=0):
    return pl.CostEstimate(flops=int(flops), bytes_accessed=int(nbytes), transcendentals=int(trans))


MESH = pl.DeviceIdType.MESH
BITS = 3
ORDERS = ((0, 1, 2), (0, 2, 1))
NZ = 4


def bit_of(dp, b):
    return dp // (1 << b) % 2


def slot_of(dp, order):
    out = 0
    for b in order:
        out = out * 2 + bit_of(dp, b)
    return out


def partner(dp, b):
    return dp + (1 - 2 * bit_of(dp, b)) * (1 << b)


def greet(plane, line):
    dp = lax.axis_index("dp")
    t = lax.axis_index("tensor")
    barrier = pltpu.get_barrier_semaphore()
    if plane:
        for b in range(BITS):
            pl.semaphore_signal(barrier, inc=1, device_id=(partner(dp, b), t), device_id_type=MESH)
    if line:
        for s in range(1, NZ):
            pl.semaphore_signal(barrier, inc=1, device_id=(dp, (t + s) % NZ), device_id_type=MESH)
    pl.semaphore_wait(barrier, BITS * plane + (NZ - 1) * line)


def remote(src, dst, send, recv, dp, t):
    return pltpu.make_async_remote_copy(
        src_ref=src, dst_ref=dst, send_sem=send, recv_sem=recv, device_id=(dp, t), device_id_type=MESH
    )


def aligned(x, n=16):
    return pl.multiple_of(x, n)


def dma(n):
    return pltpu.SemaphoreType.DMA((n,))


def any_spec(n=1):
    return [pl.BlockSpec(memory_space=pl.ANY)] * n


class Job:
    plane = line = 0
    steps = BITS

    def bind(self, ins, outs, scr):
        self.at = 0
        self.i, self.o, self.s = ins, outs, scr
        self.dp = lax.axis_index("dp")
        self.t = lax.axis_index("tensor")

    def wait(self, s):
        pass

    def advance(self):
        if 0 < self.at <= self.steps:
            self.wait(self.at - 1)
        if self.at < self.steps:
            self.start(self.at)
        self.at += 1

    def complete(self):
        while self.at <= self.steps:
            self.advance()


class Gather(Job):
    plane = 1

    def __init__(self, piece):
        self.rows, n = piece.shape
        self.half = n // 2
        self.ins, self.in_specs = [piece], vmem(1)
        self.outs, self.out_specs = [jax.ShapeDtypeStruct((self.rows << BITS, n), BF)], any_spec()
        self.scratch = [dma(2 * BITS), dma(2 * BITS), dma(2)]

    def cols(self, i):
        return pl.ds(i * self.half, self.half)

    def own(self, i):
        at = slot_of(self.dp, ORDERS[i]) * self.rows
        return pltpu.make_async_copy(
            self.i[0].at[:, self.cols(i)],
            self.o[0].at[pl.ds(aligned(at), self.rows), self.cols(i)],
            self.s[2].at[i],
        )

    def copy(self, s, i):
        b = ORDERS[i][BITS - 1 - s]
        size = self.rows << s
        at = slot_of(self.dp, ORDERS[i]) // (1 << s) * size
        there = self.o[0].at[pl.ds(aligned(at), size), self.cols(i)]
        return remote(
            self.i[0].at[:, self.cols(i)] if s == 0 else there, there,
            self.s[0].at[2 * s + i], self.s[1].at[2 * s + i], partner(self.dp, b), self.t,
        )

    def start(self, s):
        for i in range(2):
            self.copy(s, i).start()
            if s == 0:
                self.own(i).start()

    def wait(self, s):
        for i in range(2):
            self.copy(s, i).wait()
            if s == 0:
                self.own(i).wait()


class Reduce(Job):
    plane = 1

    def __init__(self, a, b, part=0, parts=1):
        self.full = a.shape[0]
        widths = (a.shape[1] // parts, b.shape[1] // parts)
        self.cols = [pl.ds(part * w, w) for w in widths]
        self.ins, self.in_specs = [a, b], any_spec(2)
        self.outs = [jax.ShapeDtypeStruct((self.full >> BITS, w), BF) for w in widths]
        self.out_specs = vmem(2)
        self.scratch = [pltpu.VMEM((self.full // 2, w), BF) for w in widths]
        for w in widths:
            self.scratch += [pltpu.VMEM((self.full >> (s + 1), w), BF) for s in range(BITS)]
        self.scratch += [dma(2 * BITS), dma(2 * BITS), dma(2)]

    def got(self, s, i):
        return self.s[2 + i * BITS + s]

    def offset(self, s, i):
        at = 0
        for j in range(1, s):
            at = at + bit_of(self.dp, ORDERS[i][j]) * (self.full >> (j + 1))
        return at

    def copy(self, s, i):
        b = ORDERS[i][s]
        size = self.full >> (s + 1)
        at = (1 - bit_of(self.dp, b)) * size
        if s == 0:
            there = self.i[i].at[pl.ds(aligned(at), size), self.cols[i]]
        else:
            there = self.s[i].at[pl.ds(aligned(self.offset(s, i) + at), size), :]
        send, recv = self.s[2 + 2 * BITS], self.s[3 + 2 * BITS]
        return remote(
            there, self.got(s, i), send.at[2 * s + i], recv.at[2 * s + i], partner(self.dp, b), self.t
        )

    def own(self, i):
        size = self.full // 2
        at = bit_of(self.dp, ORDERS[i][0]) * size
        return pltpu.make_async_copy(
            self.i[i].at[pl.ds(aligned(at), size), self.cols[i]], self.s[i], self.s[4 + 2 * BITS].at[i]
        )

    def start(self, s):
        for i in range(2):
            self.copy(s, i).start()
            if s == 0:
                self.own(i).start()

    def wait(self, s):
        for i in range(2):
            self.copy(s, i).wait()
            if s == 0:
                self.own(i).wait()
            size = self.full >> (s + 1)
            base = self.offset(s + 1, i)
            keep, got, out = self.s[i], self.got(s, i), self.o[i]
            last = s == BITS - 1
            step = 48 if size % 48 == 0 else size

            def add(j, carry):
                rows = pl.ds(aligned(base + j * step), step)
                here = pl.ds(aligned(j * step), step)
                total = (keep[rows, :].astype(F32) + got[here, :].astype(F32)).astype(BF)
                if last:
                    out[here, :] = total
                else:
                    keep[rows, :] = total
                return carry

            lax.fori_loop(0, size // step, add, 0)


class Line(Job):
    line = 1
    steps = NZ - 1

    def __init__(self, parts, wide):
        self.count, self.rows, self.w = parts.shape
        self.wide = wide
        self.ins, self.in_specs = [parts], vmem(1)
        if wide:
            shape = (self.rows, self.count * NZ * self.w)
        else:
            shape = (NZ, self.count, self.rows, self.w)
        self.outs, self.out_specs = [jax.ShapeDtypeStruct(shape, BF)], any_spec()
        m = self.count * 2 * self.steps
        self.scratch = [dma(m), dma(m), dma(self.count)]

    def place(self, p, z):
        if self.wide:
            at = (p * NZ + z) * self.w
            return self.o[0].at[:, pl.ds(aligned(at, 128), self.w)]
        return self.o[0].at[z, p]

    def copy(self, s, p, way):
        z = (self.t - way * s) % NZ
        k = (s * 2 + (way > 0)) * self.count + p
        there = self.place(p, z)
        return remote(
            self.i[0].at[p] if s == 0 else there, there, self.s[0].at[k], self.s[1].at[k],
            self.dp, (self.t + way) % NZ,
        )

    def inside(self, s, way, receiver):
        t = self.t
        if receiver:
            return (t - way * (s + 1) >= 0) & (t - way * (s + 1) < NZ)
        return (t - way * s >= 0) & (t - way * s < NZ) & (t + way >= 0) & (t + way < NZ)

    def own(self, p):
        return pltpu.make_async_copy(self.i[0].at[p], self.place(p, self.t), self.s[2].at[p])

    def start(self, s):
        for way in (1, -1):

            @pl.when(self.inside(s, way, False))
            def _(way=way):
                for p in range(self.count):
                    self.copy(s, p, way).start()

        if s == 0:
            for p in range(self.count):
                self.own(p).start()

    def wait(self, s):
        for way in (1, -1):

            @pl.when(self.inside(s, way, True))
            def _(way=way):
                for p in range(self.count):
                    self.copy(s, p, way).wait_recv()

            @pl.when(self.inside(s, way, False))
            def _(way=way):
                for p in range(self.count):
                    self.copy(s, p, way).wait_send()

        if s == 0:
            for p in range(self.count):
                self.own(p).wait()


class LineSum(Job):
    line = 1
    steps = 1

    def __init__(self, parts):
        shape = parts.shape[1:]
        self.ins, self.in_specs = [parts], vmem(1)
        self.outs, self.out_specs = [jax.ShapeDtypeStruct(shape, parts.dtype)], vmem(1)
        self.scratch = [pltpu.VMEM((NZ - 1,) + shape, parts.dtype), dma(3), dma(3)]

    def copies(self):
        for s in (1, 2, 3):
            z = (self.t + s) % NZ
            yield remote(
                self.i[0].at[z], self.s[0].at[s - 1], self.s[1].at[s - 1], self.s[2].at[s - 1], self.dp, z
            )

    def start(self, s):
        for c in self.copies():
            c.start()

    def wait(self, s):
        for c in self.copies():
            c.wait()
        got = self.s[0]
        total = self.i[0][self.t].astype(F32)
        for k in range(NZ - 1):
            total = total + got[k].astype(F32)
        self.o[0][...] = total.astype(self.o[0].dtype)


class PlaneSum(Job):
    plane = 1

    def __init__(self, x):
        self.ins, self.in_specs = [x], vmem(1)
        self.outs, self.out_specs = [jax.ShapeDtypeStruct(x.shape, F32)], vmem(1)
        self.scratch = [pltpu.VMEM((BITS,) + x.shape, F32), dma(BITS), dma(BITS)]

    def copy(self, s):
        return remote(
            self.i[0] if s == 0 else self.o[0], self.s[0].at[s], self.s[1].at[s], self.s[2].at[s],
            partner(self.dp, s), self.t,
        )

    def start(self, s):
        self.copy(s).start()

    def wait(self, s):
        self.copy(s).wait()
        self.o[0][...] = (self.i[0] if s == 0 else self.o[0])[...] + self.s[0][s]


class Spread(Job):
    line = 1
    steps = 0

    def __init__(self, a):
        self.ins, self.in_specs = [a], any_spec()
        self.outs, self.out_specs = [jax.ShapeDtypeStruct(a.shape, BF)] * 2, any_spec(2)
        self.scratch = [pltpu.VMEM(a.shape, BF), pltpu.VMEM(a.shape, BF), dma(2), dma(2), dma(2)]

    def put(self, src, which, to, k):
        return remote(src, self.s[which], self.s[2].at[k], self.s[3].at[which], self.dp, to)

    def save(self, which):
        return pltpu.make_async_copy(self.s[which], self.o[which], self.s[4].at[which])

    def begin(self):
        a, t = self.i[0], self.t

        @pl.when(t == 2)
        def _():
            self.put(a, 0, 1, 0).start()
            self.put(a, 0, 3, 1).start()

        @pl.when(t % 2 == 0)
        def _():
            self.s[0][...] = jnp.zeros_like(self.s[0])

        @pl.when(t >= 2)
        def _():
            self.s[1][...] = jnp.zeros_like(self.s[1])

    def first(self):
        a, t = self.i[0], self.t

        @pl.when(t % 2 == 1)
        def _():
            self.put(a, 0, 1, 0).wait_recv()

        @pl.when(t == 1)
        def _():
            self.put(self.s[0], 1, 0, 0).start()

        @pl.when(t == 3)
        def _():
            self.put(a, 1, 1, 0).start()

        self.save(0).start()

    def second(self):
        @pl.when(self.t < 2)
        def _():
            self.put(self.i[0], 1, 1, 0).wait_recv()

        self.save(1).start()

    def end(self):
        a, t = self.i[0], self.t

        @pl.when(t >= 1)
        def _():
            self.put(a, 0, 1, 0).wait_send()

        @pl.when(t == 2)
        def _():
            self.put(a, 0, 3, 1).wait_send()

        self.save(0).wait()
        self.save(1).wait()


class Early(Job):
    line = 1
    steps = 0

    def __init__(self, shape):
        self.ins, self.in_specs = [], []
        self.outs, self.out_specs = [jax.ShapeDtypeStruct(shape, BF)], any_spec()
        self.scratch = [dma(1), dma(1)]

    def put(self, src, to):
        return remote(src, self.o[0], self.s[0].at[0], self.s[1].at[0], self.dp, to)

    def go(self, das):
        @pl.when(self.t < 2)
        def _():
            self.put(das, 2 * self.t + 1).start()

    def end(self, das):
        @pl.when(self.t < 2)
        def _():
            self.put(das, 1).wait_send()

        @pl.when(self.t % 2 == 1)
        def _():
            self.put(das, 1).wait_recv()


class Return(Job):
    line = 1
    steps = 0

    def __init__(self, daf, got):
        self.ins, self.in_specs = [daf, got], vmem(2)
        self.outs, self.out_specs = [], []
        sd = pltpu.VMEM(daf.shape, BF)
        self.scratch = [sd, sd, sd, dma(1), dma(2)]

    def put(self, src, which):
        return remote(src, self.s[which], self.s[3].at[0], self.s[4].at[which], self.dp, 2)

    def begin(self):
        daf, got = self.i

        @pl.when(self.t == 1)
        def _():
            self.s[2][...] = (daf[...].astype(F32) + got[...].astype(F32)).astype(BF)
            self.put(self.s[2], 0).start()

        @pl.when(self.t == 3)
        def _():
            self.put(daf, 1).start()

    def end(self, acc):
        daf, got = self.i

        @pl.when(self.t == 2)
        def _():
            self.put(daf, 0).wait_recv()
            self.put(daf, 1).wait_recv()
            acc[...] += self.s[0][...].astype(F32) + self.s[1][...].astype(F32)

        @pl.when(self.t == 3)
        def _():
            acc[...] += got[...].astype(F32)

        @pl.when(self.t % 2 == 1)
        def _():
            self.put(daf, 0).wait_send()


def steps_at(jobs, point, points):
    for s in range(max([j.steps for j in jobs], default=0)):
        now = [j for j in jobs if s < j.steps and s * points // j.steps == point]
        for j in now:
            if s > 0:
                j.wait(s - 1)
        for j in now:
            j.start(s)


def finish(jobs):
    for j in jobs:
        if j.steps:
            j.wait(j.steps - 1)


class In:
    def __init__(self, hbm, ref, sem):
        self.ref = ref
        self.copy = pltpu.make_async_copy(hbm, ref, sem)
        self.copy.start()

    def __call__(self):
        if self.copy is not None:
            self.copy.wait()
            self.copy = None
        return self.ref


class Out:
    def __init__(self, hbm, ref, sem):
        self.ref = ref
        self.copy = pltpu.make_async_copy(ref, hbm, sem)
        self.sent = False

    def flush(self):
        if not self.sent:
            self.copy.start()
            self.sent = True


def meet(jobs):
    greet(max(j.plane for j in jobs), max(j.line for j in jobs))


def lazily(body, ins, in_specs, outs, out_specs, scratch):
    lazy = [sp.memory_space != pltpu.SMEM for sp in in_specs]
    bufs = [pltpu.VMEM(x.shape, x.dtype) for x, z in zip(ins, lazy) if z]
    bufs += [pltpu.VMEM(x.shape, x.dtype) for x in outs]
    own = len(scratch)
    count = sum(lazy)

    def wrapped(i, o, s, jobs):
        mine, rest = s[:own], s[own:]
        vm, sin, sout = rest[:-2], rest[-2], rest[-1]
        given = []
        k = 0
        for ref, z in zip(i, lazy):
            if z:
                given.append(In(ref, vm[k], sin.at[k]))
                k += 1
            else:
                given.append(ref)
        results = [Out(ref, vm[count + k], sout.at[k]) for k, ref in enumerate(o)]
        if jobs:
            meet(jobs)
        body(given, results, mine, jobs)
        for x, z in zip(given, lazy):
            if z:
                x()
        for x in results:
            x.flush()
        for x in results:
            x.copy.wait()

    specs = [any_spec()[0] if z else sp for sp, z in zip(in_specs, lazy)]
    return wrapped, specs, any_spec(len(outs)), list(scratch) + bufs + [dma(count), dma(len(outs))]


def run(body, name, ins, in_specs, outs, out_specs, scratch, jobs, cid, flops, nbytes, grid=None):
    late = grid is None and len(ins) > 0
    if late:
        body, in_specs, out_specs, scratch = lazily(body, ins, in_specs, outs, out_specs, scratch)
    cuts = []
    for what in ("ins", "outs", "scratch"):
        own = {"ins": ins, "outs": outs, "scratch": scratch}[what]
        cuts.append([len(own)] + [len(getattr(j, what)) for j in jobs])

    def kernel(*refs):
        at = 0
        groups = []
        for cut in cuts:
            g = []
            for c in cut:
                g.append(refs[at : at + c])
                at += c
            groups.append(g)
        for k, j in enumerate(jobs):
            j.bind(groups[0][k + 1], groups[1][k + 1], groups[2][k + 1])
        if jobs and not late:
            if grid is None:
                meet(jobs)
            else:
                pl.when(pl.program_id(0) == 0)(functools.partial(meet, jobs))
        body(groups[0][0], groups[1][0], groups[2][0], jobs)

    for j in jobs:
        ins, in_specs = list(ins) + j.ins, list(in_specs) + j.in_specs
        outs, out_specs = list(outs) + j.outs, list(out_specs) + j.out_specs
        scratch = list(scratch) + j.scratch
    res = pl.pallas_call(
        kernel,
        out_shape=tuple(outs),
        in_specs=list(in_specs),
        out_specs=tuple(out_specs),
        scratch_shapes=list(scratch),
        compiler_params=params(collective_id=cid, has_side_effects=True) if jobs else params(),
        cost_estimate=cost(flops, nbytes),
        name=name,
        **({} if grid is None else {"grid": grid}),
    )(*ins)
    at = cuts[1][0]
    extra = []
    for c in cuts[1][1:]:
        extra.append(res[at : at + c])
        at += c
    return res[: cuts[1][0]], extra


def only_jobs(ins, outs, scr, jobs):
    for s in range(max(j.steps for j in jobs) + 1):
        for j in jobs:
            if s <= j.steps:
                j.advance()


def transfer(name, jobs, cid):
    return run(only_jobs, name, [], [], [], [], [], jobs, cid, 1, 1 << 24)[1]


def turned(out, tmp, cos, sin):
    for g in range(out.shape[1] // 128):
        sl = slice(g * 128, g * 128 + 128)
        out[:, sl] = turn(tmp[:, sl], cos[...], sin[...]).astype(BF)


def near_bias(info, bias):
    n = bias.shape[0]
    length = info[0]
    noisy = info[1] < 2
    base = info[1] % 2 * n
    j = lax.broadcasted_iota(jnp.int32, (n, n), 0)
    i = lax.broadcasted_iota(jnp.int32, (n, n), 1)
    bi = i // BLK
    bj = j // BLK
    low = jnp.where(noisy, bi, 0)
    seen = (bj <= bi) & (bj >= low) & (j + base < length)
    bias[...] = jnp.where(seen | (i == j), 0.0, NEG)


def far_masks(info, first, second, hot):
    n = hot.shape[1]
    length = info[0]
    noisy = info[1] < 2
    odd = info[1] % 2
    key = lax.broadcasted_iota(jnp.int32, (n, 128), 0)
    block = lax.broadcasted_iota(jnp.int32, (n, 128), 1) % HD
    real = block < n // BLK
    odd_lim = jnp.where(odd == 1, length, 0)
    lim = jnp.where(noisy, length - odd * n, 0)
    first[...] = jnp.where(real & (key >= odd_lim), NEG, 0.0).astype(BF)
    hidden = (key // BLK >= block) | (key >= lim)
    second[...] = jnp.where(real & hidden, NEG, 0.0).astype(BF)
    row = lax.broadcasted_iota(jnp.int32, (128, n), 0) % HD
    query = lax.broadcasted_iota(jnp.int32, (128, n), 1)
    hot[...] = jnp.where(query // BLK == row, 1.0, 0.0).astype(BF)


def half_of(h, shape, axis):
    at = lax.broadcasted_iota(jnp.int32, shape, axis)
    return (at < HD) if h == 0 else (at >= HD)


def attend_body(ins, outs, scr, jobs):
    info, a_in, w_in, cos_in, sin_in, cosf_in, sinf_in, x_in, gain_in = ins
    q_ref, ko_ref, vo_ref, kf_ref, vf_ref, ks_ref, vs_ref, o_ref, lse_ref, xm_ref, m_ref = [
        x.ref for x in outs
    ]
    tmp, bias, mask1, mask2, hot, acc, top, tot = scr
    spread = jobs[0]
    rest = jobs[1:]
    af_ref, as_ref = spread.s[0:2]
    n, d = x_in.ref.shape
    pairs = d // 128
    gather = rest[0]
    line = rest[1:]
    spread.begin()
    gather.advance()
    near_bias(info, bias)
    far_masks(info, mask1, mask2, hot)
    a_ref = a_in()
    w_ref = w_in()
    cos = cos_in()
    sin = sin_in()

    tmp[...] = mm(a_ref[...], w_ref[:, 0:d]) * SCALE
    turned(q_ref, tmp, cos, sin)

    def keys_of(src, kk, vv, c, s):
        av = src[...]
        tmp[...] = mm(av, w_ref[:, d : 2 * d])
        turned(kk, tmp, c, s)
        vv[...] = mm(av, w_ref[:, 2 * d : 3 * d]).astype(BF)

    keys_of(a_ref, ko_ref, vo_ref, cos, sin)
    for k in range(3):
        outs[k].flush()

    def segment(kk, vv, mask, full, first, last):
        def pair(g, carry):
            sl = pl.ds(aligned(g * 128, 128), 128)
            qt = q_ref[:, sl].T
            k2 = kk[:, sl]
            vt = vv[:, sl].T
            other_q = jnp.zeros_like(qt) if mask is None else hot[...]
            other_k = k2 if mask is None else mask[...]
            rows = pl.ds(aligned(g * 128, 128), 128)
            if not first:
                olds = top[g]
                tots = tot[g]
                before = acc[rows, :]
            tops, sums, outs = [], [], []
            chains = [(h, b) for h in range(2) for b in range(n // QB)]
            scores = []
            for h, b in chains:
                qh = jnp.where(half_of(h, qt.shape, 0), qt, other_q)
                kh = jnp.where(half_of(h, k2.shape, 1), k2, other_k)
                width = n if full else (b + 1) * QB
                scores.append(mm(kh[0:width], qh[:, b * QB : b * QB + QB]))
            for (h, b), s in zip(chains, scores):
                cs = slice(b * QB, b * QB + QB)
                width = s.shape[0]
                if mask is None:
                    s = s + bias[0:width, cs]
                mx = jnp.max(s, axis=0, keepdims=True)
                if not first:
                    old = olds[h : h + 1, cs]
                    mx = jnp.maximum(mx, old)
                    scale = jnp.exp(old - mx)
                e = jnp.exp(s - mx)
                total = jnp.sum(e, axis=0, keepdims=True)
                out = mm(vt[h * HD : h * HD + HD, 0:width], e.astype(BF))
                if not first:
                    total = total + tots[h : h + 1, cs] * scale
                    out = out + before[h * HD : h * HD + HD, cs] * scale
                if last:
                    mx = mx + jnp.log(total)
                    out = out / total
                tops.append(mx)
                sums.append(total)
                outs.append(out)
            for (h, b), mx, total, out in zip(chains, tops, sums, outs):
                cs = slice(b * QB, b * QB + QB)
                if last:
                    lse_ref[g, h : h + 1, cs] = mx
                else:
                    top[g, h : h + 1, cs] = mx
                    tot[g, h : h + 1, cs] = total
                    acc[pl.ds(aligned(g * 128 + h * HD, HD), HD), cs] = out
            if last:
                ot = jnp.concatenate(
                    [jnp.concatenate(outs[i : i + n // QB], axis=1) for i in (0, n // QB)], axis=0
                )
                o_ref[:, sl] = ot.T.astype(BF)
            return carry

        return pair

    lax.fori_loop(0, pairs, segment(ko_ref, vo_ref, None, False, True, False), 0)
    gather.advance()
    spread.first()
    keys_of(af_ref, kf_ref, vf_ref, cosf_in(), sinf_in())
    outs[3].flush()
    outs[4].flush()
    lax.fori_loop(0, pairs, segment(kf_ref, vf_ref, mask1, True, False, False), 0)
    spread.second()
    for j in line:
        j.advance()
    keys_of(as_ref, ks_ref, vs_ref, cos, sin)
    outs[5].flush()
    outs[6].flush()
    last = segment(ks_ref, vs_ref, mask2, False, False, True)
    lax.fori_loop(0, pairs // 2, last, 0)
    gather.advance()
    for j in line:
        j.advance()
    lax.fori_loop(pairs // 2, pairs, last, 0)
    for j in line:
        j.advance()
    outs[7].flush()
    outs[8].flush()
    xm = x_in()[...].astype(F32) + mm(o_ref[...], w_ref[:, 3 * d : 4 * d], NT)
    xm_ref[...] = xm
    outs[9].flush()
    xh, _ = norm_stats(xm)
    m_ref[...] = (xh * gain_in()[...]).astype(BF)
    outs[10].flush()
    spread.end()
    gather.complete()
    for j in line:
        j.complete()


def attend(info, x, a, w, cosf, sinf, cos, sin, gain, jobs, cid):
    n, d = x.shape
    sd = jax.ShapeDtypeStruct((n, d), BF)
    heads = (d // 128, 8, n)
    return run(
        attend_body, "attend",
        [info, a, w, cos, sin, cosf, sinf, x, gain], [smem()] + vmem(8),
        [sd] * 8 + [jax.ShapeDtypeStruct(heads, F32), jax.ShapeDtypeStruct((n, d), F32), sd],
        vmem(11),
        [
            pltpu.VMEM((n, d), F32),
            pltpu.VMEM((n, n), F32),
            pltpu.VMEM((n, 128), BF),
            pltpu.VMEM((n, 128), BF),
            pltpu.VMEM((128, n), BF),
            pltpu.VMEM((d, n), F32),
            pltpu.VMEM(heads, F32),
            pltpu.VMEM(heads, F32),
        ],
        [Spread(a)] + jobs, cid,
        16 * n * d * d + 40 * QB * QB * d * 4, 2 * (4 * d * d + 16 * n * d),
    )


MLP_STEPS = 6


def gelu(u):
    return 0.5 * u * (1.0 + jnp.tanh(GC * (u + GA * (u * u * u))))


def grid_steps(jobs):
    step = pl.program_id(0)
    for point in range(MLP_STEPS):
        if any(s * MLP_STEPS // j.steps == point for j in jobs for s in range(j.steps)):
            pl.when(step == point)(functools.partial(steps_at, jobs, point, MLP_STEPS))


def mlp_body(ins, outs, scr, jobs):
    xm_ref, m_ref, up_ref, dn_ref, gain = ins
    x_ref, a_ref, u_ref = outs
    (acc,) = scr
    step = pl.program_id(0)
    grid_steps(jobs)

    @pl.when(step == 0)
    def _():
        acc[...] = xm_ref[...]

    u = mm(m_ref[...], up_ref[...])
    u_ref[...] = u.astype(BF)
    acc[...] += mm(gelu(u).astype(BF), dn_ref[...], NT)

    @pl.when(step == MLP_STEPS - 1)
    def _():
        x = acc[...]
        x_ref[...] = x
        xh, _ = norm_stats(x)
        a_ref[...] = (xh * gain[...]).astype(BF)
        finish(jobs)


def mlp(xm, m, w, gain, jobs, cid):
    n, d = xm.shape
    ff = w.shape[1] // 2
    steps = MLP_STEPS
    fc = ff // steps
    full = pl.BlockSpec((n, d), lambda i: (0, 0))
    return run(
        mlp_body, "mlp",
        [xm, m, w, w, gain],
        [
            full,
            full,
            pl.BlockSpec((d, fc), lambda i: (0, i)),
            pl.BlockSpec((d, fc), lambda i: (0, i + steps)),
            pl.BlockSpec((1, d), lambda i: (0, 0)),
        ],
        [
            jax.ShapeDtypeStruct((n, d), F32),
            jax.ShapeDtypeStruct((n, d), BF),
            jax.ShapeDtypeStruct((n, ff), BF),
        ],
        [full, full, pl.BlockSpec((n, fc), lambda i: (0, i))],
        [pltpu.VMEM((n, d), F32)],
        jobs, cid,
        4 * n * d * ff, 4 * d * ff + 2 * n * ff + 10 * n * d, grid=(steps,),
    )


def mlp_back_body(ins, outs, scr, jobs):
    g_ref, xm_ref, m_ref, u_ref, up_ref, dn_ref, gain = ins
    gm_ref, go_ref, dup_ref, ddn_ref, dgain_ref = outs
    gy, gyt, mt, dm = scr
    step = pl.program_id(0)
    grid_steps(jobs)

    @pl.when(step == 0)
    def _():
        gb = g_ref[...].astype(BF)
        gy[...] = gb
        gyt[...] = gb.T
        mt[...] = m_ref[...].T
        dm[...] = jnp.zeros_like(dm)

    u = u_ref[...].astype(F32)
    dh = mm(gy[...], dn_ref[...])
    u2 = u * u
    th = jnp.tanh(GC * (u + GA * (u2 * u)))
    half = 0.5 * (1.0 + th)
    h = (u * half).astype(BF)
    slope = half + 0.5 * u * (1.0 - th * th) * (GC * (1.0 + 3.0 * GA * u2))
    du = (dh * slope).astype(BF)
    dm[...] += mm(du, up_ref[...], NT)
    dup_ref[...] = mm(mt[...], du).astype(BF)
    ddn_ref[...] = mm(gyt[...], h).astype(BF)

    @pl.when(step == MLP_STEPS - 1)
    def _():
        dz, dgain = norm_back(xm_ref[...], gain[...], dm[...])
        gm = g_ref[...] + dz
        gm_ref[...] = gm
        go_ref[...] = gm.astype(BF)
        dgain_ref[...] = dgain
        finish(jobs)


def mlp_back(g, xm, m, u, w, gain, jobs, cid):
    n, d = xm.shape
    ff = w.shape[1] // 2
    steps = MLP_STEPS
    fc = ff // steps
    full = pl.BlockSpec((n, d), lambda i: (0, 0))
    row = pl.BlockSpec((1, d), lambda i: (0, 0))
    wide = pl.BlockSpec((d, fc), lambda i: (0, i))
    return run(
        mlp_back_body, "mlp_back",
        [g, xm, m, u, w, w, gain],
        [
            full, full, full,
            pl.BlockSpec((n, fc), lambda i: (0, i)),
            wide,
            pl.BlockSpec((d, fc), lambda i: (0, i + steps)),
            row,
        ],
        [
            jax.ShapeDtypeStruct((n, d), F32),
            jax.ShapeDtypeStruct((n, d), BF),
            jax.ShapeDtypeStruct((d, ff), BF),
            jax.ShapeDtypeStruct((d, ff), BF),
            jax.ShapeDtypeStruct((1, d), F32),
        ],
        [full, full, wide, wide, row],
        [
            pltpu.VMEM((n, d), BF),
            pltpu.VMEM((d, n), BF),
            pltpu.VMEM((d, n), BF),
            pltpu.VMEM((n, d), F32),
        ],
        jobs, cid,
        8 * n * d * ff, 8 * d * ff + 2 * n * ff + 16 * n * d, grid=(steps,),
    )


def back_pair(g, segs, q_ref, do_ref, o_ref, lse_ref, hot, dqt, dka, dva):
    n = q_ref.shape[0]
    sl = pl.ds(aligned(g * 128, 128), 128)
    q2 = q_ref[:, sl]
    do2 = do_ref[:, sl]
    qt = q2.T
    dot = do2.T
    prod = dot.astype(F32) * o_ref[:, sl].T.astype(F32)
    for h in range(2):
        hs = slice(h * HD, h * HD + HD)
        low = half_of(h, qt.shape, 0)
        side = half_of(h, q2.shape, 1)
        none = jnp.zeros_like(q2)
        qth = jnp.where(low, qt, jnp.zeros_like(qt) if hot is None else hot[...])
        doth = jnp.where(low, dot, jnp.zeros_like(dot))
        qh = jnp.where(side, q2, none)
        doh = jnp.where(side, do2, none)
        dsum = jnp.sum(prod[hs], axis=0, keepdims=True)
        ls = lse_ref[g, h : h + 1, :]
        for at, (kr, vr, mask, bias, whole, base) in enumerate(segs):
            k2 = kr[:, sl]
            v2 = vr[:, sl]
            kt = k2.T
            kh = jnp.where(side, k2, none if mask is None else mask[...])
            for b in range(n // QB):
                cs = slice(b * QB, b * QB + QB)
                width = n if whole else (b + 1) * QB
                s = mm(kh[0:width], qth[:, cs])
                if bias is not None:
                    s = s + bias[0:width, cs]
                p = jnp.exp(s - ls[:, cs])
                dp = mm(v2[0:width], doth[:, cs])
                ds = (p * (dp - dsum[:, cs])).astype(BF)
                dv = mm(p.astype(BF), doh[cs])
                dk = mm(ds, qh[cs])
                dq = mm(kt[hs, 0:width], ds)
                if h == 0 and b == 0:
                    dva[base : base + width, :] = dv
                    dka[base : base + width, :] = dk
                elif h == 0 and not whole:
                    dva[base : base + width - QB, :] += dv[: width - QB]
                    dka[base : base + width - QB, :] += dk[: width - QB]
                    dva[base + width - QB : base + width, :] = dv[width - QB :]
                    dka[base + width - QB : base + width, :] = dk[width - QB :]
                else:
                    dva[base : base + width, :] += dv
                    dka[base : base + width, :] += dk
                if at == 0:
                    dqt[hs, cs] = dq
                else:
                    dqt[hs, cs] += dq
    return sl


def back_far_body(ins, outs, scr, jobs):
    (
        info, go_in, w_in, q_in, o_in, lse_in, ks_in, vs_in, cos_in, sin_in, kf_in, vf_in, cosf_in, sinf_in,
    ) = ins
    do_ref, dqp_ref, dkf_ref, dvf_ref, dks_ref, dvs_ref, daf_ref = [x.ref for x in outs]
    mask1, mask2, hot, dqt, dka, dva, das = scr
    early = jobs[0]
    rest = jobs[1:]
    n, d = go_in.ref.shape
    pairs = d // 128
    for j in rest:
        j.advance()
    far_masks(info, mask1, mask2, hot)
    go_ref = go_in()
    w_ref = w_in()
    do_ref[...] = mm(go_ref[...], w_ref[:, 3 * d : 4 * d]).astype(BF)
    outs[0].flush()
    wk = w_ref[:, d : 2 * d]
    wv = w_ref[:, 2 * d : 3 * d]

    def part(k_in, v_in, mask, whole, c_in, s_in, dk_ref, dv_ref, begin):
        q_ref, o_ref, lse_ref = q_in(), o_in(), lse_in()
        k_ref, v_ref = k_in(), v_in()
        cos, sin = c_in(), s_in()

        def pair(g, carry):
            segs = ((k_ref, v_ref, mask, None, whole, 0),)
            sl = back_pair(g, segs, q_ref, do_ref, o_ref, lse_ref, hot, dqt, dka, dva)
            if begin:
                dqp_ref[sl, :] = dqt[...]
            else:
                dqp_ref[sl, :] += dqt[...]
            dk_ref[:, sl] = turn(dka[...], cos[...], -sin[...]).astype(BF)
            dv_ref[:, sl] = dva[...].astype(BF)
            return carry

        return pair

    pair = part(ks_in, vs_in, mask2, False, cos_in, sin_in, dks_ref, dvs_ref, True)
    lax.fori_loop(0, pairs, pair, 0)
    for j in rest:
        j.advance()
    das[...] = (mm(dks_ref[...], wk, NT) + mm(dvs_ref[...], wv, NT)).astype(BF)
    early.go(das)
    outs[4].flush()
    outs[5].flush()
    pair = part(kf_in, vf_in, mask1, True, cosf_in, sinf_in, dkf_ref, dvf_ref, False)
    lax.fori_loop(0, pairs, pair, 0)
    outs[1].flush()
    outs[2].flush()
    outs[3].flush()
    daf_ref[...] = (mm(dkf_ref[...], wk, NT) + mm(dvf_ref[...], wv, NT)).astype(BF)
    outs[6].flush()
    for j in rest:
        j.advance()
    early.end(das)
    for j in rest:
        j.complete()


def back_far(info, go, o, lse, q, kf, vf, ks, vs, w, cosf, sinf, cos, sin, jobs, cid):
    n, d = go.shape
    sd = jax.ShapeDtypeStruct((n, d), BF)
    return run(
        back_far_body, "back_far",
        [info, go, w, q, o, lse, ks, vs, cos, sin, kf, vf, cosf, sinf], [smem()] + vmem(13),
        [sd, jax.ShapeDtypeStruct((d, n), F32)] + [sd] * 5, vmem(7),
        [
            pltpu.VMEM((n, 128), BF),
            pltpu.VMEM((n, 128), BF),
            pltpu.VMEM((128, n), BF),
            pltpu.VMEM((128, n), F32),
            pltpu.VMEM((n, 128), F32),
            pltpu.VMEM((n, 128), F32),
            pltpu.VMEM((n, d), BF),
        ],
        [Early((n, d))] + jobs, cid,
        10 * n * d * d + 70 * QB * QB * d * 4, 2 * (4 * d * d + 18 * n * d),
    )


def back_near_body(ins, outs, scr, jobs):
    (
        info, q_in, do_in, o_in, lse_in, ko_in, vo_in, dqp_in, cos_in, sin_in, go_in, af_in, dkf_in, dvf_in,
        as_in, dks_in, dvs_in, ao_in, w_in, x_in, gm_in, gain_in,
    ) = ins
    da_ref, db_ref, g_ref, dgain_ref = [x.ref for x in outs]
    bias, dqt, dka, dva, dq_s, dko_s, dvo_s, dao = scr
    back = jobs[0]
    rest = jobs[1:]
    n, d = do_in.ref.shape
    pairs = d // 128
    back.begin()
    for j in rest:
        j.advance()
    near_bias(info, bias)
    q_ref, do_ref, o_ref, lse_ref = q_in(), do_in(), o_in(), lse_in()
    ko_ref, vo_ref, dqp_ref, cos, sin = ko_in(), vo_in(), dqp_in(), cos_in(), sin_in()

    def pair(g, carry):
        segs = ((ko_ref, vo_ref, None, bias, False, 0),)
        sl = back_pair(g, segs, q_ref, do_ref, o_ref, lse_ref, None, dqt, dka, dva)
        dq = (dqt[...] + dqp_ref[sl, :]).T
        dq_s[:, sl] = turn(dq * SCALE, cos[...], -sin[...]).astype(BF)
        dko_s[:, sl] = turn(dka[...], cos[...], -sin[...]).astype(BF)
        dvo_s[:, sl] = dva[...].astype(BF)
        return carry

    lax.fori_loop(0, pairs, pair, 0)
    for j in rest:
        j.advance()
    db_ref[:, d : 2 * d] = mm(go_in()[...].T, o_ref[...]).astype(BF)
    aot = ao_in()[...].T
    aft = af_in()[...].T
    ast = as_in()[...].T
    db_ref[:, 0:d] = (
        mm(aot, dvo_s[...]) + mm(aft, dvf_in()[...]) + mm(ast, dvs_in()[...])
    ).astype(BF)
    outs[1].flush()
    for j in rest:
        j.advance()
    da_ref[:, 0:d] = mm(aot, dq_s[...]).astype(BF)
    da_ref[:, d : 2 * d] = (
        mm(aot, dko_s[...]) + mm(aft, dkf_in()[...]) + mm(ast, dks_in()[...])
    ).astype(BF)
    outs[0].flush()
    w_ref = w_in()
    dao[...] = (
        mm(dko_s[...], w_ref[:, d : 2 * d], NT)
        + mm(dvo_s[...], w_ref[:, 2 * d : 3 * d], NT)
        + mm(dq_s[...], w_ref[:, 0:d], NT)
    )
    for j in rest:
        j.advance()
    back.end(dao)
    dz, dgain = norm_back(x_in()[...].astype(F32), gain_in()[...], dao[...])
    g_ref[...] = gm_in()[...] + dz
    dgain_ref[...] = dgain
    for j in rest:
        j.complete()


def back_near(ins, daf, got, jobs, cid):
    n, d = ins[1].shape
    wide = jax.ShapeDtypeStruct((d, 2 * d), BF)
    return run(
        back_near_body, "back_near",
        ins, [smem()] + vmem(len(ins) - 1),
        [wide, wide, jax.ShapeDtypeStruct((n, d), F32), jax.ShapeDtypeStruct((1, d), F32)], vmem(4),
        [
            pltpu.VMEM((n, n), F32),
            pltpu.VMEM((128, n), F32),
            pltpu.VMEM((n, 128), F32),
            pltpu.VMEM((n, 128), F32),
            pltpu.VMEM((n, d), BF),
            pltpu.VMEM((n, d), BF),
            pltpu.VMEM((n, d), BF),
            pltpu.VMEM((n, d), F32),
        ],
        [Return(daf, got)] + jobs, cid,
        22 * n * d * d + 30 * QB * QB * d * 4, 2 * (8 * d * d + 24 * n * d),
    )


def first_body(ins, outs, scr, jobs):
    x_in, gain_in = ins
    a_ref = outs[0].ref
    for j in jobs:
        j.advance()
    xh, _ = norm_stats(x_in()[...].astype(F32))
    a_ref[...] = (xh * gain_in()[...]).astype(BF)
    for j in jobs:
        j.complete()


def first(x, gain, jobs, cid):
    n, d = x.shape
    return run(
        first_body, "first", [x, gain], vmem(2), [jax.ShapeDtypeStruct((n, d), BF)], vmem(1), [],
        jobs, cid, 10 * n * d, 4 * n * d,
    )


def layout_body(ins, outs, scr, jobs):
    count = len(ins) // 2
    for k in reversed(range(count)):
        ref = ins[count + k]()
        f = ref.shape[1] // 2
        outs[4].ref[k] = ref[:, 0:f].astype(F32)
        outs[5].ref[k] = ref[:, f : 2 * f].astype(F32).T
    outs[4].flush()
    outs[5].flush()
    for k in reversed(range(count)):
        v = ins[k]()[...].astype(F32)
        w = v.shape[1] // 4
        for i in range(3):
            outs[i].ref[k] = v[:, i * w : i * w + w]
        outs[3].ref[k] = v[:, 3 * w : 4 * w].T
    for i in range(4):
        outs[i].flush()


def layout(att, mlps):
    layers = len(att)
    d = att[0].shape[0]
    w = att[0].shape[1] // 4
    f = mlps[0].shape[1] // 2
    shapes = [(layers, d, w)] * 3 + [(layers, w, d), (layers, d, f), (layers, f, d)]
    return run(
        layout_body, "layout", att + mlps, vmem(2 * layers),
        [jax.ShapeDtypeStruct(x, F32) for x in shapes], vmem(6), [], [], None, 1, 6 * layers * d * (4 * w + 2 * f),
    )[0]


def wide_of(every, widths):
    outs = []
    at = 0
    for w in widths:
        outs += [every[z, :, at : at + w] for z in range(NZ)]
        at += w
    return jnp.concatenate(outs, axis=1)


def by_line(halves, counts):
    n = lax.axis_size("dp")
    cols = []
    for x, c in zip(halves, counts):
        for b in range(BITS, n.bit_length() - 1):
            x = x + lax.ppermute(x, "dp", [(i, i ^ (1 << b)) for i in range(n)])
        w = x.shape[1] // c
        for j in range(c):
            cols.append(x[:, j * w : (j + 1) * w].reshape(x.shape[0], NZ, w // NZ))
    return jnp.concatenate(cols, axis=2).transpose(1, 0, 2)


def on_device(
    tokens, lengths, noise_mask, cotangent, attn_gain, query_weight, key_weight, value_weight,
    out_weight, mlp_gain, up_weight, down_weight,
):
    n, d = tokens.shape
    dp = lax.axis_index("dp")
    t = lax.axis_index("tensor")
    info = jnp.stack([lengths[0], t]).astype(jnp.int32)
    base = (t % 2) * n
    piece_rows = d >> BITS
    at_a = slot_of(dp, ORDERS[0]) * piece_rows
    at_b = slot_of(dp, ORDERS[1]) * piece_rows

    def rows_of(w, at):
        return lax.dynamic_slice_in_dim(w, at, piece_rows, 0)

    def cols_of(w, at):
        return lax.dynamic_slice_in_dim(w, at, piece_rows, 1).T

    pa = []
    pm = []
    for l in range(LAYERS):
        pa.append(
            jnp.concatenate(
                [
                    rows_of(query_weight[l], at_a),
                    rows_of(key_weight[l], at_a),
                    rows_of(value_weight[l], at_b),
                    cols_of(out_weight[l], at_b),
                ],
                axis=1,
            )[None]
        )
        pm.append(jnp.stack([rows_of(up_weight[l], at_a), cols_of(down_weight[l], at_b)]))
    widths = (d // NZ,) * 4

    position = jnp.arange(LMAX, dtype=jnp.int32).astype(F32)
    frequency = jnp.exp(
        -math.log(10000.0) * jnp.arange(HD // 2, dtype=jnp.int32).astype(F32) / (HD // 2)
    )
    angles = position[:, None] * frequency[None, :]
    cos1 = jnp.cos(angles)
    sin1 = jnp.sin(angles)
    cos_all = jnp.concatenate([cos1] * 4, axis=1)
    sin_all = jnp.concatenate([-sin1, sin1] * 2, axis=1)
    cosf, sinf = cos_all[:n], sin_all[:n]
    cos = lax.dynamic_slice_in_dim(cos_all, base, n, 0)
    sin = lax.dynamic_slice_in_dim(sin_all, base, n, 0)

    pos = base + jnp.arange(n, dtype=jnp.int32)
    masked = lax.dynamic_slice_in_dim(noise_mask[0], base, n, 0)
    weight = ((pos < lengths[0]) & ((t >= 2) | (masked == 1))).astype(F32)

    (a,), ((every,),) = first(tokens, attn_gain[0:1], [Line(pa[0], False)], 0)
    piece = wide_of(every[:, 0], widths)
    ((wa,), (wide,)) = transfer("gather_first", [Gather(piece), Line(pm[0], True)], 1)
    was, wms, saved = [], [], []
    x = tokens
    for l in range(LAYERS):
        more = l + 1 < LAYERS
        jobs = [Gather(wide)] + ([Line(pa[l + 1], False)] if more else [])
        res, extra = attend(
            info, x, a, wa, cosf, sinf, cos, sin, mlp_gain[l : l + 1], jobs, 10 + l
        )
        q, ko, vo, kf, vf, ks, vs, o, lse, xm, m = res
        af, as_ = extra[0]
        wm = extra[1][0]
        was.append(wa)
        wms.append(wm)
        jobs = []
        if more:
            piece = wide_of(extra[2][0][:, 0], widths)
            jobs = [Gather(piece), Line(pm[l + 1], True)]
        nxt = min(l + 1, LAYERS - 1)
        (x_next, a_next, u), extra = mlp(xm, m, wm, attn_gain[nxt : nxt + 1], jobs, 20 + l)
        if more:
            wa, wide = extra[0][0], extra[1][0]
        saved.append((x, a, af, as_, q, kf, vf, ks, vs, ko, vo, o, lse, xm, m, u))
        x, a = x_next, a_next
    block_out = x

    g = cotangent.astype(F32) * weight[:, None]
    gains = [None] * (2 * LAYERS)
    att = [None] * LAYERS
    mlps = [None] * LAYERS
    att_grads = mlp_parts = None

    def joined(parts):
        return [jnp.concatenate([p[i] for p in parts], axis=1) for i in (0, 1)]

    for l in reversed(range(LAYERS)):
        x, a, af, as_, q, kf, vf, ks, vs, ko, vo, o, lse, xm, m, u = saved[l]
        above = l + 1 < LAYERS
        jobs = []
        if above:
            jobs = [Reduce(*att_grads), LineSum(by_line(joined(mlp_parts), (1, 1)))]
        res, extra = mlp_back(g, xm, m, u, wms[l], mlp_gain[l : l + 1], jobs, 30 + l)
        gm, go, dup, ddn, gains[LAYERS + l] = res
        jobs = [Reduce(dup, ddn, 0, 2)]
        if above:
            jobs += [LineSum(by_line(extra[0], (2, 2))), Gather(extra[1][0])]
        res, extra = back_far(
            info, go, o, lse, q, kf, vf, ks, vs, was[l], cosf, sinf, cos, sin, jobs, 40 + l
        )
        do, dqp, dkf, dvf, dks, dvs, daf = res
        got = extra[0][0]
        mlp_parts = [extra[1]]
        jobs = [Reduce(dup, ddn, 1, 2)]
        if above:
            mlps[l + 1] = extra[3][0]
            jobs.append(Gather(extra[2][0]))
        res, extra = back_near(
            [
                info, q, do, o, lse, ko, vo, dqp, cos, sin, go, af, dkf, dvf, as_, dks, dvs, a, was[l],
                x, gm, attn_gain[l : l + 1],
            ],
            daf, got, jobs, 50 + l,
        )
        mlp_parts.append(extra[1])
        if above:
            att[l + 1] = extra[2][0]
        att_grads = res[0:2]
        g, gains[l] = res[2:4]

    gain_rows = jnp.concatenate(gains, axis=0)
    (sums, (gain_rows,), (mlp_sum,)) = transfer(
        "reduce_last",
        [Reduce(*att_grads), PlaneSum(gain_rows), LineSum(by_line(joined(mlp_parts), (1, 1)))],
        2,
    )
    for b in range(BITS, lax.axis_size("dp").bit_length() - 1):
        size = lax.axis_size("dp")
        gain_rows = gain_rows + lax.ppermute(
            gain_rows, "dp", [(i, i ^ (1 << b)) for i in range(size)]
        )
    (part,), (gain_sums,), (mlps[0],) = transfer(
        "line_last",
        [
            LineSum(by_line(sums, (2, 2))),
            LineSum(jnp.broadcast_to(gain_rows, (NZ,) + gain_rows.shape)),
            Gather(mlp_sum),
        ],
        3,
    )
    ((att[0],),) = transfer("gather_last", [Gather(part)], 4)
    grads = layout(att, mlps)
    return (
        block_out, g, gain_sums[:LAYERS], grads[0], grads[1], grads[2], grads[3],
        gain_sums[LAYERS:], grads[4], grads[5],
    )


def solution(mesh):
    rows = P(("dp", "tensor"), None)
    cols = P(None, None, "tensor")
    mids = P(None, "tensor", None)
    return jax.shard_map(
        on_device,
        mesh=mesh,
        in_specs=(
            rows, P("dp"), P("dp", None), rows, P(), cols, cols, cols, mids, P(), cols, mids,
        ),
        out_specs=(rows, rows, P(), cols, cols, cols, mids, P(), cols, mids),
        check_vma=False,
    )
```

time: 1040 us -> 559 us (0.54)
  waiting for transfers between devices: 431 us -> 0 us
  Pallas kernels: 274 us -> 505 us
  blocking collectives: 181 us -> 0 us
  other arithmetic: 53.6 us -> 16.3 us
  starting transfers between devices: 34.6 us -> 0 us
  local copies, waits for them, and re-layouts: 45.4 us -> 28.7 us
  between operations: 16 us -> 2.56 us
    reduce_scatter x8 -> x0, waiting for transfers between devices: 283 us -> none  [the longest x4 197 us: reduce_weights(): part = lax.psum_scatter(dw, 'dp', scatter_dimension=0, tiled=True)]
    pallas_call x15 -> x16, Pallas kernels: 274 us -> 505 us  [run(): pl.pallas_call(kernel, out_shape=tuple(outs), in_specs=list(in_specs), ou...]
    all_gather x12 -> x0, blocking collectives: 181 us -> none  [gather_weights(): all_z = lax.all_gather(mine, 'tensor', axis=0)]
    ppermute x17 -> x0, waiting for transfers between devices: 92.9 us -> none  [the longest x12 84 us: send(): return lax.ppermute(x, 'tensor', pairs)]
    all_gather x8 -> x0, waiting for transfers between devices: 54.4 us -> none  [the longest x4 54.4 us: reduce_weights(): full = lax.all_gather(mine, 'dp', axis=0, tiled=True).astype(F32)]
    ppermute x17 -> x0, starting transfers between devices: 34 us -> none  [the longest x2 18.7 us: sum_all(): x = x + lax.ppermute(x, 'tensor', [(i, i ^ step) for i in range(4)])]
    concatenate x11 -> x5, other arithmetic: 27.1 us -> 3.5 us  [the longest x4 2.22 us: joined(): return [jnp.concatenate([p[i] for p in parts], axis=1) for i in (0, 1)]]
  transfers between devices with their start and end apart: 33 -> 0, of which waited for: 19 -> 0; matrix products, arithmetic and copies ran while one was open for 7% -> 0% of each run, Pallas kernels for 17% -> 0%
where the time goes in v3:
time: 559 us; the launch traced here: 553 us
  Pallas kernels  505 us (90%)
  local copies, waits for them, and re-layouts  28.7 us (5%)
  other arithmetic  16.3 us (3%)
    pallas_call x16, Pallas kernels, run(): pl.pallas_call(kernel, out_shape=tuple(outs), in_specs=list(in_specs), ou...  505 us

profile of v3, /device:TPU:0, one launch (start us, length us, event | category | flops | bytes accessed | tf_op | source)
XLA Modules:
  0.0 552.8 jit_solution(10483471054019845483)
XLA Ops:
  10.0 20.1 %first.1 = (bf16[512,768]{1,0:T(8,128)(2,1)}, bf16[4,1,96,768]{3,2,1,0:T(8,128)(2,1)}) custom-call(bf16[512,768]{1,0:T(8,128)(2,1)} %refs_19_.1, f32[1,768]{1,0:T(1,128)} %get-tuple-element.303.refs_1_.refs_21_, bf16[1,96,768]{2,1,0:T(8,128)(2,1)} %maximum_bitcast_fusion.4.refs_2_), custom_call_target="tpu_custom_call" | custom-call | flops 3932160 | bytes 1572864 | tf_op jit(solution)/shard_map/first/pallas_call | solution.py:643
  30.1 1.4 slice_bitcast_fusion.16
  32.7 1.9 fusion
  39.6 1.5 copy-done.1
  43.2 28.4 %gather_first.1 = (bf16[768,3072]{1,0:T(8,128)(2,1)}, bf16[96,6144]{1,0:T(8,128)(2,1)}) custom-call(bf16[96,3072]{1,0:T(8,128)(2,1)} %concatenate.46.refs_0_, bf16[2,96,768]{2,1,0:T(8,128)(2,1)} %pad_maximum_fusion.6.refs_1_), custom_call_target="tpu_custom_call" | custom-call | flops 1 | bytes 16777216 | tf_op jit(solution)/shard_map/gather_first/pallas_call | solution.py:643
  71.6 56.3 %attend.2 = (bf16[512,768]{1,0:T(8,128)(2,1)}, bf16[512,768]{1,0:T(8,128)(2,1)}, bf16[512,768]{1,0:T(8,128)(2,1)}, bf16[512,768]{1,0:T(8,128)(2,1)}, bf16[512,76...) custom-call(s32[2]{0:T(128)} %pad_add_fusion.refs_0_, ...), custom_call_target="tpu_custom_call" | custom-call | flops 12884901888 | bytes 17301504 | tf_op jit(solution)/shard_map/attend/pallas_call | solution.py:643
  128.0 1.4 slice_bitcast_fusion
  130.5 31.6 %mlp.2 = (f32[512,768]{1,0:T(8,128)}, bf16[512,768]{1,0:T(8,128)(2,1)}, bf16[512,3072]{1,0:T(8,128)(2,1)}, bf16[768,3072]{1,0:T(8,128)(2,1)}, bf16[96,6144]{1,0:T(8,128)(2,1)}) custom-call(f32[512,768]{1,0:T(8,128)} %get-tuple-element.115.refs_0_.refs_1_, bf16[512,768]{1,0:T(8,128)(2,1)} %get-tuple-element.116.refs_1_.refs_2_, ...), custom_call_target="tpu_custom_call" | custom-call | flops 4831838208 | bytes 16515072 | tf_op jit(solution)/shard_map/mlp/pallas_call | solution.py:643
  162.1 51.5 %attend.3 = (bf16[512,768]{1,0:T(8,128)(2,1)}, bf16[512,768]{1,0:T(8,128)(2,1)}, bf16[512,768]{1,0:T(8,128)(2,1)}, bf16[512,768]{1,0:T(8,128)(2,1)}, bf16[512,76...) custom-call(s32[2]{0:T(128)} %pad_add_fusion.refs_0_, ...), custom_call_target="tpu_custom_call" | custom-call | flops 12884901888 | bytes 17301504 | tf_op jit(solution)/shard_map/attend/pallas_call | solution.py:643
  213.7 12.3 %mlp.3 = (f32[512,768]{1,0:T(8,128)}, bf16[512,768]{1,0:T(8,128)(2,1)}, bf16[512,3072]{1,0:T(8,128)(2,1)}) custom-call(f32[512,768]{1,0:T(8,128)} %get-tuple-element.123.refs_0_.refs_1_, bf16[512,768]{1,0:T(8,128)(2,1)} %get-tuple-element.124.refs_1_.refs_2_, bf16[768,6144]{1,0:T(8,128)(2,1)} %get-tuple-element.125.refs_2_.refs_3_.refs_4_.refs_5_, ...), custom_call_target="tpu_custom_call" | custom-call | flops 4831838208 | bytes 16515072 | tf_op jit(solution)/shard_map/mlp/pallas_call | solution.py:643
  226.0 20.1 %mlp_back.2 = (f32[512,768]{1,0:T(8,128)}, bf16[512,768]{1,0:T(8,128)(2,1)}, bf16[768,3072]{1,0:T(8,128)(2,1)}, bf16[768,3072]{1,0:T(8,128)(2,1)}, f32[1,768]{1,0:T(1,128)}) custom-call(f32[512,768]{1,0:T(8,128)} %convert_multiply_fusion.refs_0_, f32[512,768]{1,0:T(8,128)} %get-tuple-element.123.refs_0_.refs_1_, ...), custom_call_target="tpu_custom_call" | custom-call | flops 9663676416 | bytes 28311552 | tf_op jit(solution)/shard_map/mlp_back/pallas_call | solution.py:643
  246.1 37.4 %back_far.2 = (bf16[512,768]{1,0:T(8,128)(2,1)}, f32[768,512]{1,0:T(8,128)}, bf16[512,768]{1,0:T(8,128)(2,1)}, bf16[512,768]{1,0:T(8,128)(2,1)}, bf16[512,768]{1...) custom-call(s32[2]{0:T(128)} %pad_add_fusion.refs_0_, ...), custom_call_target="tpu_custom_call" | custom-call | flops 17112760320 | bytes 18874368 | tf_op jit(solution)/shard_map/back_far/pallas_call | solution.py:643
  283.5 39.5 %back_near.2 = (bf16[768,1536]{1,0:T(8,128)(2,1)}, bf16[768,1536]{1,0:T(8,128)(2,1)}, f32[512,768]{1,0:T(8,128)}, f32[1,768]{1,0:T(1,128)}, bf16[96,1536]{1,0:T(8,128)(2,1)}, /*index=5*/bf16[96,1536]{1,0:T(8,128)(2,1)}) custom-call(s32[2]{0:T(128)} %pad_add_fusion.refs_0_, bf16[512,768]{1,0:T(8,128)(2,1)} %get-tuple-element.128.refs_3_.refs_1_, ...), custom_call_target="tpu_custom_call" | custom-call | flops 12683575296 | bytes 28311552 | tf_op jit(solution)/shard_map/back_near/pallas_call | solution.py:643
  325.4 35.6 %mlp_back.3 = (f32[512,768]{1,0:T(8,128)}, bf16[512,768]{1,0:T(8,128)(2,1)}, bf16[768,3072]{1,0:T(8,128)(2,1)}, bf16[768,3072]{1,0:T(8,128)(2,1)}, f32[1,768]{1,...) custom-call(f32[512,768]{1,0:T(8,128)} %get-tuple-element.152.refs_0_, ...), custom_call_target="tpu_custom_call" | custom-call | flops 9663676416 | bytes 28311552 | tf_op jit(solution)/shard_map/mlp_back/pallas_call | solution.py:643
  364.1 40.4 %back_far.3 = (bf16[512,768]{1,0:T(8,128)(2,1)}, f32[768,512]{1,0:T(8,128)}, bf16[512,768]{1,0:T(8,128)(2,1)}, bf16[512,768]{1,0:T(8,128)(2,1)}, bf16[512,768]{1...) custom-call(s32[2]{0:T(128)} %pad_add_fusion.refs_0_, ...), custom_call_target="tpu_custom_call" | custom-call | flops 17112760320 | bytes 18874368 | tf_op jit(solution)/shard_map/back_far/pallas_call | solution.py:643
  404.6 44.7 %back_near.3 = (bf16[768,1536]{1,0:T(8,128)(2,1)}, bf16[768,1536]{1,0:T(8,128)(2,1)}, f32[512,768]{1,0:T(8,128)}, f32[1,768]{1,0:T(1,128)}, bf16[96,1536]{1,0:T(...) custom-call(s32[2]{0:T(128)} %pad_add_fusion.refs_0_, ...), custom_call_target="tpu_custom_call" | custom-call | flops 12683575296 | bytes 28311552 | tf_op jit(solution)/shard_map/back_near/pallas_call | solution.py:643
  452.9 32.3 %reduce_last.1 = (bf16[96,1536]{1,0:T(8,128)(2,1)}, bf16[96,1536]{1,0:T(8,128)(2,1)}, f32[4,768]{1,0:T(4,128)}, bf16[96,1536]{1,0:T(8,128)(2,1)}) custom-call(bf16[768,1536]{1,0:T(8,128)(2,1)} %get-tuple-element.187.refs_0_, bf16[768,1536]{1,0:T(8,128)(2,1)} %get-tuple-element.188.refs_1_, f32[4,768]{1,0:T(4,128)} %pad_maximum_fusion.8.refs_2_, ...), custom_call_target="tpu_custom_call" | custom-call | flops 1 | bytes 16777216 | tf_op jit(solution)/shard_map/reduce_last/pallas_call | solution.py:643
  489.0 32.0 %line_last.1 = (bf16[96,768]{1,0:T(8,128)(2,1)}, f32[4,768]{1,0:T(4,128)}, bf16[768,1536]{1,0:T(8,128)(2,1)}) custom-call(bf16[4,96,768]{2,1,0:T(8,128)(2,1)} %maximum_bitcast_fusion.3.refs_0_, f32[4,4,768]{2,1,0:T(4,128)} %broadcast_in_dim.14.refs_1_, bf16[96,1536]{1,0:T(8,128)(2,1)} %get-tuple-element.200.refs_2_), custom_call_target="tpu_custom_call" | custom-call | flops 1 | bytes 16777216 | tf_op jit(solution)/shard_map/line_last/pallas_call | solution.py:643
  521.0 1.4 fusion.15
  522.4 13.2 %gather_last.1.refs_0_ = bf16[768,768]{1,0:T(8,128)(2,1)} custom-call(bf16[96,768]{1,0:T(8,128)(2,1)} %get-tuple-element.202.refs_0_), custom_call_target="tpu_custom_call" | custom-call | flops 1 | bytes 16777216 | tf_op jit(solution)/shard_map/gather_last/pallas_call | solution.py:643
  535.6 9.6 %layout.1 = (f32[2,768,192]{2,1,0:T(8,128)}, f32[2,768,192]{2,1,0:T(8,128)}, f32[2,768,192]{2,1,0:T(8,128)}, f32[2,192,768]{2,1,0:T(8,128)}, f32[2,768,768]{2,1,0:T(8,128)}, /*index=5*/f32[2,768,768]{2,1,0:T(8,128)}) custom-call(bf16[768,768]{1,0:T(8,128)(2,1)} %gather_last.1.refs_0_, bf16[768,768]{1,0:T(8,128)(2,1)} %get-tuple-element.203.refs_1_, ...), custom_call_target="tpu_custom_call" | custom-call | flops 1 | bytes 21233664 | tf_op jit(solution)/shard_map/layout/pallas_call | solution.py:643
  545.3 3.0 copy.83
  548.3 1.5 copy.84
  549.7 1.5 copy.85
  (115 shorter events, 31.5 us)
Async XLA Ops:
  0.6 6.3 %copy-start.6 = (bf16[2,768,192]{1,2,0:T(8,128)(2,1)S(1)}, bf16[2,768,192]{1,2,0:T(8,128)(2,1)}, u32[]{:S(2)}) copy-start(bf16[2,768,192]{1,2,0:T(8,128)(2,1)} %param.18) | copy-start | bytes 1769476
  6.6 1.1 copy-start.7
  7.0 1.1 copy-start.8
  35.5 1.7 copy-start.5
  37.2 2.2 copy-start
  39.4 1.7 copy-start.1
  283.5 39.5 %copy-start.15 = (bf16[96,1536]{1,0:T(8,128)(2,1)S(1)}, bf16[96,1536]{1,0:T(8,128)(2,1)}, u32[]{:S(2)}) copy-start(bf16[96,1536]{1,0:T(8,128)(2,1)} %get-tuple-element.156) | copy-start | bytes 884740
  323.0 1.1 copy-start.14
  323.0 1.1 copy-start.16
  361.0 1.5 copy-start.9
  404.5 44.7 %copy-start.18 = (f32[1,768]{1,0:T(1,128)S(1)}, f32[1,768]{1,0:T(1,128)}, u32[]{:S(2)}) copy-start(f32[1,768]{1,0:T(1,128)} %get-tuple-element.192) | copy-start | bytes 9220
  404.6 44.7 %copy-start.19 = (f32[1,768]{1,0:T(1,128)S(1)}, f32[1,768]{1,0:T(1,128)}, u32[]{:S(2)}) copy-start(f32[1,768]{1,0:T(1,128)} %get-tuple-element.190) | copy-start | bytes 9220
  404.6 44.7 %copy-start.20 = (f32[1,768]{1,0:T(1,128)S(1)}, f32[1,768]{1,0:T(1,128)}, u32[]{:S(2)}) copy-start(f32[1,768]{1,0:T(1,128)} %get-tuple-element.191) | copy-start | bytes 9220
  404.6 46.0 %copy-start.12 = (bf16[96,1536]{1,0:T(8,128)(2,1)S(1)}, bf16[96,1536]{1,0:T(8,128)(2,1)}, u32[]{:S(2)}) copy-start(bf16[96,1536]{1,0:T(8,128)(2,1)} %get-tuple-element.193) | copy-start | bytes 884740
  450.6 1.1 copy-start.11
  450.6 1.1 copy-start.13
  485.2 1.3 copy-start.17
  485.2 2.2 copy-start.10
  545.3 3.0 copy-start.4
  548.3 1.5 copy-start.3
  549.7 1.5 copy-start.2

commit v4 on v3

--- a/solution.py
+++ b/solution.py
@@ -3,6 +3,7 @@
 
 import jax
 import jax.numpy as jnp
+import numpy as np
 from jax import lax
 from jax.experimental import pallas as pl
 from jax.experimental.pallas import tpu as pltpu
@@ -138,15 +139,17 @@
         pass
 
     def advance(self):
-        if 0 < self.at <= self.steps:
-            self.wait(self.at - 1)
         if self.at < self.steps:
+            if self.at > 0:
+                self.wait(self.at - 1)
             self.start(self.at)
-        self.at += 1
+            self.at += 1
 
     def complete(self):
-        while self.at <= self.steps:
+        while self.at < self.steps:
             self.advance()
+        if self.steps:
+            self.wait(self.steps - 1)
 
 
 class Gather(Job):
@@ -271,10 +274,11 @@
     line = 1
     steps = NZ - 1
 
-    def __init__(self, parts, wide):
-        self.count, self.rows, self.w = parts.shape
+    def __init__(self, parts, wide, shape=None):
+        self.count, self.rows, self.w = shape if parts is None else parts.shape
         self.wide = wide
-        self.ins, self.in_specs = [parts], vmem(1)
+        self.src = None
+        self.ins, self.in_specs = ([], []) if parts is None else ([parts], vmem(1))
         if wide:
             shape = (self.rows, self.count * NZ * self.w)
         else:
@@ -294,9 +298,12 @@
         k = (s * 2 + (way > 0)) * self.count + p
         there = self.place(p, z)
         return remote(
-            self.i[0].at[p] if s == 0 else there, there, self.s[0].at[k], self.s[1].at[k],
+            self.source().at[p] if s == 0 else there, there, self.s[0].at[k], self.s[1].at[k],
             self.dp, (self.t + way) % NZ,
         )
+
+    def source(self):
+        return self.i[0] if self.src is None else self.src
 
     def inside(self, s, way, receiver):
         t = self.t
@@ -305,7 +312,7 @@
         return (t - way * s >= 0) & (t - way * s < NZ) & (t + way >= 0) & (t + way < NZ)
 
     def own(self, p):
-        return pltpu.make_async_copy(self.i[0].at[p], self.place(p, self.t), self.s[2].at[p])
+        return pltpu.make_async_copy(self.source().at[p], self.place(p, self.t), self.s[2].at[p])
 
     def start(self, s):
         for way in (1, -1):
@@ -576,8 +583,14 @@
 
 
 def lazily(body, ins, in_specs, outs, out_specs, scratch):
-    lazy = [sp.memory_space != pltpu.SMEM for sp in in_specs]
-    bufs = [pltpu.VMEM(x.shape, x.dtype) for x, z in zip(ins, lazy) if z]
+    lazy = [sp.memory_space == pltpu.VMEM for sp in in_specs]
+    picks = [x[1] if isinstance(x, tuple) else None for x in ins]
+    ins = [x[0] if isinstance(x, tuple) else x for x in ins]
+    bufs = [
+        pltpu.VMEM(x.shape if p is None else x.shape[1:], x.dtype)
+        for x, z, p in zip(ins, lazy, picks)
+        if z
+    ]
     bufs += [pltpu.VMEM(x.shape, x.dtype) for x in outs]
     own = len(scratch)
     count = sum(lazy)
@@ -587,8 +600,10 @@
         vm, sin, sout = rest[:-2], rest[-2], rest[-1]
         given = []
         k = 0
-        for ref, z in zip(i, lazy):
+        for ref, z, p in zip(i, lazy, picks):
             if z:
+                if p is not None:
+                    ref = ref.at[lax.axis_index("tensor") % 2 if p else 0]
                 given.append(In(ref, vm[k], sin.at[k]))
                 k += 1
             else:
@@ -606,13 +621,13 @@
             x.copy.wait()
 
     specs = [any_spec()[0] if z else sp for sp, z in zip(in_specs, lazy)]
-    return wrapped, specs, any_spec(len(outs)), list(scratch) + bufs + [dma(count), dma(len(outs))]
+    return wrapped, ins, specs, any_spec(len(outs)), list(scratch) + bufs + [dma(count), dma(len(outs))]
 
 
 def run(body, name, ins, in_specs, outs, out_specs, scratch, jobs, cid, flops, nbytes, grid=None):
     late = grid is None and len(ins) > 0
     if late:
-        body, in_specs, out_specs, scratch = lazily(body, ins, in_specs, outs, out_specs, scratch)
+        body, ins, in_specs, out_specs, scratch = lazily(body, ins, in_specs, outs, out_specs, scratch)
     cuts = []
     for what in ("ins", "outs", "scratch"):
         own = {"ins": ins, "outs": outs, "scratch": scratch}[what]
@@ -660,10 +675,11 @@
 
 
 def only_jobs(ins, outs, scr, jobs):
-    for s in range(max(j.steps for j in jobs) + 1):
+    for s in range(max(j.steps for j in jobs)):
         for j in jobs:
-            if s <= j.steps:
-                j.advance()
+            j.advance()
+    for j in jobs:
+        j.complete()
 
 
 def transfer(name, jobs, cid):
@@ -679,8 +695,9 @@
 def near_bias(info, bias):
     n = bias.shape[0]
     length = info[0]
-    noisy = info[1] < 2
-    base = info[1] % 2 * n
+    t = lax.axis_index("tensor")
+    noisy = t < 2
+    base = t % 2 * n
     j = lax.broadcasted_iota(jnp.int32, (n, n), 0)
     i = lax.broadcasted_iota(jnp.int32, (n, n), 1)
     bi = i // BLK
@@ -693,8 +710,9 @@
 def far_masks(info, first, second, hot):
     n = hot.shape[1]
     length = info[0]
-    noisy = info[1] < 2
-    odd = info[1] % 2
+    t = lax.axis_index("tensor")
+    noisy = t < 2
+    odd = t % 2
     key = lax.broadcasted_iota(jnp.int32, (n, 128), 0)
     block = lax.broadcasted_iota(jnp.int32, (n, 128), 1) % HD
     real = block < n // BLK
@@ -713,7 +731,7 @@
     return (at < HD) if h == 0 else (at >= HD)
 
 
-def attend_body(ins, outs, scr, jobs):
+def attend_body(row, ins, outs, scr, jobs):
     info, a_in, w_in, cos_in, sin_in, cosf_in, sinf_in, x_in, gain_in = ins
     q_ref, ko_ref, vo_ref, kf_ref, vf_ref, ks_ref, vs_ref, o_ref, lse_ref, xm_ref, m_ref = [
         x.ref for x in outs
@@ -835,7 +853,7 @@
     xm_ref[...] = xm
     outs[9].flush()
     xh, _ = norm_stats(xm)
-    m_ref[...] = (xh * gain_in()[...]).astype(BF)
+    m_ref[...] = (xh * gain_in()[row : row + 1]).astype(BF)
     outs[10].flush()
     spread.end()
     gather.complete()
@@ -843,12 +861,12 @@
         j.complete()
 
 
-def attend(info, x, a, w, cosf, sinf, cos, sin, gain, jobs, cid):
+def attend(info, x, a, w, cosf, sinf, cos, sin, gain, row, jobs, cid):
     n, d = x.shape
     sd = jax.ShapeDtypeStruct((n, d), BF)
     heads = (d // 128, 8, n)
     return run(
-        attend_body, "attend",
+        functools.partial(attend_body, row), "attend",
         [info, a, w, cos, sin, cosf, sinf, x, gain], [smem()] + vmem(8),
         [sd] * 8 + [jax.ShapeDtypeStruct(heads, F32), jax.ShapeDtypeStruct((n, d), F32), sd],
         vmem(11),
@@ -868,10 +886,12 @@
 
 
 MLP_STEPS = 6
+SPLIT = 2
+SPLITB = 2
 
 
 def gelu(u):
-    return 0.5 * u * (1.0 + jnp.tanh(GC * (u + GA * (u * u * u))))
+    return u * (0.5 * jnp.tanh(u * (GC + (GC * GA) * (u * u))) + 0.5)
 
 
 def grid_steps(jobs):
@@ -881,7 +901,7 @@
             pl.when(step == point)(functools.partial(steps_at, jobs, point, MLP_STEPS))
 
 
-def mlp_body(ins, outs, scr, jobs):
+def mlp_body(row, ins, outs, scr, jobs):
     xm_ref, m_ref, up_ref, dn_ref, gain = ins
     x_ref, a_ref, u_ref = outs
     (acc,) = scr
@@ -892,34 +912,39 @@
     def _():
         acc[...] = xm_ref[...]
 
-    u = mm(m_ref[...], up_ref[...])
-    u_ref[...] = u.astype(BF)
-    acc[...] += mm(gelu(u).astype(BF), dn_ref[...], NT)
-
-    @pl.when(step == MLP_STEPS - 1)
+    up = up_ref[...]
+    dn = dn_ref[...]
+    cut = m_ref.shape[0] // SPLIT
+    us = [mm(m_ref[i * cut : (i + 1) * cut], up) for i in range(SPLIT)]
+    for i, u in enumerate(us):
+        rows = slice(i * cut, (i + 1) * cut)
+        u_ref[rows] = u.astype(BF)
+        acc[rows] += mm(gelu(u).astype(BF), dn, NT)
+
+    @pl.when(step == pl.num_programs(0) - 1)
     def _():
         x = acc[...]
         x_ref[...] = x
         xh, _ = norm_stats(x)
-        a_ref[...] = (xh * gain[...]).astype(BF)
+        a_ref[...] = (xh * gain[row : row + 1]).astype(BF)
         finish(jobs)
 
 
-def mlp(xm, m, w, gain, jobs, cid):
+def mlp(xm, m, w, gain, row, jobs, cid):
     n, d = xm.shape
     ff = w.shape[1] // 2
-    steps = MLP_STEPS
+    steps = MLP_STEPS if jobs else MLP_STEPS // 2
     fc = ff // steps
     full = pl.BlockSpec((n, d), lambda i: (0, 0))
     return run(
-        mlp_body, "mlp",
+        functools.partial(mlp_body, row), "mlp",
         [xm, m, w, w, gain],
         [
             full,
             full,
             pl.BlockSpec((d, fc), lambda i: (0, i)),
             pl.BlockSpec((d, fc), lambda i: (0, i + steps)),
-            pl.BlockSpec((1, d), lambda i: (0, 0)),
+            pl.BlockSpec(gain.shape, lambda i: (0, 0)),
         ],
         [
             jax.ShapeDtypeStruct((n, d), F32),
@@ -933,12 +958,26 @@
     )
 
 
-def mlp_back_body(ins, outs, scr, jobs):
-    g_ref, xm_ref, m_ref, u_ref, up_ref, dn_ref, gain = ins
+def mlp_back_body(at, ins, outs, scr, jobs):
+    g_ref, xm_ref, m_ref, u_ref, up_ref, dn_ref, gain = ins[:7]
     gm_ref, go_ref, dup_ref, ddn_ref, dgain_ref = outs
-    gy, gyt, mt, dm = scr
+    gy, gyt, mt, dm = scr[:4]
     step = pl.program_id(0)
     grid_steps(jobs)
+    if len(ins) > 7:
+        counted, info = ins[7:]
+        cot_ref, g_ref = g_ref, scr[4]
+
+        @pl.when(step == 0)
+        def _():
+            n = cot_ref.shape[0]
+            t = lax.axis_index("tensor")
+            base = t % 2 * n
+            masked = counted[:, pl.ds(aligned(base, 128), n)]
+            pos = base + lax.broadcasted_iota(jnp.int32, (1, n), 1)
+            live = (pos < info[0]) & ((t >= 2) | (masked == 1))
+            col = jnp.broadcast_to(jnp.where(live, 1.0, 0.0), (8, n)).T[:, 0:1]
+            g_ref[...] = cot_ref[...].astype(F32) * col
 
     @pl.when(step == 0)
     def _():
@@ -948,21 +987,28 @@
         mt[...] = m_ref[...].T
         dm[...] = jnp.zeros_like(dm)
 
-    u = u_ref[...].astype(F32)
-    dh = mm(gy[...], dn_ref[...])
-    u2 = u * u
-    th = jnp.tanh(GC * (u + GA * (u2 * u)))
-    half = 0.5 * (1.0 + th)
-    h = (u * half).astype(BF)
-    slope = half + 0.5 * u * (1.0 - th * th) * (GC * (1.0 + 3.0 * GA * u2))
-    du = (dh * slope).astype(BF)
-    dm[...] += mm(du, up_ref[...], NT)
-    dup_ref[...] = mm(mt[...], du).astype(BF)
-    ddn_ref[...] = mm(gyt[...], h).astype(BF)
+    cut = u_ref.shape[1] // SPLITB
+    gyv, gytv, mtv = gy[...], gyt[...], mt[...]
+    parts = [slice(i * cut, (i + 1) * cut) for i in range(SPLITB)]
+    dhs = [mm(gyv, dn_ref[:, c]) for c in parts]
+    add = None
+    for c, dh in zip(parts, dhs):
+        u = u_ref[:, c].astype(F32)
+        u2 = u * u
+        th = jnp.tanh(u * (GC + (GC * GA) * u2))
+        half = 0.5 * th + 0.5
+        h = (u * half).astype(BF)
+        slope = half + (u * (1.0 - th * th)) * ((0.5 * GC) + (1.5 * GC * GA) * u2)
+        du = (dh * slope).astype(BF)
+        more = mm(du, up_ref[:, c], NT)
+        add = more if add is None else add + more
+        dup_ref[:, c] = mm(mtv, du).astype(BF)
+        ddn_ref[:, c] = mm(gytv, h).astype(BF)
+    dm[...] += add
 
     @pl.when(step == MLP_STEPS - 1)
     def _():
-        dz, dgain = norm_back(xm_ref[...], gain[...], dm[...])
+        dz, dgain = norm_back(xm_ref[...], gain[at : at + 1], dm[...])
         gm = g_ref[...] + dz
         gm_ref[...] = gm
         go_ref[...] = gm.astype(BF)
@@ -970,7 +1016,7 @@
         finish(jobs)
 
 
-def mlp_back(g, xm, m, u, w, gain, jobs, cid):
+def mlp_back(g, xm, m, u, w, gain, at, top, jobs, cid):
     n, d = xm.shape
     ff = w.shape[1] // 2
     steps = MLP_STEPS
@@ -979,15 +1025,16 @@
     row = pl.BlockSpec((1, d), lambda i: (0, 0))
     wide = pl.BlockSpec((d, fc), lambda i: (0, i))
     return run(
-        mlp_back_body, "mlp_back",
-        [g, xm, m, u, w, w, gain],
+        functools.partial(mlp_back_body, at), "mlp_back",
+        [g, xm, m, u, w, w, gain] + top,
         [
             full, full, full,
             pl.BlockSpec((n, fc), lambda i: (0, i)),
             wide,
             pl.BlockSpec((d, fc), lambda i: (0, i + steps)),
-            row,
-        ],
+            pl.BlockSpec(gain.shape, lambda i: (0, 0)),
+        ]
+        + ([pl.BlockSpec(top[0].shape, lambda i: (0, 0)), smem()] if top else []),
         [
             jax.ShapeDtypeStruct((n, d), F32),
             jax.ShapeDtypeStruct((n, d), BF),
@@ -1001,7 +1048,8 @@
             pltpu.VMEM((d, n), BF),
             pltpu.VMEM((d, n), BF),
             pltpu.VMEM((n, d), F32),
-        ],
+        ]
+        + ([pltpu.VMEM((n, d), F32)] if top else []),
         jobs, cid,
         8 * n * d * ff, 8 * d * ff + 2 * n * ff + 16 * n * d, grid=(steps,),
     )
@@ -1078,6 +1126,8 @@
     w_ref = w_in()
     do_ref[...] = mm(go_ref[...], w_ref[:, 3 * d : 4 * d]).astype(BF)
     outs[0].flush()
+    for j in rest:
+        j.advance()
     wk = w_ref[:, d : 2 * d]
     wv = w_ref[:, 2 * d : 3 * d]
 
@@ -1101,21 +1151,20 @@
 
     pair = part(ks_in, vs_in, mask2, False, cos_in, sin_in, dks_ref, dvs_ref, True)
     lax.fori_loop(0, pairs, pair, 0)
-    for j in rest:
-        j.advance()
     das[...] = (mm(dks_ref[...], wk, NT) + mm(dvs_ref[...], wv, NT)).astype(BF)
     early.go(das)
     outs[4].flush()
     outs[5].flush()
     pair = part(kf_in, vf_in, mask1, True, cosf_in, sinf_in, dkf_ref, dvf_ref, False)
-    lax.fori_loop(0, pairs, pair, 0)
+    lax.fori_loop(0, pairs // 3, pair, 0)
+    for j in rest:
+        j.advance()
+    lax.fori_loop(pairs // 3, pairs, pair, 0)
     outs[1].flush()
     outs[2].flush()
     outs[3].flush()
     daf_ref[...] = (mm(dkf_ref[...], wk, NT) + mm(dvf_ref[...], wv, NT)).astype(BF)
     outs[6].flush()
-    for j in rest:
-        j.advance()
     early.end(das)
     for j in rest:
         j.complete()
@@ -1142,7 +1191,7 @@
     )
 
 
-def back_near_body(ins, outs, scr, jobs):
+def back_near_body(row, ins, outs, scr, jobs):
     (
         info, q_in, do_in, o_in, lse_in, ko_in, vo_in, dqp_in, cos_in, sin_in, go_in, af_in, dkf_in, dvf_in,
         as_in, dks_in, dvs_in, ao_in, w_in, x_in, gm_in, gain_in,
@@ -1169,9 +1218,10 @@
         dvo_s[:, sl] = dva[...].astype(BF)
         return carry
 
-    lax.fori_loop(0, pairs, pair, 0)
+    lax.fori_loop(0, pairs // 2, pair, 0)
     for j in rest:
         j.advance()
+    lax.fori_loop(pairs // 2, pairs, pair, 0)
     db_ref[:, d : 2 * d] = mm(go_in()[...].T, o_ref[...]).astype(BF)
     aot = ao_in()[...].T
     aft = af_in()[...].T
@@ -1180,34 +1230,32 @@
         mm(aot, dvo_s[...]) + mm(aft, dvf_in()[...]) + mm(ast, dvs_in()[...])
     ).astype(BF)
     outs[1].flush()
-    for j in rest:
-        j.advance()
     da_ref[:, 0:d] = mm(aot, dq_s[...]).astype(BF)
     da_ref[:, d : 2 * d] = (
         mm(aot, dko_s[...]) + mm(aft, dkf_in()[...]) + mm(ast, dks_in()[...])
     ).astype(BF)
     outs[0].flush()
+    for j in rest:
+        j.advance()
     w_ref = w_in()
     dao[...] = (
         mm(dko_s[...], w_ref[:, d : 2 * d], NT)
         + mm(dvo_s[...], w_ref[:, 2 * d : 3 * d], NT)
         + mm(dq_s[...], w_ref[:, 0:d], NT)
     )
-    for j in rest:
-        j.advance()
     back.end(dao)
-    dz, dgain = norm_back(x_in()[...].astype(F32), gain_in()[...], dao[...])
+    dz, dgain = norm_back(x_in()[...].astype(F32), gain_in()[row : row + 1], dao[...])
     g_ref[...] = gm_in()[...] + dz
     dgain_ref[...] = dgain
     for j in rest:
         j.complete()
 
 
-def back_near(ins, daf, got, jobs, cid):
+def back_near(row, ins, daf, got, jobs, cid):
     n, d = ins[1].shape
     wide = jax.ShapeDtypeStruct((d, 2 * d), BF)
     return run(
-        back_near_body, "back_near",
+        functools.partial(back_near_body, row), "back_near",
         ins, [smem()] + vmem(len(ins) - 1),
         [wide, wide, jax.ShapeDtypeStruct((n, d), F32), jax.ShapeDtypeStruct((1, d), F32)], vmem(4),
         [
@@ -1226,21 +1274,71 @@
 
 
 def first_body(ins, outs, scr, jobs):
-    x_in, gain_in = ins
-    a_ref = outs[0].ref
-    for j in jobs:
-        j.advance()
+    x_in, gain_in = ins[0:2]
+    narrow, (up, down) = ins[2:6], ins[6:8]
+    layers, d = up.shape[0:2]
+    pa0, ob, db, ot, dt, sem = scr
+    rows = pa0.shape[1]
+    pas = [pa0] + [x.ref for x in outs[1:layers]]
+    pms = [x.ref for x in outs[layers:]]
+    dp = lax.axis_index("dp")
+    at_a = pl.ds(aligned(slot_of(dp, ORDERS[0]) * rows), rows)
+    at_b = pl.ds(aligned(slot_of(dp, ORDERS[1]) * rows), rows)
+    copies = []
+    for l in range(layers):
+        for i, (src, dst) in enumerate(
+            [(x.at[l], ob.at[l, p]) for p, x in enumerate(narrow)]
+            + [(down.at[l], db.at[l]), (up.at[l, at_a, :], pms[l].at[0])]
+        ):
+            copies.append(pltpu.make_async_copy(src, dst, sem.at[l * 6 + i]))
+            copies[-1].start()
+
+    def narrow_parts(l):
+        for p in range(4):
+            ot[p] = ob[l, p].T
+            pas[l][p] = ot[p, at_a if p < 2 else at_b, :]
+
+    for c in copies[0:4]:
+        c.wait()
+    narrow_parts(0)
+    line = jobs[0]
+    line.src = pa0
+    line.advance()
     xh, _ = norm_stats(x_in()[...].astype(F32))
-    a_ref[...] = (xh * gain_in()[...]).astype(BF)
-    for j in jobs:
-        j.complete()
-
-
-def first(x, gain, jobs, cid):
+    outs[0].ref[...] = (xh * gain_in()[0:1]).astype(BF)
+    outs[0].flush()
+    line.advance()
+    for c in copies[4:]:
+        c.wait()
+    for l in range(layers):
+        dt[...] = db[l].T
+        pms[l][1] = dt[at_b, :]
+    line.advance()
+    for l in range(1, layers):
+        narrow_parts(l)
+    line.complete()
+
+
+def first(x, gain, weights, cid):
     n, d = x.shape
+    q, up = weights[0], weights[4]
+    layers, rows = q.shape[0], d >> BITS
+    w, f = q.shape[1], up.shape[2]
+    pa = jax.ShapeDtypeStruct((4, rows, w), BF)
+    pm = jax.ShapeDtypeStruct((2, rows, d), BF)
+    assert f == d
     return run(
-        first_body, "first", [x, gain], vmem(2), [jax.ShapeDtypeStruct((n, d), BF)], vmem(1), [],
-        jobs, cid, 10 * n * d, 4 * n * d,
+        first_body, "first", [x, gain] + list(weights), vmem(2) + any_spec(6),
+        [jax.ShapeDtypeStruct((n, d), BF)] + [pa] * (layers - 1) + [pm] * layers, vmem(2 * layers),
+        [
+            pltpu.VMEM((4, rows, w), BF),
+            pltpu.VMEM((layers, 4, w, d), BF),
+            pltpu.VMEM((layers, f, d), BF),
+            pltpu.VMEM((4, d, w), BF),
+            pltpu.VMEM((d, f), BF),
+            dma(6 * layers),
+        ],
+        [Line(None, False, (4, rows, w))], cid, 10 * n * d, 4 * n * d,
     )
 
 
@@ -1256,9 +1354,9 @@
     for k in reversed(range(count)):
         v = ins[k]()[...].astype(F32)
         w = v.shape[1] // 4
-        for i in range(3):
-            outs[i].ref[k] = v[:, i * w : i * w + w]
-        outs[3].ref[k] = v[:, 3 * w : 4 * w].T
+        vt = v.T
+        for i in range(4):
+            outs[i].ref[k] = vt[i * w : i * w + w]
     for i in range(4):
         outs[i].flush()
 
@@ -1268,20 +1366,28 @@
     d = att[0].shape[0]
     w = att[0].shape[1] // 4
     f = mlps[0].shape[1] // 2
-    shapes = [(layers, d, w)] * 3 + [(layers, w, d), (layers, d, f), (layers, f, d)]
+    shapes = [(layers, w, d)] * 4 + [(layers, d, f), (layers, f, d)]
     return run(
         layout_body, "layout", att + mlps, vmem(2 * layers),
         [jax.ShapeDtypeStruct(x, F32) for x in shapes], vmem(6), [], [], None, 1, 6 * layers * d * (4 * w + 2 * f),
     )[0]
 
 
-def wide_of(every, widths):
-    outs = []
-    at = 0
-    for w in widths:
-        outs += [every[z, :, at : at + w] for z in range(NZ)]
-        at += w
-    return jnp.concatenate(outs, axis=1)
+def wide_of(every):
+    return jnp.concatenate(
+        [every[z, p] for p in range(every.shape[1]) for z in range(NZ)], axis=1
+    )
+
+
+def turning(n):
+    position = np.arange(LMAX, dtype=np.float32)
+    frequency = np.exp(
+        (-math.log(10000.0) * np.arange(HD // 2, dtype=np.float32) / (HD // 2)).astype(np.float32)
+    )
+    angles = (position[:, None] * frequency[None, :]).astype(np.float32).astype(np.float64)
+    cos = np.concatenate([np.cos(angles)] * 4, axis=1)
+    sin = np.concatenate([-np.sin(angles), np.sin(angles)] * 2, axis=1)
+    return [jnp.asarray(x.astype(np.float32).reshape(LMAX // n, n, 128)) for x in (cos, sin)]
 
 
 def by_line(halves, counts):
@@ -1301,64 +1407,27 @@
     out_weight, mlp_gain, up_weight, down_weight,
 ):
     n, d = tokens.shape
-    dp = lax.axis_index("dp")
-    t = lax.axis_index("tensor")
-    info = jnp.stack([lengths[0], t]).astype(jnp.int32)
-    base = (t % 2) * n
-    piece_rows = d >> BITS
-    at_a = slot_of(dp, ORDERS[0]) * piece_rows
-    at_b = slot_of(dp, ORDERS[1]) * piece_rows
-
-    def rows_of(w, at):
-        return lax.dynamic_slice_in_dim(w, at, piece_rows, 0)
-
-    def cols_of(w, at):
-        return lax.dynamic_slice_in_dim(w, at, piece_rows, 1).T
-
-    pa = []
-    pm = []
-    for l in range(LAYERS):
-        pa.append(
-            jnp.concatenate(
-                [
-                    rows_of(query_weight[l], at_a),
-                    rows_of(key_weight[l], at_a),
-                    rows_of(value_weight[l], at_b),
-                    cols_of(out_weight[l], at_b),
-                ],
-                axis=1,
-            )[None]
-        )
-        pm.append(jnp.stack([rows_of(up_weight[l], at_a), cols_of(down_weight[l], at_b)]))
-    widths = (d // NZ,) * 4
-
-    position = jnp.arange(LMAX, dtype=jnp.int32).astype(F32)
-    frequency = jnp.exp(
-        -math.log(10000.0) * jnp.arange(HD // 2, dtype=jnp.int32).astype(F32) / (HD // 2)
+    info = lengths
+    cos_t, sin_t = turning(n)
+    cosf, sinf, cos, sin = (cos_t, 0), (sin_t, 0), (cos_t, 1), (sin_t, 1)
+
+    res, ((every,),) = first(
+        tokens, attn_gain,
+        [x.transpose(0, 2, 1) for x in (query_weight, key_weight, value_weight)]
+        + [out_weight, up_weight, down_weight],
+        0,
     )
-    angles = position[:, None] * frequency[None, :]
-    cos1 = jnp.cos(angles)
-    sin1 = jnp.sin(angles)
-    cos_all = jnp.concatenate([cos1] * 4, axis=1)
-    sin_all = jnp.concatenate([-sin1, sin1] * 2, axis=1)
-    cosf, sinf = cos_all[:n], sin_all[:n]
-    cos = lax.dynamic_slice_in_dim(cos_all, base, n, 0)
-    sin = lax.dynamic_slice_in_dim(sin_all, base, n, 0)
-
-    pos = base + jnp.arange(n, dtype=jnp.int32)
-    masked = lax.dynamic_slice_in_dim(noise_mask[0], base, n, 0)
-    weight = ((pos < lengths[0]) & ((t >= 2) | (masked == 1))).astype(F32)
-
-    (a,), ((every,),) = first(tokens, attn_gain[0:1], [Line(pa[0], False)], 0)
-    piece = wide_of(every[:, 0], widths)
-    ((wa,), (wide,)) = transfer("gather_first", [Gather(piece), Line(pm[0], True)], 1)
+    a = res[0]
+    pa = [None] + list(res[1:LAYERS])
+    pm = res[LAYERS:]
+    ((wa,), (wide,)) = transfer("gather_first", [Gather(wide_of(every)), Line(pm[0], True)], 1)
     was, wms, saved = [], [], []
     x = tokens
     for l in range(LAYERS):
         more = l + 1 < LAYERS
         jobs = [Gather(wide)] + ([Line(pa[l + 1], False)] if more else [])
         res, extra = attend(
-            info, x, a, wa, cosf, sinf, cos, sin, mlp_gain[l : l + 1], jobs, 10 + l
+            info, x, a, wa, cosf, sinf, cos, sin, mlp_gain, l, jobs, 10 + l
         )
         q, ko, vo, kf, vf, ks, vs, o, lse, xm, m = res
         af, as_ = extra[0]
@@ -1367,17 +1436,18 @@
         wms.append(wm)
         jobs = []
         if more:
-            piece = wide_of(extra[2][0][:, 0], widths)
+            piece = wide_of(extra[2][0])
             jobs = [Gather(piece), Line(pm[l + 1], True)]
         nxt = min(l + 1, LAYERS - 1)
-        (x_next, a_next, u), extra = mlp(xm, m, wm, attn_gain[nxt : nxt + 1], jobs, 20 + l)
+        (x_next, a_next, u), extra = mlp(xm, m, wm, attn_gain, nxt, jobs, 20 + l)
         if more:
             wa, wide = extra[0][0], extra[1][0]
         saved.append((x, a, af, as_, q, kf, vf, ks, vs, ko, vo, o, lse, xm, m, u))
         x, a = x_next, a_next
     block_out = x
 
-    g = cotangent.astype(F32) * weight[:, None]
+    g = cotangent
+    top = [noise_mask, info]
     gains = [None] * (2 * LAYERS)
     att = [None] * LAYERS
     mlps = [None] * LAYERS
@@ -1392,7 +1462,8 @@
         jobs = []
         if above:
             jobs = [Reduce(*att_grads), LineSum(by_line(joined(mlp_parts), (1, 1)))]
-        res, extra = mlp_back(g, xm, m, u, wms[l], mlp_gain[l : l + 1], jobs, 30 + l)
+        res, extra = mlp_back(g, xm, m, u, wms[l], mlp_gain, l, top, jobs, 30 + l)
+        top = []
         gm, go, dup, ddn, gains[LAYERS + l] = res
         jobs = [Reduce(dup, ddn, 0, 2)]
         if above:
@@ -1408,9 +1479,10 @@
             mlps[l + 1] = extra[3][0]
             jobs.append(Gather(extra[2][0]))
         res, extra = back_near(
+            l,
             [
                 info, q, do, o, lse, ko, vo, dqp, cos, sin, go, af, dkf, dvf, as_, dks, dvs, a, was[l],
-                x, gm, attn_gain[l : l + 1],
+                x, gm, attn_gain,
             ],
             daf, got, jobs, 50 + l,
         )
@@ -1443,7 +1515,7 @@
     ((att[0],),) = transfer("gather_last", [Gather(part)], 4)
     grads = layout(att, mlps)
     return (
-        block_out, g, gain_sums[:LAYERS], grads[0], grads[1], grads[2], grads[3],
+        block_out, g, gain_sums[:LAYERS], *[x.transpose(0, 2, 1) for x in grads[:3]], grads[3],
         gain_sums[LAYERS:], grads[4], grads[5],
     )
 

time: 559 us -> 504 us (0.902)
  Pallas kernels: 505 us -> 478 us
  local copies, waits for them, and re-layouts: 28.7 us -> 12 us
  other arithmetic: 16.3 us -> 7.89 us
    pallas_call x16, Pallas kernels: 505 us -> 478 us  [run(): pl.pallas_call(kernel, out_shape=tuple(outs), in_specs=list(in_specs), ou...]
    unnamed x46 -> x25, local copies, waits for them, and re-layouts: 9.9 us -> 1.2 us
    slice x10 -> x0, local copies, waits for them, and re-layouts: 5.91 us -> none  [the longest x2 1.67 us: on_device(): cosf, sinf = (cos_all[:n], sin_all[:n])]
where the time goes in v4:
time: 504 us; the launch traced here: 500 us
  Pallas kernels  478 us (95%)
  local copies, waits for them, and re-layouts  12 us (2%)
  other arithmetic  7.89 us (2%)
    pallas_call x16, Pallas kernels, run(): pl.pallas_call(kernel, out_shape=tuple(outs), in_specs=list(in_specs), ou...  478 us

profile of v4, /device:TPU:0, one launch (start us, length us, event | category | flops | bytes accessed | tf_op | source)
XLA Modules:
  0.0 499.5 jit_solution(17287628316004678983)
XLA Ops:
  1.3 24.0 %first.1 = (bf16[512,768]{1,0:T(8,128)(2,1)}, bf16[4,96,192]{2,1,0:T(8,128)(2,1)}, bf16[2,96,768]{2,1,0:T(8,128)(2,1)}, bf16[2,96,768]{2,1,0:T(8,128)(2,1)}, bf16[4,4,96,192]{3,2,1,0:T(8,128)(2,1)}) custom-call(bf16[512,768]{1,0:T(8,128)(2,1)} %refs_19_.1, f32[2,768]{1,0:T(2,128)} %refs_21_.3, bf16[2,192,768]{2,1,0:T(8,128)(2,1)} %bitcast.102, ...), custom_call_target="tpu_custom_call" | custom-call | flops 3932160 | bytes 1572864 | tf_op jit(solution)/shard_map/first/pallas_call | solution.py:658
  25.3 1.2 slice_bitcast_fusion.16
  26.5 1.1 concatenate.33.refs_0_
  27.7 28.4 %gather_first.1 = (bf16[768,3072]{1,0:T(8,128)(2,1)}, bf16[96,6144]{1,0:T(8,128)(2,1)}) custom-call(bf16[96,3072]{1,0:T(8,128)(2,1)} %concatenate.33.refs_0_, bf16[2,96,768]{2,1,0:T(8,128)(2,1)} %get-tuple-element.116.refs_1_), custom_call_target="tpu_custom_call" | custom-call | flops 1 | bytes 16777216 | tf_op jit(solution)/shard_map/gather_first/pallas_call | solution.py:658
  56.0 58.2 %attend.2 = (bf16[512,768]{1,0:T(8,128)(2,1)}, bf16[512,768]{1,0:T(8,128)(2,1)}, bf16[512,768]{1,0:T(8,128)(2,1)}, bf16[512,768]{1,0:T(8,128)(2,1)}, bf16[512,76...) custom-call(s32[1]{0:T(128)S(6)} %copy.49.refs_0_.refs_8_, ...), custom_call_target="tpu_custom_call" | custom-call | flops 12884901888 | bytes 17301504 | tf_op jit(solution)/shard_map/attend/pallas_call | solution.py:658
  114.3 1.2 slice_bitcast_fusion
  115.5 1.1 concatenate.34.refs_5_
  116.6 32.3 %mlp.2 = (f32[512,768]{1,0:T(8,128)}, bf16[512,768]{1,0:T(8,128)(2,1)}, bf16[512,3072]{1,0:T(8,128)(2,1)}, bf16[768,3072]{1,0:T(8,128)(2,1)}, bf16[96,6144]{1,0:T(8,128)(2,1)}) custom-call(f32[512,768]{1,0:T(8,128)} %get-tuple-element.120.refs_0_.refs_1_, bf16[512,768]{1,0:T(8,128)(2,1)} %get-tuple-element.121.refs_1_.refs_2_, ...), custom_call_target="tpu_custom_call" | custom-call | flops 4831838208 | bytes 16515072 | tf_op jit(solution)/shard_map/mlp/pallas_call | solution.py:658
  148.9 51.8 %attend.3 = (bf16[512,768]{1,0:T(8,128)(2,1)}, bf16[512,768]{1,0:T(8,128)(2,1)}, bf16[512,768]{1,0:T(8,128)(2,1)}, bf16[512,768]{1,0:T(8,128)(2,1)}, bf16[512,76...) custom-call(s32[1]{0:T(128)S(6)} %copy.49.refs_0_.refs_8_, ...), custom_call_target="tpu_custom_call" | custom-call | flops 12884901888 | bytes 17301504 | tf_op jit(solution)/shard_map/attend/pallas_call | solution.py:658
  200.7 11.2 %mlp.3 = (f32[512,768]{1,0:T(8,128)}, bf16[512,768]{1,0:T(8,128)(2,1)}, bf16[512,3072]{1,0:T(8,128)(2,1)}) custom-call(f32[512,768]{1,0:T(8,128)} %get-tuple-element.129.refs_0_.refs_1_, bf16[512,768]{1,0:T(8,128)(2,1)} %get-tuple-element.130.refs_1_.refs_2_, bf16[768,6144]{1,0:T(8,128)(2,1)} %get-tuple-element.131.refs_2_.refs_3_.refs_4_.refs_5_, ...), custom_call_target="tpu_custom_call" | custom-call | flops 4831838208 | bytes 16515072 | tf_op jit(solution)/shard_map/mlp/pallas_call | solution.py:658
  211.9 18.9 %mlp_back.2 = (f32[512,768]{1,0:T(8,128)}, bf16[512,768]{1,0:T(8,128)(2,1)}, bf16[768,3072]{1,0:T(8,128)(2,1)}, bf16[768,3072]{1,0:T(8,128)(2,1)}, f32[1,768]{1,0:T(1,128)}) custom-call(bf16[512,768]{1,0:T(8,128)(2,1)} %refs_0_.9, f32[512,768]{1,0:T(8,128)} %get-tuple-element.129.refs_0_.refs_1_, bf16[512,768]{1,0:T(8,128)(2,1)} %get-tuple-element.130.refs_1_.refs_2_, ...), custom_call_target="tpu_custom_call" | custom-call | flops 9663676416 | bytes 28311552 | tf_op jit(solution)/shard_map/mlp_back/pallas_call | solution.py:658
  230.8 34.2 %back_far.2 = (bf16[512,768]{1,0:T(8,128)(2,1)}, f32[768,512]{1,0:T(8,128)}, bf16[512,768]{1,0:T(8,128)(2,1)}, bf16[512,768]{1,0:T(8,128)(2,1)}, bf16[512,768]{1...) custom-call(s32[1]{0:T(128)S(6)} %copy.49.refs_0_.refs_8_, ...), custom_call_target="tpu_custom_call" | custom-call | flops 17112760320 | bytes 18874368 | tf_op jit(solution)/shard_map/back_far/pallas_call | solution.py:658
  265.0 35.2 %back_near.2 = (bf16[768,1536]{1,0:T(8,128)(2,1)}, bf16[768,1536]{1,0:T(8,128)(2,1)}, f32[512,768]{1,0:T(8,128)}, f32[1,768]{1,0:T(1,128)}, bf16[96,1536]{1,0:T(8,128)(2,1)}, /*index=5*/bf16[96,1536]{1,0:T(8,128)(2,1)}) custom-call(s32[1]{0:T(128)S(6)} %copy.49.refs_0_.refs_8_, bf16[512,768]{1,0:T(8,128)(2,1)} %get-tuple-element.134.refs_3_.refs_1_, ...), custom_call_target="tpu_custom_call" | custom-call | flops 12683575296 | bytes 28311552 | tf_op jit(solution)/shard_map/back_near/pallas_call | solution.py:658
  300.2 1.2 pad_maximum_fusion
  302.6 36.4 %mlp_back.3 = (f32[512,768]{1,0:T(8,128)}, bf16[512,768]{1,0:T(8,128)(2,1)}, bf16[768,3072]{1,0:T(8,128)(2,1)}, bf16[768,3072]{1,0:T(8,128)(2,1)}, f32[1,768]{1,...) custom-call(f32[512,768]{1,0:T(8,128)} %get-tuple-element.158.refs_0_, ...), custom_call_target="tpu_custom_call" | custom-call | flops 9663676416 | bytes 28311552 | tf_op jit(solution)/shard_map/mlp_back/pallas_call | solution.py:658
  342.1 38.3 %back_far.3 = (bf16[512,768]{1,0:T(8,128)(2,1)}, f32[768,512]{1,0:T(8,128)}, bf16[512,768]{1,0:T(8,128)(2,1)}, bf16[512,768]{1,0:T(8,128)(2,1)}, bf16[512,768]{1...) custom-call(s32[1]{0:T(128)S(6)} %copy.49.refs_0_.refs_8_, ...), custom_call_target="tpu_custom_call" | custom-call | flops 17112760320 | bytes 18874368 | tf_op jit(solution)/shard_map/back_far/pallas_call | solution.py:658
  380.5 36.0 %back_near.3 = (bf16[768,1536]{1,0:T(8,128)(2,1)}, bf16[768,1536]{1,0:T(8,128)(2,1)}, f32[512,768]{1,0:T(8,128)}, f32[1,768]{1,0:T(1,128)}, bf16[96,1536]{1,0:T(...) custom-call(s32[1]{0:T(128)S(6)} %copy.49.refs_0_.refs_8_, ...), custom_call_target="tpu_custom_call" | custom-call | flops 12683575296 | bytes 28311552 | tf_op jit(solution)/shard_map/back_near/pallas_call | solution.py:658
  416.6 1.3 pad_maximum_fusion.4.refs_2_
  420.2 33.3 %reduce_last.1 = (bf16[96,1536]{1,0:T(8,128)(2,1)}, bf16[96,1536]{1,0:T(8,128)(2,1)}, f32[4,768]{1,0:T(4,128)}, bf16[96,1536]{1,0:T(8,128)(2,1)}) custom-call(bf16[768,1536]{1,0:T(8,128)(2,1)} %get-tuple-element.193.refs_0_, bf16[768,1536]{1,0:T(8,128)(2,1)} %get-tuple-element.194.refs_1_, f32[4,768]{1,0:T(4,128)} %pad_maximum_fusion.4.refs_2_, ...), custom_call_target="tpu_custom_call" | custom-call | flops 1 | bytes 16777216 | tf_op jit(solution)/shard_map/reduce_last/pallas_call | solution.py:658
  457.3 18.2 %line_last.1 = (bf16[96,768]{1,0:T(8,128)(2,1)}, f32[4,768]{1,0:T(4,128)}, bf16[768,1536]{1,0:T(8,128)(2,1)}) custom-call(bf16[4,96,768]{2,1,0:T(8,128)(2,1)} %maximum_bitcast_fusion.3.refs_0_, f32[4,4,768]{2,1,0:T(4,128)} %broadcast_in_dim.3.refs_1_, bf16[96,1536]{1,0:T(8,128)(2,1)} %get-tuple-element.206.refs_2_), custom_call_target="tpu_custom_call" | custom-call | flops 1 | bytes 16777216 | tf_op jit(solution)/shard_map/line_last/pallas_call | solution.py:658
  475.5 1.4 fusion.4
  476.9 11.9 %gather_last.1.refs_0_ = bf16[768,768]{1,0:T(8,128)(2,1)} custom-call(bf16[96,768]{1,0:T(8,128)(2,1)} %get-tuple-element.208.refs_0_), custom_call_target="tpu_custom_call" | custom-call | flops 1 | bytes 16777216 | tf_op jit(solution)/shard_map/gather_last/pallas_call | solution.py:658
  488.8 9.3 %layout.1 = (f32[2,192,768]{2,1,0:T(8,128)}, f32[2,192,768]{2,1,0:T(8,128)}, f32[2,192,768]{2,1,0:T(8,128)}, f32[2,192,768]{2,1,0:T(8,128)}, f32[2,768,768]{2,1,0:T(8,128)}, /*index=5*/f32[2,768,768]{2,1,0:T(8,128)}) custom-call(bf16[768,768]{1,0:T(8,128)(2,1)} %gather_last.1.refs_0_, bf16[768,768]{1,0:T(8,128)(2,1)} %get-tuple-element.209.refs_1_, ...), custom_call_target="tpu_custom_call" | custom-call | flops 1 | bytes 21233664 | tf_op jit(solution)/shard_map/layout/pallas_call | solution.py:658
  498.2 1.1 copy.50
  (55 shorter events, 10.2 us)
Async XLA Ops:
  265.0 35.3 %copy-start.1 = (bf16[96,1536]{1,0:T(8,128)(2,1)S(1)}, bf16[96,1536]{1,0:T(8,128)(2,1)}, u32[]{:S(2)}) copy-start(bf16[96,1536]{1,0:T(8,128)(2,1)} %get-tuple-element.162) | copy-start | bytes 884740
  265.0 35.3 %copy-start.2 = (bf16[96,1536]{1,0:T(8,128)(2,1)S(1)}, bf16[96,1536]{1,0:T(8,128)(2,1)}, u32[]{:S(2)}) copy-start(bf16[96,1536]{1,0:T(8,128)(2,1)} %get-tuple-element.164) | copy-start | bytes 884740
  339.0 1.5 copy-start.3
  380.5 36.1 %copy-start.9 = (f32[1,768]{1,0:T(1,128)S(1)}, f32[1,768]{1,0:T(1,128)}, u32[]{:S(2)}) copy-start(f32[1,768]{1,0:T(1,128)} %get-tuple-element.198) | copy-start | bytes 9220
  380.5 36.1 %copy-start.10 = (f32[1,768]{1,0:T(1,128)S(1)}, f32[1,768]{1,0:T(1,128)}, u32[]{:S(2)}) copy-start(f32[1,768]{1,0:T(1,128)} %get-tuple-element.196) | copy-start | bytes 9220
  380.5 36.1 %copy-start.11 = (f32[1,768]{1,0:T(1,128)S(1)}, f32[1,768]{1,0:T(1,128)}, u32[]{:S(2)}) copy-start(f32[1,768]{1,0:T(1,128)} %get-tuple-element.197) | copy-start | bytes 9220
  380.5 37.4 %copy-start.6 = (bf16[96,1536]{1,0:T(8,128)(2,1)S(1)}, bf16[96,1536]{1,0:T(8,128)(2,1)}, u32[]{:S(2)}) copy-start(bf16[96,1536]{1,0:T(8,128)(2,1)} %get-tuple-element.199) | copy-start | bytes 884740
  417.9 1.1 copy-start.5
  417.9 1.1 copy-start.7
  453.5 1.3 copy-start.8
  453.5 2.2 copy-start.4
  488.8 9.4 %copy-start = (f32[512,768]{1,0:T(8,128)S(1)}, f32[512,768]{1,0:T(8,128)}, u32[]{:S(2)}) copy-start(f32[512,768]{1,0:T(8,128)} %get-tuple-element.273) | copy-start | bytes 4718596

commit v5 on v4

--- a/solution.py
+++ b/solution.py
@@ -155,20 +155,24 @@
 class Gather(Job):
     plane = 1
 
-    def __init__(self, piece):
-        self.rows, n = piece.shape
+    def __init__(self, piece, shape=None):
+        self.rows, n = shape if piece is None else piece.shape
         self.half = n // 2
-        self.ins, self.in_specs = [piece], vmem(1)
+        self.src = None
+        self.ins, self.in_specs = ([], []) if piece is None else ([piece], vmem(1))
         self.outs, self.out_specs = [jax.ShapeDtypeStruct((self.rows << BITS, n), BF)], any_spec()
         self.scratch = [dma(2 * BITS), dma(2 * BITS), dma(2)]
 
     def cols(self, i):
         return pl.ds(i * self.half, self.half)
+
+    def source(self):
+        return self.i[0] if self.src is None else self.src
 
     def own(self, i):
         at = slot_of(self.dp, ORDERS[i]) * self.rows
         return pltpu.make_async_copy(
-            self.i[0].at[:, self.cols(i)],
+            self.source().at[:, self.cols(i)],
             self.o[0].at[pl.ds(aligned(at), self.rows), self.cols(i)],
             self.s[2].at[i],
         )
@@ -179,7 +183,7 @@
         at = slot_of(self.dp, ORDERS[i]) // (1 << s) * size
         there = self.o[0].at[pl.ds(aligned(at), size), self.cols(i)]
         return remote(
-            self.i[0].at[:, self.cols(i)] if s == 0 else there, there,
+            self.source().at[:, self.cols(i)] if s == 0 else there, there,
             self.s[0].at[2 * s + i], self.s[1].at[2 * s + i], partner(self.dp, b), self.t,
         )
 
@@ -348,17 +352,27 @@
     line = 1
     steps = 1
 
-    def __init__(self, parts):
-        shape = parts.shape[1:]
-        self.ins, self.in_specs = [parts], vmem(1)
-        self.outs, self.out_specs = [jax.ShapeDtypeStruct(shape, parts.dtype)], vmem(1)
-        self.scratch = [pltpu.VMEM((NZ - 1,) + shape, parts.dtype), dma(3), dma(3)]
+    def __init__(self, parts, shape=None, kind=BF, same=False):
+        shape = parts.shape[1:] if shape is None else shape
+        self.same = same
+        self.src = self.dst = None
+        self.outs = self.out_specs = []
+        self.ins, self.in_specs = ([], []) if parts is None else ([parts], vmem(1))
+        if parts is not None:
+            kind = parts.dtype
+            self.outs, self.out_specs = [jax.ShapeDtypeStruct(shape, kind)], vmem(1)
+        self.scratch = [pltpu.VMEM((NZ - 1,) + tuple(shape), kind), dma(3), dma(3)]
+
+    def source(self, z):
+        ref = self.i[0] if self.src is None else self.src
+        return ref if self.same else ref.at[z]
 
     def copies(self):
         for s in (1, 2, 3):
             z = (self.t + s) % NZ
             yield remote(
-                self.i[0].at[z], self.s[0].at[s - 1], self.s[1].at[s - 1], self.s[2].at[s - 1], self.dp, z
+                self.source(z), self.s[0].at[s - 1], self.s[1].at[s - 1], self.s[2].at[s - 1],
+                self.dp, z,
             )
 
     def start(self, s):
@@ -369,10 +383,59 @@
         for c in self.copies():
             c.wait()
         got = self.s[0]
-        total = self.i[0][self.t].astype(F32)
+        total = self.source(self.t)[...].astype(F32)
         for k in range(NZ - 1):
             total = total + got[k].astype(F32)
-        self.o[0][...] = total.astype(self.o[0].dtype)
+        out = self.o[0] if self.dst is None else self.dst
+        out[...] = total.astype(out.dtype)
+
+
+class LineSumWide(Job):
+    line = 1
+    steps = 1
+
+    def __init__(self, arrays):
+        self.w = arrays[0].shape[1] // 2
+        self.ins, self.in_specs = list(arrays), vmem(4)
+        shape = arrays[0].shape
+        self.outs, self.out_specs = [jax.ShapeDtypeStruct(shape, BF)], vmem(1)
+        self.scratch = [pltpu.VMEM((NZ - 1,) + shape, BF), dma(6), dma(6)]
+
+    def part(self, kind, half, z):
+        return self.i[2 * kind + half].at[:, pl.ds(aligned(z % 2 * self.w, 128), self.w)]
+
+    def copy(self, s, kind, half):
+        z = (self.t + s) % NZ
+        k = (s - 1) * 2 + kind
+        return remote(
+            self.part(kind, half, z), self.s[0].at[s - 1, :, pl.ds(kind * self.w, self.w)],
+            self.s[1].at[k], self.s[2].at[k], self.dp, z,
+        )
+
+    def start(self, step):
+        for s in (1, 2, 3):
+            for half in (0, 1):
+
+                @pl.when((self.t + s) % NZ // 2 == half)
+                def _(s=s, half=half):
+                    for kind in (0, 1):
+                        self.copy(s, kind, half).start()
+
+    def wait(self, step):
+        for s in (1, 2, 3):
+            for kind in (0, 1):
+                self.copy(s, kind, 0).wait()
+        got, out = self.s[0], self.o[0]
+        for half in (0, 1):
+
+            @pl.when(self.t // 2 == half)
+            def _(half=half):
+                for kind in (0, 1):
+                    at = slice(kind * self.w, (kind + 1) * self.w)
+                    total = self.part(kind, half, self.t)[...].astype(F32)
+                    for k in range(NZ - 1):
+                        total = total + got[k, :, at].astype(F32)
+                    out[:, at] = total.astype(BF)
 
 
 class PlaneSum(Job):
@@ -537,17 +600,21 @@
             self.put(daf, 0).wait_send()
 
 
+def at_points(j, points):
+    return points.get(type(j).__name__, (0,) * j.steps)
+
+
 def steps_at(jobs, point, points):
-    for s in range(max([j.steps for j in jobs], default=0)):
-        now = [j for j in jobs if s < j.steps and s * points // j.steps == point]
-        for j in now:
-            if s > 0:
-                j.wait(s - 1)
-        for j in now:
-            j.start(s)
-
-
-def finish(jobs):
+    for j in jobs:
+        for s in range(j.steps):
+            if at_points(j, points)[s] == point:
+                if s > 0:
+                    j.wait(s - 1)
+                j.start(s)
+
+
+def finish(jobs, points):
+    steps_at(jobs, -1, points)
     for j in jobs:
         if j.steps:
             j.wait(j.steps - 1)
@@ -894,11 +961,15 @@
     return u * (0.5 * jnp.tanh(u * (GC + (GC * GA) * (u * u))) + 0.5)
 
 
-def grid_steps(jobs):
+FORWARD = {"Gather": (0, 2, -1), "Line": (0, 3, -1)}
+BACKWARD = {"Reduce": (0, 1, 5)}
+
+
+def grid_steps(jobs, points):
     step = pl.program_id(0)
     for point in range(MLP_STEPS):
-        if any(s * MLP_STEPS // j.steps == point for j in jobs for s in range(j.steps)):
-            pl.when(step == point)(functools.partial(steps_at, jobs, point, MLP_STEPS))
+        if any(point in at_points(j, points) for j in jobs):
+            pl.when(step == point)(functools.partial(steps_at, jobs, point, points))
 
 
 def mlp_body(row, ins, outs, scr, jobs):
@@ -906,7 +977,7 @@
     x_ref, a_ref, u_ref = outs
     (acc,) = scr
     step = pl.program_id(0)
-    grid_steps(jobs)
+    grid_steps(jobs, FORWARD)
 
     @pl.when(step == 0)
     def _():
@@ -927,7 +998,7 @@
         x_ref[...] = x
         xh, _ = norm_stats(x)
         a_ref[...] = (xh * gain[row : row + 1]).astype(BF)
-        finish(jobs)
+        finish(jobs, FORWARD)
 
 
 def mlp(xm, m, w, gain, row, jobs, cid):
@@ -963,7 +1034,7 @@
     gm_ref, go_ref, dup_ref, ddn_ref, dgain_ref = outs
     gy, gyt, mt, dm = scr[:4]
     step = pl.program_id(0)
-    grid_steps(jobs)
+    grid_steps(jobs, BACKWARD)
     if len(ins) > 7:
         counted, info = ins[7:]
         cot_ref, g_ref = g_ref, scr[4]
@@ -1013,7 +1084,7 @@
         gm_ref[...] = gm
         go_ref[...] = gm.astype(BF)
         dgain_ref[...] = dgain
-        finish(jobs)
+        finish(jobs, BACKWARD)
 
 
 def mlp_back(g, xm, m, u, w, gain, at, top, jobs, cid):
@@ -1390,6 +1461,68 @@
     return [jnp.asarray(x.astype(np.float32).reshape(LMAX // n, n, 128)) for x in (cos, sin)]
 
 
+def over_rest(arrays):
+    n = lax.axis_size("dp")
+    for b in range(BITS, n.bit_length() - 1):
+        arrays = [x + lax.ppermute(x, "dp", [(i, i ^ (1 << b)) for i in range(n)]) for x in arrays]
+    return arrays
+
+
+def tail_body(ins, outs, scr, jobs):
+    red, gains, wide, gain_line, att_line, wide_gather, att_gather = jobs
+    every, part, total = scr
+    for j in (red, gains, wide):
+        j.advance()
+    red.advance()
+    gains.advance()
+    red.advance()
+    gains.advance()
+    wide.complete()
+    wide_gather.src = wide.o[0]
+    gains.complete()
+    gain_line.src, gain_line.dst = gains.o[0], total
+    gain_line.advance()
+    red.complete()
+    a = red.o[0][...].astype(F32)
+    b = red.o[1][...].astype(F32)
+    w = a.shape[1] // 2
+    c = w // NZ
+    for z in range(NZ):
+        cols = [x[:, k * w + z * c : k * w + z * c + c] for x in (a, b) for k in (0, 1)]
+        every[z] = jnp.concatenate(cols, axis=1).astype(BF)
+    att_line.src, att_line.dst = every, part
+    att_line.advance()
+    wide_gather.advance()
+    wide_gather.advance()
+    att_line.complete()
+    att_gather.src = part
+    att_gather.advance()
+    wide_gather.advance()
+    att_gather.advance()
+    wide_gather.complete()
+    att_gather.advance()
+    gain_line.complete()
+    outs[0].ref[...] = total[...]
+    att_gather.complete()
+
+
+def tail(att_grads, gain_rows, mlp_arrays, cid):
+    rows = att_grads[0].shape[0] >> BITS
+    w = att_grads[0].shape[1] // 2
+    wide = LineSumWide(mlp_arrays)
+    jobs = [
+        Reduce(*att_grads), PlaneSum(gain_rows), wide,
+        LineSum(None, gain_rows.shape, F32, True), LineSum(None, (rows, w)),
+        Gather(None, wide.outs[0].shape), Gather(None, (rows, w)),
+    ]
+    res, extra = run(
+        tail_body, "tail", [gain_rows], vmem(1), [jax.ShapeDtypeStruct(gain_rows.shape, F32)], vmem(1),
+        [pltpu.VMEM((NZ, rows, w), BF), pltpu.VMEM((rows, w), BF), pltpu.VMEM(gain_rows.shape, F32)],
+        jobs, cid, 1, 1 << 24,
+    )
+    return res[0], extra[5][0], extra[6][0]
+
+
 def by_line(halves, counts):
     n = lax.axis_size("dp")
     cols = []
@@ -1420,7 +1553,7 @@
     a = res[0]
     pa = [None] + list(res[1:LAYERS])
     pm = res[LAYERS:]
-    ((wa,), (wide,)) = transfer("gather_first", [Gather(wide_of(every)), Line(pm[0], True)], 1)
+    (wa,), (wide,) = transfer("gather_first", [Gather(wide_of(every)), Line(pm[0], True)], 1)
     was, wms, saved = [], [], []
     x = tokens
     for l in range(LAYERS):
@@ -1437,11 +1570,11 @@
         jobs = []
         if more:
             piece = wide_of(extra[2][0])
-            jobs = [Gather(piece), Line(pm[l + 1], True)]
+            jobs = [Line(pm[l + 1], True), Gather(piece)]
         nxt = min(l + 1, LAYERS - 1)
         (x_next, a_next, u), extra = mlp(xm, m, wm, attn_gain, nxt, jobs, 20 + l)
         if more:
-            wa, wide = extra[0][0], extra[1][0]
+            wide, wa = extra[0][0], extra[1][0]
         saved.append((x, a, af, as_, q, kf, vf, ks, vs, ko, vo, o, lse, xm, m, u))
         x, a = x_next, a_next
     block_out = x
@@ -1451,17 +1584,14 @@
     gains = [None] * (2 * LAYERS)
     att = [None] * LAYERS
     mlps = [None] * LAYERS
-    att_grads = mlp_parts = None
-
-    def joined(parts):
-        return [jnp.concatenate([p[i] for p in parts], axis=1) for i in (0, 1)]
+    att_grads = mlp_parts = mlp_arrays = None
 
     for l in reversed(range(LAYERS)):
         x, a, af, as_, q, kf, vf, ks, vs, ko, vo, o, lse, xm, m, u = saved[l]
         above = l + 1 < LAYERS
         jobs = []
         if above:
-            jobs = [Reduce(*att_grads), LineSum(by_line(joined(mlp_parts), (1, 1)))]
+            jobs = [Reduce(*att_grads), LineSumWide(mlp_arrays)]
         res, extra = mlp_back(g, xm, m, u, wms[l], mlp_gain, l, top, jobs, 30 + l)
         top = []
         gm, go, dup, ddn, gains[LAYERS + l] = res
@@ -1487,32 +1617,36 @@
             daf, got, jobs, 50 + l,
         )
         mlp_parts.append(extra[1])
+        mlp_arrays = over_rest([p[i] for i in (0, 1) for p in mlp_parts])
         if above:
             att[l + 1] = extra[2][0]
         att_grads = res[0:2]
         g, gains[l] = res[2:4]
 
     gain_rows = jnp.concatenate(gains, axis=0)
-    (sums, (gain_rows,), (mlp_sum,)) = transfer(
-        "reduce_last",
-        [Reduce(*att_grads), PlaneSum(gain_rows), LineSum(by_line(joined(mlp_parts), (1, 1)))],
-        2,
-    )
-    for b in range(BITS, lax.axis_size("dp").bit_length() - 1):
-        size = lax.axis_size("dp")
-        gain_rows = gain_rows + lax.ppermute(
-            gain_rows, "dp", [(i, i ^ (1 << b)) for i in range(size)]
+    if lax.axis_size("dp") == 1 << BITS:
+        gain_sums, mlps[0], att[0] = tail(att_grads, gain_rows, mlp_arrays, 2)
+    else:
+        (sums, (gain_rows,), (mlp_sum,)) = transfer(
+            "reduce_last",
+            [Reduce(*att_grads), PlaneSum(gain_rows), LineSumWide(mlp_arrays)],
+            2,
         )
-    (part,), (gain_sums,), (mlps[0],) = transfer(
-        "line_last",
-        [
-            LineSum(by_line(sums, (2, 2))),
-            LineSum(jnp.broadcast_to(gain_rows, (NZ,) + gain_rows.shape)),
-            Gather(mlp_sum),
-        ],
-        3,
-    )
-    ((att[0],),) = transfer("gather_last", [Gather(part)], 4)
+        for b in range(BITS, lax.axis_size("dp").bit_length() - 1):
+            size = lax.axis_size("dp")
+            gain_rows = gain_rows + lax.ppermute(
+                gain_rows, "dp", [(i, i ^ (1 << b)) for i in range(size)]
+            )
+        (part,), (gain_sums,), (mlps[0],) = transfer(
+            "line_last",
+            [
+                LineSum(by_line(sums, (2, 2))),
+                LineSum(jnp.broadcast_to(gain_rows, (NZ,) + gain_rows.shape)),
+                Gather(mlp_sum),
+            ],
+            3,
+        )
+        ((att[0],),) = transfer("gather_last", [Gather(part)], 4)
     grads = layout(att, mlps)
     return (
         block_out, g, gain_sums[:LAYERS], *[x.transpose(0, 2, 1) for x in grads[:3]], grads[3],

time: 504 us -> 489 us (0.970)
  Pallas kernels: 478 us -> 472 us
  other arithmetic: 7.89 us -> 2.36 us
    pallas_call x16 -> x14, Pallas kernels: 478 us -> 472 us  [run(): pl.pallas_call(kernel, out_shape=tuple(outs), in_specs=list(in_specs), ou...]
where the time goes in v5:
time: 489 us; the launch traced here: 485 us
  Pallas kernels  472 us (97%)
  local copies, waits for them, and re-layouts  9.27 us (2%)
    pallas_call x14, Pallas kernels, run(): pl.pallas_call(kernel, out_shape=tuple(outs), in_specs=list(in_specs), ou...  472 us

profile of v5, /device:TPU:0, one launch (start us, length us, event | category | flops | bytes accessed | tf_op | source)
XLA Modules:
  0.0 484.9 jit_solution(16955129303805479792)
XLA Ops:
  1.3 24.0 %first.1 = (bf16[512,768]{1,0:T(8,128)(2,1)}, bf16[4,96,192]{2,1,0:T(8,128)(2,1)}, bf16[2,96,768]{2,1,0:T(8,128)(2,1)}, bf16[2,96,768]{2,1,0:T(8,128)(2,1)}, bf16[4,4,96,192]{3,2,1,0:T(8,128)(2,1)}) custom-call(bf16[512,768]{1,0:T(8,128)(2,1)} %refs_19_.1, f32[2,768]{1,0:T(2,128)} %refs_21_.3, bf16[2,192,768]{2,1,0:T(8,128)(2,1)} %bitcast.72, ...), custom_call_target="tpu_custom_call" | custom-call | flops 3932160 | bytes 1572864 | tf_op jit(solution)/shard_map/first/pallas_call | solution.py:725
  25.3 1.2 slice_bitcast_fusion.16
  26.5 1.1 concatenate.12.refs_0_
  27.6 28.4 %gather_first.1 = (bf16[768,3072]{1,0:T(8,128)(2,1)}, bf16[96,6144]{1,0:T(8,128)(2,1)}) custom-call(bf16[96,3072]{1,0:T(8,128)(2,1)} %concatenate.12.refs_0_, bf16[2,96,768]{2,1,0:T(8,128)(2,1)} %get-tuple-element.112.refs_1_), custom_call_target="tpu_custom_call" | custom-call | flops 1 | bytes 16777216 | tf_op jit(solution)/shard_map/gather_first/pallas_call | solution.py:725
  56.0 58.2 %attend.2 = (bf16[512,768]{1,0:T(8,128)(2,1)}, bf16[512,768]{1,0:T(8,128)(2,1)}, bf16[512,768]{1,0:T(8,128)(2,1)}, bf16[512,768]{1,0:T(8,128)(2,1)}, bf16[512,76...) custom-call(s32[1]{0:T(128)S(6)} %copy.29.refs_0_.refs_8_, ...), custom_call_target="tpu_custom_call" | custom-call | flops 12884901888 | bytes 17301504 | tf_op jit(solution)/shard_map/attend/pallas_call | solution.py:725
  114.2 1.2 slice_bitcast_fusion
  115.4 1.1 concatenate.13.refs_6_
  116.6 30.5 %mlp.2 = (f32[512,768]{1,0:T(8,128)}, bf16[512,768]{1,0:T(8,128)(2,1)}, bf16[512,3072]{1,0:T(8,128)(2,1)}, bf16[96,6144]{1,0:T(8,128)(2,1)}, bf16[768,3072]{1,0:T(8,128)(2,1)}) custom-call(f32[512,768]{1,0:T(8,128)} %get-tuple-element.116.refs_0_.refs_1_, bf16[512,768]{1,0:T(8,128)(2,1)} %get-tuple-element.117.refs_1_.refs_2_, ...), custom_call_target="tpu_custom_call" | custom-call | flops 4831838208 | bytes 16515072 | tf_op jit(solution)/shard_map/mlp/pallas_call | solution.py:725
  147.1 53.1 %attend.3 = (bf16[512,768]{1,0:T(8,128)(2,1)}, bf16[512,768]{1,0:T(8,128)(2,1)}, bf16[512,768]{1,0:T(8,128)(2,1)}, bf16[512,768]{1,0:T(8,128)(2,1)}, bf16[512,76...) custom-call(s32[1]{0:T(128)S(6)} %copy.29.refs_0_.refs_8_, ...), custom_call_target="tpu_custom_call" | custom-call | flops 12884901888 | bytes 17301504 | tf_op jit(solution)/shard_map/attend/pallas_call | solution.py:725
  200.2 11.1 %mlp.3 = (f32[512,768]{1,0:T(8,128)}, bf16[512,768]{1,0:T(8,128)(2,1)}, bf16[512,3072]{1,0:T(8,128)(2,1)}) custom-call(f32[512,768]{1,0:T(8,128)} %get-tuple-element.125.refs_0_.refs_1_, bf16[512,768]{1,0:T(8,128)(2,1)} %get-tuple-element.126.refs_1_.refs_2_, bf16[768,6144]{1,0:T(8,128)(2,1)} %get-tuple-element.127.refs_2_.refs_3_.refs_4_.refs_5_, ...), custom_call_target="tpu_custom_call" | custom-call | flops 4831838208 | bytes 16515072 | tf_op jit(solution)/shard_map/mlp/pallas_call | solution.py:725
  211.3 19.1 %mlp_back.2 = (f32[512,768]{1,0:T(8,128)}, bf16[512,768]{1,0:T(8,128)(2,1)}, bf16[768,3072]{1,0:T(8,128)(2,1)}, bf16[768,3072]{1,0:T(8,128)(2,1)}, f32[1,768]{1,0:T(1,128)}) custom-call(bf16[512,768]{1,0:T(8,128)(2,1)} %refs_0_.9, f32[512,768]{1,0:T(8,128)} %get-tuple-element.125.refs_0_.refs_1_, bf16[512,768]{1,0:T(8,128)(2,1)} %get-tuple-element.126.refs_1_.refs_2_, ...), custom_call_target="tpu_custom_call" | custom-call | flops 9663676416 | bytes 28311552 | tf_op jit(solution)/shard_map/mlp_back/pallas_call | solution.py:725
  230.5 35.7 %back_far.2 = (bf16[512,768]{1,0:T(8,128)(2,1)}, f32[768,512]{1,0:T(8,128)}, bf16[512,768]{1,0:T(8,128)(2,1)}, bf16[512,768]{1,0:T(8,128)(2,1)}, bf16[512,768]{1...) custom-call(s32[1]{0:T(128)S(6)} %copy.29.refs_0_.refs_8_, ...), custom_call_target="tpu_custom_call" | custom-call | flops 17112760320 | bytes 18874368 | tf_op jit(solution)/shard_map/back_far/pallas_call | solution.py:725
  266.1 34.6 %back_near.2 = (bf16[768,1536]{1,0:T(8,128)(2,1)}, bf16[768,1536]{1,0:T(8,128)(2,1)}, f32[512,768]{1,0:T(8,128)}, f32[1,768]{1,0:T(1,128)}, bf16[96,1536]{1,0:T(8,128)(2,1)}, /*index=5*/bf16[96,1536]{1,0:T(8,128)(2,1)}) custom-call(s32[1]{0:T(128)S(6)} %copy.29.refs_0_.refs_8_, bf16[512,768]{1,0:T(8,128)(2,1)} %get-tuple-element.130.refs_3_.refs_1_, ...), custom_call_target="tpu_custom_call" | custom-call | flops 12683575296 | bytes 28311552 | tf_op jit(solution)/shard_map/back_near/pallas_call | solution.py:725
  300.8 36.8 %mlp_back.3 = (f32[512,768]{1,0:T(8,128)}, bf16[512,768]{1,0:T(8,128)(2,1)}, bf16[768,3072]{1,0:T(8,128)(2,1)}, bf16[768,3072]{1,0:T(8,128)(2,1)}, f32[1,768]{1,...) custom-call(f32[512,768]{1,0:T(8,128)} %get-tuple-element.154.refs_0_, ...), custom_call_target="tpu_custom_call" | custom-call | flops 9663676416 | bytes 28311552 | tf_op jit(solution)/shard_map/mlp_back/pallas_call | solution.py:725
  337.6 1.2 fusion
  338.7 0.2 reshape.32
  339.7 1.1 maximum_bitcast_fusion.refs_16_
  340.7 38.7 %back_far.3 = (bf16[512,768]{1,0:T(8,128)(2,1)}, f32[768,512]{1,0:T(8,128)}, bf16[512,768]{1,0:T(8,128)(2,1)}, bf16[512,768]{1,0:T(8,128)(2,1)}, bf16[512,768]{1...) custom-call(s32[1]{0:T(128)S(6)} %copy.29.refs_0_.refs_8_, ...), custom_call_target="tpu_custom_call" | custom-call | flops 17112760320 | bytes 18874368 | tf_op jit(solution)/shard_map/back_far/pallas_call | solution.py:725
  379.5 35.8 %back_near.3 = (bf16[768,1536]{1,0:T(8,128)(2,1)}, bf16[768,1536]{1,0:T(8,128)(2,1)}, f32[512,768]{1,0:T(8,128)}, f32[1,768]{1,0:T(1,128)}, bf16[96,1536]{1,0:T(...) custom-call(s32[1]{0:T(128)S(6)} %copy.29.refs_0_.refs_8_, ...), custom_call_target="tpu_custom_call" | custom-call | flops 12683575296 | bytes 28311552 | tf_op jit(solution)/shard_map/back_near/pallas_call | solution.py:725
  415.3 1.3 pad_maximum_fusion.refs_0_.refs_3_
  416.6 56.2 %tail.1 = (f32[4,768]{1,0:T(4,128)}, bf16[96,1536]{1,0:T(8,128)(2,1)}, bf16[96,1536]{1,0:T(8,128)(2,1)}, f32[4,768]{1,0:T(4,128)}, bf16[96,1536]{1,0:T(8,128)(2,...) custom-call(f32[4,768]{1,0:T(4,128)} %pad_maximum_fusion.refs_0_.refs_3_, ...), custom_call_target="tpu_custom_call" | custom-call | flops 1 | bytes 16777216 | tf_op jit(solution)/shard_map/tail/pallas_call | solution.py:725
  472.7 1.4 fusion.2
  474.1 9.3 %layout.1 = (f32[2,192,768]{2,1,0:T(8,128)}, f32[2,192,768]{2,1,0:T(8,128)}, f32[2,192,768]{2,1,0:T(8,128)}, f32[2,192,768]{2,1,0:T(8,128)}, f32[2,768,768]{2,1,0:T(8,128)}, /*index=5*/f32[2,768,768]{2,1,0:T(8,128)}) custom-call(bf16[768,768]{1,0:T(8,128)(2,1)} %get-tuple-element.200.refs_0_, bf16[768,768]{1,0:T(8,128)(2,1)} %get-tuple-element.201.refs_1_, ...), custom_call_target="tpu_custom_call" | custom-call | flops 1 | bytes 21233664 | tf_op jit(solution)/shard_map/layout/pallas_call | solution.py:725
  483.5 1.1 copy.30
  (15 shorter events, 0.7 us)
Async XLA Ops:
  379.4 35.8 %copy-start.1 = (f32[1,768]{1,0:T(1,128)S(1)}, f32[1,768]{1,0:T(1,128)}, u32[]{:S(2)}) copy-start(f32[1,768]{1,0:T(1,128)} %get-tuple-element.192) | copy-start | bytes 9220
  379.4 35.8 %copy-start.2 = (f32[1,768]{1,0:T(1,128)S(1)}, f32[1,768]{1,0:T(1,128)}, u32[]{:S(2)}) copy-start(f32[1,768]{1,0:T(1,128)} %get-tuple-element.190) | copy-start | bytes 9220
  379.4 35.8 %copy-start.3 = (f32[1,768]{1,0:T(1,128)S(1)}, f32[1,768]{1,0:T(1,128)}, u32[]{:S(2)}) copy-start(f32[1,768]{1,0:T(1,128)} %get-tuple-element.191) | copy-start | bytes 9220
  474.1 9.4 %copy-start = (f32[512,768]{1,0:T(8,128)S(1)}, f32[512,768]{1,0:T(8,128)}, u32[]{:S(2)}) copy-start(f32[512,768]{1,0:T(8,128)} %get-tuple-element.261) | copy-start | bytes 4718596

commit v6 on v5

--- a/solution.py
+++ b/solution.py
@@ -155,13 +155,14 @@
 class Gather(Job):
     plane = 1
 
-    def __init__(self, piece, shape=None):
+    def __init__(self, piece, shape=None, early=False):
+        self.early = early
         self.rows, n = shape if piece is None else piece.shape
         self.half = n // 2
         self.src = None
         self.ins, self.in_specs = ([], []) if piece is None else ([piece], vmem(1))
         self.outs, self.out_specs = [jax.ShapeDtypeStruct((self.rows << BITS, n), BF)], any_spec()
-        self.scratch = [dma(2 * BITS), dma(2 * BITS), dma(2)]
+        self.scratch = [dma(4 * BITS), dma(4 * BITS), dma(2)]
 
     def cols(self, i):
         return pl.ds(i * self.half, self.half)
@@ -187,15 +188,36 @@
             self.s[0].at[2 * s + i], self.s[1].at[2 * s + i], partner(self.dp, b), self.t,
         )
 
+    def across(self, s, i):
+        slot = slot_of(self.dp, ORDERS[i])
+        level = max(s - 1, 0)
+        block = slot // (1 << level)
+        if s > 0:
+            block = block + 1 - 2 * (block % 2)
+        size = self.rows << level
+        there = self.o[0].at[pl.ds(aligned(block * size), size), self.cols(i)]
+        k = 2 * BITS + 2 * s + i
+        return remote(
+            self.source().at[:, self.cols(i)] if s == 0 else there, there,
+            self.s[0].at[k], self.s[1].at[k], partner(self.dp, ORDERS[i][0]), self.t,
+        )
+
     def start(self, s):
         for i in range(2):
-            self.copy(s, i).start()
+            if s < BITS - 1 or not self.early:
+                self.copy(s, i).start()
+            if self.early:
+                self.across(s, i).start()
             if s == 0:
                 self.own(i).start()
 
     def wait(self, s):
         for i in range(2):
-            self.copy(s, i).wait()
+            if s < BITS - 1 or not self.early:
+                self.copy(s, i).wait()
+            else:
+                for k in range(BITS):
+                    self.across(k, i).wait()
             if s == 0:
                 self.own(i).wait()
 
@@ -1558,7 +1580,7 @@
     x = tokens
     for l in range(LAYERS):
         more = l + 1 < LAYERS
-        jobs = [Gather(wide)] + ([Line(pa[l + 1], False)] if more else [])
+        jobs = [Gather(wide, None, True)] + ([Line(pa[l + 1], False)] if more else [])
         res, extra = attend(
             info, x, a, wa, cosf, sinf, cos, sin, mlp_gain, l, jobs, 10 + l
         )

time: 489 us -> 487 us (level)
  no operation moved by 1% of the time
where the time goes in v6:
time: 487 us; the launch traced here: 483 us
  Pallas kernels  469 us (96%)
  local copies, waits for them, and re-layouts  9.27 us (2%)
    pallas_call x14, Pallas kernels, run(): pl.pallas_call(kernel, out_shape=tuple(outs), in_specs=list(in_specs), ou...  469 us

profile of v6, /device:TPU:0, one launch (start us, length us, event | category | flops | bytes accessed | tf_op | source)
XLA Modules:
  0.0 482.7 jit_solution(5716069296558800196)
XLA Ops:
  1.3 24.0 %first.1 = (bf16[512,768]{1,0:T(8,128)(2,1)}, bf16[4,96,192]{2,1,0:T(8,128)(2,1)}, bf16[2,96,768]{2,1,0:T(8,128)(2,1)}, bf16[2,96,768]{2,1,0:T(8,128)(2,1)}, bf16[4,4,96,192]{3,2,1,0:T(8,128)(2,1)}) custom-call(bf16[512,768]{1,0:T(8,128)(2,1)} %refs_19_.1, f32[2,768]{1,0:T(2,128)} %refs_21_.3, bf16[2,192,768]{2,1,0:T(8,128)(2,1)} %bitcast.72, ...), custom_call_target="tpu_custom_call" | custom-call | flops 3932160 | bytes 1572864 | tf_op jit(solution)/shard_map/first/pallas_call | solution.py:747
  25.3 1.2 slice_bitcast_fusion.16
  26.5 1.1 concatenate.12.refs_0_
  27.6 28.5 %gather_first.1 = (bf16[768,3072]{1,0:T(8,128)(2,1)}, bf16[96,6144]{1,0:T(8,128)(2,1)}) custom-call(bf16[96,3072]{1,0:T(8,128)(2,1)} %concatenate.12.refs_0_, bf16[2,96,768]{2,1,0:T(8,128)(2,1)} %get-tuple-element.112.refs_1_), custom_call_target="tpu_custom_call" | custom-call | flops 1 | bytes 16777216 | tf_op jit(solution)/shard_map/gather_first/pallas_call | solution.py:747
  56.1 58.3 %attend.2 = (bf16[512,768]{1,0:T(8,128)(2,1)}, bf16[512,768]{1,0:T(8,128)(2,1)}, bf16[512,768]{1,0:T(8,128)(2,1)}, bf16[512,768]{1,0:T(8,128)(2,1)}, bf16[512,76...) custom-call(s32[1]{0:T(128)S(6)} %copy.29.refs_0_.refs_8_, ...), custom_call_target="tpu_custom_call" | custom-call | flops 12884901888 | bytes 17301504 | tf_op jit(solution)/shard_map/attend/pallas_call | solution.py:747
  114.4 1.2 slice_bitcast_fusion
  115.6 1.1 concatenate.13.refs_6_
  116.8 30.6 %mlp.2 = (f32[512,768]{1,0:T(8,128)}, bf16[512,768]{1,0:T(8,128)(2,1)}, bf16[512,3072]{1,0:T(8,128)(2,1)}, bf16[96,6144]{1,0:T(8,128)(2,1)}, bf16[768,3072]{1,0:T(8,128)(2,1)}) custom-call(f32[512,768]{1,0:T(8,128)} %get-tuple-element.116.refs_0_.refs_1_, bf16[512,768]{1,0:T(8,128)(2,1)} %get-tuple-element.117.refs_1_.refs_2_, ...), custom_call_target="tpu_custom_call" | custom-call | flops 4831838208 | bytes 16515072 | tf_op jit(solution)/shard_map/mlp/pallas_call | solution.py:747
  147.4 50.2 %attend.3 = (bf16[512,768]{1,0:T(8,128)(2,1)}, bf16[512,768]{1,0:T(8,128)(2,1)}, bf16[512,768]{1,0:T(8,128)(2,1)}, bf16[512,768]{1,0:T(8,128)(2,1)}, bf16[512,76...) custom-call(s32[1]{0:T(128)S(6)} %copy.29.refs_0_.refs_8_, ...), custom_call_target="tpu_custom_call" | custom-call | flops 12884901888 | bytes 17301504 | tf_op jit(solution)/shard_map/attend/pallas_call | solution.py:747
  197.6 11.1 %mlp.3 = (f32[512,768]{1,0:T(8,128)}, bf16[512,768]{1,0:T(8,128)(2,1)}, bf16[512,3072]{1,0:T(8,128)(2,1)}) custom-call(f32[512,768]{1,0:T(8,128)} %get-tuple-element.125.refs_0_.refs_1_, bf16[512,768]{1,0:T(8,128)(2,1)} %get-tuple-element.126.refs_1_.refs_2_, bf16[768,6144]{1,0:T(8,128)(2,1)} %get-tuple-element.127.refs_2_.refs_3_.refs_4_.refs_5_, ...), custom_call_target="tpu_custom_call" | custom-call | flops 4831838208 | bytes 16515072 | tf_op jit(solution)/shard_map/mlp/pallas_call | solution.py:747
  208.8 19.1 %mlp_back.2 = (f32[512,768]{1,0:T(8,128)}, bf16[512,768]{1,0:T(8,128)(2,1)}, bf16[768,3072]{1,0:T(8,128)(2,1)}, bf16[768,3072]{1,0:T(8,128)(2,1)}, f32[1,768]{1,0:T(1,128)}) custom-call(bf16[512,768]{1,0:T(8,128)(2,1)} %refs_0_.9, f32[512,768]{1,0:T(8,128)} %get-tuple-element.125.refs_0_.refs_1_, bf16[512,768]{1,0:T(8,128)(2,1)} %get-tuple-element.126.refs_1_.refs_2_, ...), custom_call_target="tpu_custom_call" | custom-call | flops 9663676416 | bytes 28311552 | tf_op jit(solution)/shard_map/mlp_back/pallas_call | solution.py:747
  227.9 35.6 %back_far.2 = (bf16[512,768]{1,0:T(8,128)(2,1)}, f32[768,512]{1,0:T(8,128)}, bf16[512,768]{1,0:T(8,128)(2,1)}, bf16[512,768]{1,0:T(8,128)(2,1)}, bf16[512,768]{1...) custom-call(s32[1]{0:T(128)S(6)} %copy.29.refs_0_.refs_8_, ...), custom_call_target="tpu_custom_call" | custom-call | flops 17112760320 | bytes 18874368 | tf_op jit(solution)/shard_map/back_far/pallas_call | solution.py:747
  263.6 34.6 %back_near.2 = (bf16[768,1536]{1,0:T(8,128)(2,1)}, bf16[768,1536]{1,0:T(8,128)(2,1)}, f32[512,768]{1,0:T(8,128)}, f32[1,768]{1,0:T(1,128)}, bf16[96,1536]{1,0:T(8,128)(2,1)}, /*index=5*/bf16[96,1536]{1,0:T(8,128)(2,1)}) custom-call(s32[1]{0:T(128)S(6)} %copy.29.refs_0_.refs_8_, bf16[512,768]{1,0:T(8,128)(2,1)} %get-tuple-element.130.refs_3_.refs_1_, ...), custom_call_target="tpu_custom_call" | custom-call | flops 12683575296 | bytes 28311552 | tf_op jit(solution)/shard_map/back_near/pallas_call | solution.py:747
  298.2 36.8 %mlp_back.3 = (f32[512,768]{1,0:T(8,128)}, bf16[512,768]{1,0:T(8,128)(2,1)}, bf16[768,3072]{1,0:T(8,128)(2,1)}, bf16[768,3072]{1,0:T(8,128)(2,1)}, f32[1,768]{1,...) custom-call(f32[512,768]{1,0:T(8,128)} %get-tuple-element.154.refs_0_, ...), custom_call_target="tpu_custom_call" | custom-call | flops 9663676416 | bytes 28311552 | tf_op jit(solution)/shard_map/mlp_back/pallas_call | solution.py:747
  335.0 1.2 fusion
  336.1 0.2 reshape.32
  337.1 1.1 maximum_bitcast_fusion.refs_16_
  338.1 38.8 %back_far.3 = (bf16[512,768]{1,0:T(8,128)(2,1)}, f32[768,512]{1,0:T(8,128)}, bf16[512,768]{1,0:T(8,128)(2,1)}, bf16[512,768]{1,0:T(8,128)(2,1)}, bf16[512,768]{1...) custom-call(s32[1]{0:T(128)S(6)} %copy.29.refs_0_.refs_8_, ...), custom_call_target="tpu_custom_call" | custom-call | flops 17112760320 | bytes 18874368 | tf_op jit(solution)/shard_map/back_far/pallas_call | solution.py:747
  377.0 35.9 %back_near.3 = (bf16[768,1536]{1,0:T(8,128)(2,1)}, bf16[768,1536]{1,0:T(8,128)(2,1)}, f32[512,768]{1,0:T(8,128)}, f32[1,768]{1,0:T(1,128)}, bf16[96,1536]{1,0:T(...) custom-call(s32[1]{0:T(128)S(6)} %copy.29.refs_0_.refs_8_, ...), custom_call_target="tpu_custom_call" | custom-call | flops 12683575296 | bytes 28311552 | tf_op jit(solution)/shard_map/back_near/pallas_call | solution.py:747
  412.9 1.3 pad_maximum_fusion.refs_0_.refs_3_
  414.2 56.4 %tail.1 = (f32[4,768]{1,0:T(4,128)}, bf16[96,1536]{1,0:T(8,128)(2,1)}, bf16[96,1536]{1,0:T(8,128)(2,1)}, f32[4,768]{1,0:T(4,128)}, bf16[96,1536]{1,0:T(8,128)(2,...) custom-call(f32[4,768]{1,0:T(4,128)} %pad_maximum_fusion.refs_0_.refs_3_, ...), custom_call_target="tpu_custom_call" | custom-call | flops 1 | bytes 16777216 | tf_op jit(solution)/shard_map/tail/pallas_call | solution.py:747
  470.6 1.4 fusion.2
  472.0 9.3 %layout.1 = (f32[2,192,768]{2,1,0:T(8,128)}, f32[2,192,768]{2,1,0:T(8,128)}, f32[2,192,768]{2,1,0:T(8,128)}, f32[2,192,768]{2,1,0:T(8,128)}, f32[2,768,768]{2,1,0:T(8,128)}, /*index=5*/f32[2,768,768]{2,1,0:T(8,128)}) custom-call(bf16[768,768]{1,0:T(8,128)(2,1)} %get-tuple-element.200.refs_0_, bf16[768,768]{1,0:T(8,128)(2,1)} %get-tuple-element.201.refs_1_, ...), custom_call_target="tpu_custom_call" | custom-call | flops 1 | bytes 21233664 | tf_op jit(solution)/shard_map/layout/pallas_call | solution.py:747
  481.3 1.1 copy.30
  (15 shorter events, 0.7 us)
Async XLA Ops:
  376.9 35.9 %copy-start.1 = (f32[1,768]{1,0:T(1,128)S(1)}, f32[1,768]{1,0:T(1,128)}, u32[]{:S(2)}) copy-start(f32[1,768]{1,0:T(1,128)} %get-tuple-element.192) | copy-start | bytes 9220
  376.9 35.9 %copy-start.2 = (f32[1,768]{1,0:T(1,128)S(1)}, f32[1,768]{1,0:T(1,128)}, u32[]{:S(2)}) copy-start(f32[1,768]{1,0:T(1,128)} %get-tuple-element.190) | copy-start | bytes 9220
  377.0 35.9 %copy-start.3 = (f32[1,768]{1,0:T(1,128)S(1)}, f32[1,768]{1,0:T(1,128)}, u32[]{:S(2)}) copy-start(f32[1,768]{1,0:T(1,128)} %get-tuple-element.191) | copy-start | bytes 9220
  472.0 9.4 %copy-start = (f32[512,768]{1,0:T(8,128)S(1)}, f32[512,768]{1,0:T(8,128)}, u32[]{:S(2)}) copy-start(f32[512,768]{1,0:T(8,128)} %get-tuple-element.261) | copy-start | bytes 4718596
